TPU v7x, 32 devices: a whole 2x2x4 slice. The times are simulated.
32 devices in a mesh: seq: 8 (over z, x), mp: 2 (over y), expert: 2 (over core).
Axes of the slice: x: 2, y: 2, z: 4, core: 2. Of those that a mesh axis runs over, the one named last changes fastest.
Arguments:
- hidden_prefix: bfloat16 [4480, 2048], P('seq'), may hold values from -6 to 6
- hidden_action: bfloat16 [800, 1024], P('seq'), may hold values from -6 to 6
- norm1_prefix: bfloat16 [2048], P('seq'), may hold values from 0.5 to 1.5
- query_prefix: bfloat16 [2048, 2048], P('seq', ('mp', 'expert')), may hold values from -0.125 to 0.125
- key_prefix: bfloat16 [2048, 256], P('seq'), may hold values from -0.125 to 0.125
- value_prefix: bfloat16 [2048, 256], P('seq'), may hold values from -0.125 to 0.125
- out_prefix: bfloat16 [2048, 2048], P(('mp', 'expert'), 'seq'), may hold values from -2 to 2
- norm2_prefix: bfloat16 [2048], P('seq'), may hold values from 0.5 to 1.5
- gate_prefix: bfloat16 [2048, 16384], P('seq', ('mp', 'expert')), may hold values from -0.125 to 0.125
- up_prefix: bfloat16 [2048, 16384], P('seq', ('mp', 'expert')), may hold values from -0.125 to 0.125
- down_prefix: bfloat16 [16384, 2048], P(('mp', 'expert'), 'seq'), may hold values from -0.046875 to 0.046875
- norm1_action: bfloat16 [1024], P('seq'), may hold values from 0.5 to 1.5
- query_action: bfloat16 [1024, 2048], P('seq', ('mp', 'expert')), may hold values from -0.1875 to 0.1875
- key_action: bfloat16 [1024, 256], P('seq'), may hold values from -0.1875 to 0.1875
- value_action: bfloat16 [1024, 256], P('seq'), may hold values from -0.1875 to 0.1875
- out_action: bfloat16 [2048, 1024], P(('mp', 'expert'), 'seq'), may hold values from -2 to 2
- norm2_action: bfloat16 [1024], P('seq'), may hold values from 0.5 to 1.5
- gate_action: bfloat16 [1024, 4096], P('seq', ('mp', 'expert')), may hold values from -0.1875 to 0.1875
- up_action: bfloat16 [1024, 4096], P('seq', ('mp', 'expert')), may hold values from -0.1875 to 0.1875
- down_action: bfloat16 [4096, 1024], P(('mp', 'expert'), 'seq'), may hold values from -0.09375 to 0.09375
- cot_prefix: bfloat16 [4480, 2048], P('seq'), may hold values from -6 to 6
- cot_action: bfloat16 [800, 1024], P('seq'), may hold values from -6 to 6
- instr_len: int32 [8], replicated, may hold values from 1 to 48, as said below
- slot_source: int32 [16], P('seq'), may hold values from -1 to 1, as said below
Outputs:
- y_prefix: bfloat16 [4480, 2048], P('seq')
- y_action: bfloat16 [800, 1024], P('seq')
- grad_hidden_prefix: float32 [4480, 2048], P('seq')
- grad_hidden_action: float32 [800, 1024], P('seq')
- grad_norm1_prefix: float32 [2048], P('seq')
- grad_query_prefix: float32 [2048, 2048], P('seq', ('mp', 'expert'))
- grad_key_prefix: float32 [2048, 256], P('seq')
- grad_value_prefix: float32 [2048, 256], P('seq')
- grad_out_prefix: float32 [2048, 2048], P(('mp', 'expert'), 'seq')
- grad_norm2_prefix: float32 [2048], P('seq')
- grad_gate_prefix: float32 [2048, 16384], P('seq', ('mp', 'expert'))
- grad_up_prefix: float32 [2048, 16384], P('seq', ('mp', 'expert'))
- grad_down_prefix: float32 [16384, 2048], P(('mp', 'expert'), 'seq')
- grad_norm1_action: float32 [1024], P('seq')
- grad_query_action: float32 [1024, 2048], P('seq', ('mp', 'expert'))
- grad_key_action: float32 [1024, 256], P('seq')
- grad_value_action: float32 [1024, 256], P('seq')
- grad_out_action: float32 [2048, 1024], P(('mp', 'expert'), 'seq')
- grad_norm2_action: float32 [1024], P('seq')
- grad_gate_action: float32 [1024, 4096], P('seq', ('mp', 'expert'))
- grad_up_action: float32 [1024, 4096], P('seq', ('mp', 'expert'))
- grad_down_action: float32 [4096, 1024], P(('mp', 'expert'), 'seq')
Inputs may be any that keep to these rules, and one draw needn't show every extreme that they name: `instr_len`: each episode's instruction fills 1 to 48 of its slots; the rest of its prefix rows are padding. `slot_source`: each episode's action rows stand in exactly one slot: at its own seq index (0) or at the next seq index, cyclically (1); -1 marks an empty slot. A seq index holds 0 to 2 episodes. Episodes 0, 3, 6 and 7 always place theirs at the next seq index, episode 1 at its own.
All inputs are finite; a program needn't handle non-finite values.
Results may differ from a plain program's by a relative error of at most 0.015.
Values may be sent and summed in bfloat16 or wider, within the bound.
No kernel may reach another device: no remote copies, remote signals or barrier semaphores. Data moves between devices by JAX's collectives and lax.ppermute only.
A program may use at most 320 MiB of HBM per device.

v0:
```python
import jax
import jax.numpy as jnp
from jax import lax
from jax.sharding import PartitionSpec as P

IMG = 512


EPS = 1e-06
MASKED = -1e30


def from_behind(block, axis, distance):
    devices = range(lax.axis_size(axis))
    route = [((i - distance) % len(devices), i) for i in devices]
    return lax.ppermute(block, axis, route)


def rms_norm(values, gain_vec):
    return values * lax.rsqrt(jnp.mean(values * values, axis=-1, keepdims=True) + EPS) * gain_vec


def geglu_act(gate_pre, up_pre):
    return jax.nn.gelu(gate_pre, approximate=True) * up_pre


def unpack(row_part, col_part):
    gain_one, w_query, w_key, w_value, gain_two, w_gate, w_up = row_part
    w_out, w_down = col_part
    return (
        gain_one.astype(jnp.float32),
        w_query,
        jnp.concatenate([w_key, w_value], axis=1),
        w_out,
        gain_two.astype(jnp.float32),
        w_gate,
        w_up,
        w_down,
    )


def project(weights, hidden_in):
    hidden_full = hidden_in.astype(jnp.float32)
    normed = rms_norm(hidden_full, weights[0]).astype(jnp.bfloat16)
    query_rows = jnp.dot(normed, weights[1], preferred_element_type=jnp.float32).astype(
        jnp.bfloat16
    )
    kv_rows = jnp.dot(normed, weights[2], preferred_element_type=jnp.float32).astype(jnp.bfloat16)
    return (hidden_full, normed, query_rows, kv_rows)


def attn_scores(query_heads, key_rows, keep_mask, score_scale):
    scores = (
        jnp.einsum("qhd,kd->hqk", query_heads, key_rows, preferred_element_type=jnp.float32)
        * score_scale
    )
    return jnp.where(keep_mask[None, None, :], scores, MASKED)


def attend_forward(query_flat, key_rows, value_rows, keep_mask):
    row_count = query_flat.shape[0]
    head_size = key_rows.shape[1]
    query_heads = query_flat.reshape(row_count, -1, head_size)
    scores = attn_scores(query_heads, key_rows, keep_mask, head_size ** (-0.5))
    row_top = jnp.max(scores, axis=-1, keepdims=True)
    expo = jnp.exp(scores - row_top)
    row_total = jnp.sum(expo, axis=-1, keepdims=True)
    prob_low = (expo / row_total).astype(jnp.bfloat16)
    log_total = row_top + jnp.log(row_total)
    mixed_rows = jnp.einsum("hqk,kd->qhd", prob_low, value_rows, preferred_element_type=jnp.float32)
    return (mixed_rows.reshape(row_count, -1).astype(jnp.bfloat16), log_total)


def attend_backward(query_flat, key_rows, value_rows, keep_mask, log_total, grad_mixed):
    row_count = query_flat.shape[0]
    head_size = key_rows.shape[1]
    score_scale = head_size ** (-0.5)
    query_heads = query_flat.reshape(row_count, -1, head_size)
    scores = attn_scores(query_heads, key_rows, keep_mask, score_scale)
    prob_rows = jnp.exp(scores - log_total)
    prob_low = prob_rows.astype(jnp.bfloat16)
    grad_heads = grad_mixed.reshape(row_count, -1, head_size)
    grad_probs = jnp.einsum(
        "qhd,kd->hqk", grad_heads, value_rows, preferred_element_type=jnp.float32
    )
    row_inner = jnp.sum(grad_probs * prob_rows, axis=-1, keepdims=True)
    grad_scores = (prob_rows * (grad_probs - row_inner)).astype(jnp.bfloat16)
    grad_query = (
        jnp.einsum("hqk,kd->qhd", grad_scores, key_rows, preferred_element_type=jnp.float32)
        * score_scale
    )
    grad_query = grad_query.reshape(row_count, -1).astype(jnp.bfloat16)
    grad_keys = (
        jnp.einsum("hqk,qhd->kd", grad_scores, query_heads, preferred_element_type=jnp.float32)
        * score_scale
    )
    grad_values = jnp.einsum(
        "hqk,qhd->kd", prob_low, grad_heads, preferred_element_type=jnp.float32
    )
    return (grad_query, grad_keys, grad_values)


def mlp_forward(weights, middle):
    normed = rms_norm(middle, weights[4]).astype(jnp.bfloat16)
    gate_pre = jnp.dot(normed, weights[5], preferred_element_type=jnp.float32)
    up_pre = jnp.dot(normed, weights[6], preferred_element_type=jnp.float32)
    hidden_mid = geglu_act(gate_pre, up_pre).astype(jnp.bfloat16)
    partial_out = jnp.dot(hidden_mid, weights[7], preferred_element_type=jnp.float32)
    return (normed, gate_pre, up_pre, hidden_mid, partial_out)


def mlp_backward(weights, normed, gate_pre, up_pre, hidden_mid, grad_out16):
    grad_down = jnp.einsum("rf,rd->fd", hidden_mid, grad_out16, preferred_element_type=jnp.float32)
    grad_hidden = jnp.einsum(
        "rd,fd->rf", grad_out16, weights[7], preferred_element_type=jnp.float32
    )
    pullback = jax.vjp(geglu_act, gate_pre, up_pre)[1]
    grad_gate, grad_up = pullback(grad_hidden)
    grad_gate = grad_gate.astype(jnp.bfloat16)
    grad_up = grad_up.astype(jnp.bfloat16)
    grad_wgate = jnp.einsum("rd,rf->df", normed, grad_gate, preferred_element_type=jnp.float32)
    grad_wup = jnp.einsum("rd,rf->df", normed, grad_up, preferred_element_type=jnp.float32)
    grad_normed = jnp.einsum("rf,df->rd", grad_gate, weights[5], preferred_element_type=jnp.float32)
    grad_normed = grad_normed + jnp.einsum(
        "rf,df->rd", grad_up, weights[6], preferred_element_type=jnp.float32
    )
    return (grad_normed, grad_wgate, grad_wup, grad_down)


def norm_backward(values, gain_vec, grad_normed):
    pullback = jax.vjp(rms_norm, values, gain_vec)[1]
    return pullback(grad_normed)


def body(
    hidden_prefix,
    hidden_action,
    norm1_prefix,
    query_prefix,
    key_prefix,
    value_prefix,
    out_prefix,
    norm2_prefix,
    gate_prefix,
    up_prefix,
    down_prefix,
    norm1_action,
    query_action,
    key_action,
    value_action,
    out_action,
    norm2_action,
    gate_action,
    up_action,
    down_action,
    cot_prefix,
    cot_action,
    instr_len,
    slot_source,
):
    row_full = (
        lax.all_gather(norm1_prefix, "seq", axis=0, tiled=True),
        lax.all_gather(query_prefix, "seq", axis=0, tiled=True),
        lax.all_gather(key_prefix, "seq", axis=0, tiled=True),
        lax.all_gather(value_prefix, "seq", axis=0, tiled=True),
        lax.all_gather(norm2_prefix, "seq", axis=0, tiled=True),
        lax.all_gather(gate_prefix, "seq", axis=0, tiled=True),
        lax.all_gather(up_prefix, "seq", axis=0, tiled=True),
        lax.all_gather(norm1_action, "seq", axis=0, tiled=True),
        lax.all_gather(query_action, "seq", axis=0, tiled=True),
        lax.all_gather(key_action, "seq", axis=0, tiled=True),
        lax.all_gather(value_action, "seq", axis=0, tiled=True),
        lax.all_gather(norm2_action, "seq", axis=0, tiled=True),
        lax.all_gather(gate_action, "seq", axis=0, tiled=True),
        lax.all_gather(up_action, "seq", axis=0, tiled=True),
    )
    col_full = (
        lax.all_gather(out_prefix, "seq", axis=1, tiled=True),
        lax.all_gather(down_prefix, "seq", axis=1, tiled=True),
        lax.all_gather(out_action, "seq", axis=1, tiled=True),
        lax.all_gather(down_action, "seq", axis=1, tiled=True),
    )
    weights_p = unpack(row_full[:7], col_full[:2])
    weights_a = unpack(row_full[7:], col_full[2:])
    seq_index = lax.axis_index("seq")
    episodes = lax.axis_size("seq")
    prefix_rows = hidden_prefix.shape[0]
    slot_count = slot_source.shape[0]
    action_rows = hidden_action.shape[0] // slot_count
    positions = jnp.arange(prefix_rows, dtype=jnp.int32)
    keep_prefix = positions < IMG + instr_len[seq_index]
    live_slot = slot_source >= 0
    offsets = jnp.where(live_slot, slot_source, 0)
    source_ep = (seq_index - offsets + episodes) % episodes
    keep_slots = (positions[None, :] < IMG + instr_len[source_ep][:, None]) & live_slot[:, None]
    keep_all = jnp.concatenate(
        [keep_slots, jnp.ones((slot_count, action_rows), dtype=bool)], axis=1
    )
    from_prev = slot_source == 1
    from_here = slot_source == 0
    live_rows = jnp.repeat(live_slot.astype(jnp.float32), action_rows)[:, None]
    x_pre, normed1_p, query_p, kv_p = project(weights_p, hidden_prefix)
    x_act, normed1_a, query_a, kv_a = project(weights_a, hidden_action)
    head_size = kv_p.shape[1] // 2
    kv_prev = from_behind(kv_p, "seq", 1)
    keys_p = kv_p[:, :head_size]
    values_p = kv_p[:, head_size:]
    mixed_p, lse_p = attend_forward(query_p, keys_p, values_p, keep_prefix)
    kv_slots = jnp.where(from_prev[:, None, None], kv_prev[None], kv_p[None])
    kv_own = kv_a.reshape(slot_count, action_rows, -1)
    keys_slots = jnp.concatenate([kv_slots[:, :, :head_size], kv_own[:, :, :head_size]], axis=1)
    values_slots = jnp.concatenate([kv_slots[:, :, head_size:], kv_own[:, :, head_size:]], axis=1)
    query_slots = query_a.reshape(slot_count, action_rows, -1)
    mixed_slots, lse_a = jax.vmap(attend_forward)(query_slots, keys_slots, values_slots, keep_all)
    mixed_a = mixed_slots.reshape(slot_count * action_rows, -1)
    attn_p = jnp.dot(mixed_p, weights_p[3], preferred_element_type=jnp.float32)
    attn_a = jnp.dot(mixed_a, weights_a[3], preferred_element_type=jnp.float32) * live_rows
    attn_p, attn_a = lax.psum((attn_p, attn_a), ("mp", "expert"))
    middle_p = x_pre + attn_p
    middle_a = x_act + attn_a
    normed2_p, gate_p, upper_p, hmid_p, mlp_p = mlp_forward(weights_p, middle_p)
    normed2_a, gate_a, upper_a, hmid_a, mlp_a = mlp_forward(weights_a, middle_a)
    mlp_a = mlp_a * live_rows
    mlp_p, mlp_a = (
        lax.psum(mlp_p.astype(jnp.bfloat16), ("mp", "expert")).astype(jnp.float32),
        lax.psum(mlp_a.astype(jnp.bfloat16), ("mp", "expert")).astype(jnp.float32),
    )
    out_pre = (middle_p + mlp_p).astype(jnp.bfloat16)
    out_act = (middle_a + mlp_a).astype(jnp.bfloat16)
    grad_yp = cot_prefix.astype(jnp.float32)
    grad_ya = cot_action.astype(jnp.float32)
    gn2_p, dwg_p, dwu_p, dwd_p = mlp_backward(
        weights_p, normed2_p, gate_p, upper_p, hmid_p, grad_yp.astype(jnp.bfloat16)
    )
    gn2_a, dwg_a, dwu_a, dwd_a = mlp_backward(
        weights_a, normed2_a, gate_a, upper_a, hmid_a, (grad_ya * live_rows).astype(jnp.bfloat16)
    )
    gn2_p, gn2_a = lax.psum((gn2_p, gn2_a), ("mp", "expert"))
    dmid_norm_p, dgain2_p = norm_backward(middle_p, weights_p[4], gn2_p)
    dmid_norm_a, dgain2_a = norm_backward(middle_a, weights_a[4], gn2_a)
    dmid_p = grad_yp + dmid_norm_p
    dmid_a = grad_ya + dmid_norm_a
    dao_p = dmid_p.astype(jnp.bfloat16)
    dao_a = (dmid_a * live_rows).astype(jnp.bfloat16)
    dwo_p = jnp.einsum("rh,rd->hd", mixed_p, dao_p, preferred_element_type=jnp.float32)
    dwo_a = jnp.einsum("rh,rd->hd", mixed_a, dao_a, preferred_element_type=jnp.float32)
    dmix_p = jnp.einsum(
        "rd,hd->rh", dao_p, weights_p[3], preferred_element_type=jnp.float32
    ).astype(jnp.bfloat16)
    dmix_a = jnp.einsum(
        "rd,hd->rh", dao_a, weights_a[3], preferred_element_type=jnp.float32
    ).astype(jnp.bfloat16)
    dq_slots, dkeys_slots, dvals_slots = jax.vmap(attend_backward)(
        query_slots,
        keys_slots,
        values_slots,
        keep_all,
        lse_a,
        dmix_a.reshape(slot_count, action_rows, -1),
    )
    dkv_pre = jnp.concatenate([dkeys_slots[:, :prefix_rows], dvals_slots[:, :prefix_rows]], axis=2)
    dkv_own = jnp.concatenate(
        [dkeys_slots[:, prefix_rows:], dvals_slots[:, prefix_rows:]], axis=2
    ).reshape(slot_count * action_rows, -1)
    to_prev = jnp.sum(jnp.where(from_prev[:, None, None], dkv_pre, 0.0), axis=0)
    to_here = jnp.sum(jnp.where(from_here[:, None, None], dkv_pre, 0.0), axis=0)
    returned = from_behind(to_prev.astype(jnp.bfloat16), "seq", -1).astype(to_prev.dtype)
    dq_p, dk_p, dv_p = attend_backward(query_p, keys_p, values_p, keep_prefix, lse_p, dmix_p)
    dkv_p = jnp.concatenate([dk_p, dv_p], axis=1) + to_here + returned
    dq_a = dq_slots.reshape(slot_count * action_rows, -1)
    gq_p = jnp.einsum("rh,dh->rd", dq_p, weights_p[1], preferred_element_type=jnp.float32)
    gq_a = jnp.einsum("rh,dh->rd", dq_a, weights_a[1], preferred_element_type=jnp.float32)
    gq_p, dkv_p, gq_a, dkv_a = lax.psum((gq_p, dkv_p, gq_a, dkv_own), ("mp", "expert"))
    dkv_p16 = dkv_p.astype(jnp.bfloat16)
    dkv_a16 = dkv_a.astype(jnp.bfloat16)
    gn1_p = gq_p + jnp.einsum(
        "rk,dk->rd", dkv_p16, weights_p[2], preferred_element_type=jnp.float32
    )
    gn1_a = gq_a + jnp.einsum(
        "rk,dk->rd", dkv_a16, weights_a[2], preferred_element_type=jnp.float32
    )
    dwq_p = jnp.einsum("rd,rh->dh", normed1_p, dq_p, preferred_element_type=jnp.float32)
    dwq_a = jnp.einsum("rd,rh->dh", normed1_a, dq_a, preferred_element_type=jnp.float32)
    dwkv_p = jnp.einsum("rd,rk->dk", normed1_p, dkv_p16, preferred_element_type=jnp.float32)
    dwkv_a = jnp.einsum("rd,rk->dk", normed1_a, dkv_a16, preferred_element_type=jnp.float32)
    dx_norm_p, dgain1_p = norm_backward(x_pre, weights_p[0], gn1_p)
    dx_norm_a, dgain1_a = norm_backward(x_act, weights_a[0], gn1_a)
    dx_p = dmid_p + dx_norm_p
    dx_a = dmid_a + dx_norm_a
    rows_out = (
        lax.psum_scatter(dgain1_p, "seq", scatter_dimension=0, tiled=True),
        lax.psum_scatter(dwq_p, "seq", scatter_dimension=0, tiled=True),
        lax.psum_scatter(dwkv_p[:, :head_size], "seq", scatter_dimension=0, tiled=True),
        lax.psum_scatter(dwkv_p[:, head_size:], "seq", scatter_dimension=0, tiled=True),
        lax.psum_scatter(dgain2_p, "seq", scatter_dimension=0, tiled=True),
        lax.psum_scatter(dwg_p, "seq", scatter_dimension=0, tiled=True),
        lax.psum_scatter(dwu_p, "seq", scatter_dimension=0, tiled=True),
        lax.psum_scatter(dgain1_a, "seq", scatter_dimension=0, tiled=True),
        lax.psum_scatter(dwq_a, "seq", scatter_dimension=0, tiled=True),
        lax.psum_scatter(dwkv_a[:, :head_size], "seq", scatter_dimension=0, tiled=True),
        lax.psum_scatter(dwkv_a[:, head_size:], "seq", scatter_dimension=0, tiled=True),
        lax.psum_scatter(dgain2_a, "seq", scatter_dimension=0, tiled=True),
        lax.psum_scatter(dwg_a, "seq", scatter_dimension=0, tiled=True),
        lax.psum_scatter(dwu_a, "seq", scatter_dimension=0, tiled=True),
    )
    cols_out = (
        lax.psum_scatter(dwo_p, "seq", scatter_dimension=1, tiled=True),
        lax.psum_scatter(dwd_p, "seq", scatter_dimension=1, tiled=True),
        lax.psum_scatter(dwo_a, "seq", scatter_dimension=1, tiled=True),
        lax.psum_scatter(dwd_a, "seq", scatter_dimension=1, tiled=True),
    )
    prefix_grads = (
        rows_out[0],
        rows_out[1],
        rows_out[2],
        rows_out[3],
        cols_out[0],
        rows_out[4],
        rows_out[5],
        rows_out[6],
        cols_out[1],
    )
    action_grads = (
        rows_out[7],
        rows_out[8],
        rows_out[9],
        rows_out[10],
        cols_out[2],
        rows_out[11],
        rows_out[12],
        rows_out[13],
        cols_out[3],
    )
    return (
        out_pre,
        out_act,
        dx_p,
        dx_a,
        prefix_grads[0],
        prefix_grads[1],
        prefix_grads[2],
        prefix_grads[3],
        prefix_grads[4],
        prefix_grads[5],
        prefix_grads[6],
        prefix_grads[7],
        prefix_grads[8],
        action_grads[0],
        action_grads[1],
        action_grads[2],
        action_grads[3],
        action_grads[4],
        action_grads[5],
        action_grads[6],
        action_grads[7],
        action_grads[8],
    )


def solution(mesh):
    placed = (
        P("seq", None),
        P("seq", None),
        P("seq"),
        P("seq", ("mp", "expert")),
        P("seq", None),
        P("seq", None),
        P(("mp", "expert"), "seq"),
        P("seq"),
        P("seq", ("mp", "expert")),
        P("seq", ("mp", "expert")),
        P(("mp", "expert"), "seq"),
        P("seq"),
        P("seq", ("mp", "expert")),
        P("seq", None),
        P("seq", None),
        P(("mp", "expert"), "seq"),
        P("seq"),
        P("seq", ("mp", "expert")),
        P("seq", ("mp", "expert")),
        P(("mp", "expert"), "seq"),
        P("seq", None),
        P("seq", None),
        P(),
        P("seq"),
    )
    return jax.shard_map(
        body,
        mesh=mesh,
        in_specs=placed,
        out_specs=(
            P("seq", None),
            P("seq", None),
            P("seq", None),
            P("seq", None),
            P("seq"),
            P("seq", ("mp", "expert")),
            P("seq", None),
            P("seq", None),
            P(("mp", "expert"), "seq"),
            P("seq"),
            P("seq", ("mp", "expert")),
            P("seq", ("mp", "expert")),
            P(("mp", "expert"), "seq"),
            P("seq"),
            P("seq", ("mp", "expert")),
            P("seq", None),
            P("seq", None),
            P(("mp", "expert"), "seq"),
            P("seq"),
            P("seq", ("mp", "expert")),
            P("seq", ("mp", "expert")),
            P(("mp", "expert"), "seq"),
        ),
        check_vma=False,
    )
```

profile of v0, /device:TPU:1, one launch (start us, length us, event | category | flops | bytes accessed | tf_op | source)
XLA Modules:
  0.0 4103.8 jit_solution(15152952546116420437)
XLA Ops:
  11.9 17.9 all-gather
  32.6 26.9 all_gather.64
  59.6 25.7 all_gather.65
  85.3 12.8 all-gather.2
  111.1 29.3 all-gather.31.cloned.1.call-done
  145.3 34.7 all-gather.33.cloned.1.call-done
  182.3 49.2 %all-gather.21.cloned.1.call-done = bf16[2048,512]{1,0:T(8,128)(2,1)} async-done(((bf16[256,512]{1,0:T(8,128)(2,1)}), bf16[2048,512]{1,0:T(8,128)(2,1)}) %all-gather.21.cloned.1.call-update) | async-done | bytes 2097168 | tf_op jit(solution)/shard_map/all_gather | solution.py:163
  236.8 46.7 %all-gather.23.cloned.1.call-done = bf16[512,2048]{1,0:T(8,128)(2,1)} async-done(((bf16[512,256]{1,0:T(8,128)(2,1)}), bf16[512,2048]{1,0:T(8,128)(2,1)}) %all-gather.23.cloned.1.call-update) | async-done | bytes 2097168 | tf_op jit(solution)/shard_map/all_gather | solution.py:178
  292.9 14.8 all-gather.1
  307.7 23.7 all-gather.3
  332.0 54.4 %all-reduce.21.cloned.1.call-done = (f32[560,2048]{1,0:T(8,128)}, f32[100,1024]{1,0:T(8,128)}) async-done(((f32[560,2048]{1,0:T(8,128)}, f32[100,1024]{1,0:T(8,128)}), (f32[560,2048]{1,0:T(8,128)}, f32[100,1024]{1,0:T(8,128)})) %all-reduce.21.cloned.1.call-update) | async-done | bytes 4997136 | tf_op jit(solution)/shard_map/psum | solution.py:218
  393.5 43.5 %all-gather.35.cloned.1.call-done = bf16[1024,1024]{1,0:T(8,128)(2,1)} async-done(((bf16[128,1024]{1,0:T(8,128)(2,1)}), bf16[1024,1024]{1,0:T(8,128)(2,1)}) %all-gather.35.cloned.1.call-update) | async-done | bytes 2097168 | tf_op jit(solution)/shard_map/all_gather | solution.py:174
  439.1 47.9 %all-gather.37.cloned.1.call-done = bf16[1024,1024]{1,0:T(8,128)(2,1)} async-done(((bf16[128,1024]{1,0:T(8,128)(2,1)}), bf16[1024,1024]{1,0:T(8,128)(2,1)}) %all-gather.37.cloned.1.call-update) | async-done | bytes 2097168 | tf_op jit(solution)/shard_map/all_gather | solution.py:175
  489.1 49.9 %all-gather.39.cloned.1.call-done = bf16[1024,1024]{1,0:T(8,128)(2,1)} async-done(((bf16[1024,128]{1,0:T(8,128)(2,1)}), bf16[1024,1024]{1,0:T(8,128)(2,1)}) %all-gather.39.cloned.1.call-update) | async-done | bytes 2097168 | tf_op jit(solution)/shard_map/all_gather | solution.py:181
  547.7 219.5 %all-gather.25.cloned.1.call-done = bf16[2048,4096]{1,0:T(8,128)(2,1)} async-done(((bf16[256,4096]{1,0:T(8,128)(2,1)}), bf16[2048,4096]{1,0:T(8,128)(2,1)}) %all-gather.25.cloned.1.call-update) | async-done | bytes 16777232 | tf_op jit(solution)/shard_map/all_gather | solution.py:167
  767.2 15.3 fusion.116
  782.5 212.5 %all-gather.27.cloned.1.call-done = bf16[2048,4096]{1,0:T(8,128)(2,1)} async-done(((bf16[256,4096]{1,0:T(8,128)(2,1)}), bf16[2048,4096]{1,0:T(8,128)(2,1)}) %all-gather.27.cloned.1.call-update) | async-done | bytes 16777232 | tf_op jit(solution)/shard_map/all_gather | solution.py:168
  995.0 15.9 fusion.117
  1010.9 212.0 %all-gather.29.cloned.1.call-done = bf16[4096,2048]{1,0:T(8,128)(2,1)} async-done(((bf16[4096,256]{1,0:T(8,128)(2,1)}), bf16[4096,2048]{1,0:T(8,128)(2,1)}) %all-gather.29.cloned.1.call-update) | async-done | bytes 16777232 | tf_op jit(solution)/shard_map/all_gather | solution.py:179
  1222.9 26.1 multiply_convert_fusion
  1249.0 16.6 fusion.120
  1265.6 15.3 convolution_add_fusion.1
  1281.0 15.8 convolution_convert_fusion
  1297.1 81.4 %all-reduce.19.cloned.1.call-done = (f32[560,2048]{1,0:T(8,128)}, f32[100,1024]{1,0:T(8,128)}) async-done(((f32[560,2048]{1,0:T(8,128)}, f32[100,1024]{1,0:T(8,128)}), (f32[560,2048]{1,0:T(8,128)}, f32[100,1024]{1,0:T(8,128)})) %all-reduce.19.cloned.1.call-update) | async-done | bytes 4997136 | tf_op jit(solution)/shard_map/psum | solution.py:238
  1385.7 54.5 %all-reduce.23.cloned.1.call-done = (bf16[560,2048]{1,0:T(8,128)(2,1)}, bf16[100,1024]{1,0:T(8,128)(2,1)}) async-done(((bf16[560,2048]{1,0:T(8,128)(2,1)}, bf16[100,1024]{1,0:T(8,128)(2,1)}), (bf16[560,2048]{1,0:T(8,128)(2,1)}, bf16[100,1024]{1,0:T(8,128)(2,1)})) %all-reduce.23.cloned.1.call-update) | async-done | bytes 2498576 | tf_op jit(solution)/shard_map/psum | solution.py:225
  1440.2 6.4 fusion.11
  1488.9 6.8 collective-permute-done.1
  1497.0 44.0 %all-reduce.24 = (bf16[560,512]{1,0:T(8,128)(2,1)}, bf16[100,512]{1,0:T(8,128)(2,1)S(1)}) all-reduce(f32[560,512]{1,0:T(8,128)S(1)} %fusion.39, f32[100,512]{1,0:T(8,128)S(1)} %copy-done.45), channel_id=1, replica_groups=mesh['seq'=8,'mp'=2,'expert'=2] {'mp','expert'}, use_global_device_ids=true, to_apply=%region_21.22 | all-reduce | flops 337920 | bytes 2027520 | tf_op jit(solution)/shard_map/psum | solution.py:273
  1559.6 6.2 fusion.40
  1566.2 21.6 fusion.124
  1587.9 22.3 fusion.125
  1610.4 21.7 fusion.126
  1636.9 6.5 fusion.10
  1643.4 30.8 all-reduce.5
  1677.6 7.0 fusion.12
  1684.6 77.8 %reduce-scatter.39.cloned.1.call-done = f32[128,1024]{1,0:T(8,128)} async-done(((f32[1024,1024]{1,0:T(8,128)}), f32[128,1024]{1,0:T(8,128)}) %reduce-scatter.39.cloned.1.call-update) | async-done | bytes 524304 | tf_op jit(solution)/shard_map/reduce_scatter | solution.py:304
  1762.4 92.8 %reduce-scatter.41.cloned.1.call-done = f32[1024,128]{1,0:T(8,128)} async-done(((f32[1024,1024]{1,0:T(8,128)}), f32[1024,128]{1,0:T(8,128)}) %reduce-scatter.41.cloned.1.call-update) | async-done | bytes 524304 | tf_op jit(solution)/shard_map/reduce_scatter | solution.py:310
  1855.2 65.5 %reduce-scatter.31.cloned.1.call-done = f32[128,256]{1,0:T(8,128)} async-done(((f32[1024,256]{1,0:T(8,128)}), f32[128,256]{1,0:T(8,128)}) %reduce-scatter.31.cloned.1.call-update) | async-done | bytes 131088 | tf_op jit(solution)/shard_map/reduce_scatter | solution.py:300
  1920.6 66.8 %reduce-scatter.33.cloned.1.call-done = f32[128,256]{1,0:T(8,128)} async-done(((f32[1024,256]{1,0:T(8,128)}), f32[128,256]{1,0:T(8,128)}) %reduce-scatter.33.cloned.1.call-update) | async-done | bytes 131088 | tf_op jit(solution)/shard_map/reduce_scatter | solution.py:301
  1987.4 70.7 %reduce-scatter.29.cloned.1.call-done = f32[128,512]{1,0:T(8,128)} async-done(((f32[1024,512]{1,0:T(8,128)}), f32[128,512]{1,0:T(8,128)}) %reduce-scatter.29.cloned.1.call-update) | async-done | bytes 262160 | tf_op jit(solution)/shard_map/reduce_scatter | solution.py:299
  2058.1 71.6 %reduce-scatter.35.cloned.1.call-done = f32[512,128]{1,0:T(8,128)} async-done(((f32[512,1024]{1,0:T(8,128)}), f32[512,128]{1,0:T(8,128)}) %reduce-scatter.35.cloned.1.call-update) | async-done | bytes 262160 | tf_op jit(solution)/shard_map/reduce_scatter | solution.py:309
  2129.7 71.4 %reduce-scatter.17.cloned.1.call-done = f32[256,256]{1,0:T(8,128)} async-done(((f32[2048,256]{1,0:T(8,128)}), f32[256,256]{1,0:T(8,128)}) %reduce-scatter.17.cloned.1.call-update) | async-done | bytes 262160 | tf_op jit(solution)/shard_map/reduce_scatter | solution.py:293
  2201.1 70.0 %reduce-scatter.19.cloned.1.call-done = f32[256,256]{1,0:T(8,128)} async-done(((f32[2048,256]{1,0:T(8,128)}), f32[256,256]{1,0:T(8,128)}) %reduce-scatter.19.cloned.1.call-update) | async-done | bytes 262160 | tf_op jit(solution)/shard_map/reduce_scatter | solution.py:294
  2271.1 92.9 %reduce-scatter.15.cloned.1.call-done = f32[256,512]{1,0:T(8,128)} async-done(((f32[2048,512]{1,0:T(8,128)}), f32[256,512]{1,0:T(8,128)}) %reduce-scatter.15.cloned.1.call-update) | async-done | bytes 524304 | tf_op jit(solution)/shard_map/reduce_scatter | solution.py:292
  2364.0 92.7 %reduce-scatter.21.cloned.1.call-done = f32[512,256]{1,0:T(8,128)} async-done(((f32[512,2048]{1,0:T(8,128)}), f32[512,256]{1,0:T(8,128)}) %reduce-scatter.21.cloned.1.call-update) | async-done | bytes 524304 | tf_op jit(solution)/shard_map/reduce_scatter | solution.py:307
  2456.7 547.1 %reduce-scatter.23.cloned.1.call-done = f32[256,4096]{1,0:T(8,128)} async-done(((f32[2048,4096]{1,0:T(8,128)}), f32[256,4096]{1,0:T(8,128)}) %reduce-scatter.23.cloned.1.call-update) | async-done | bytes 4194320 | tf_op jit(solution)/shard_map/reduce_scatter | solution.py:296
  3003.8 546.4 %reduce-scatter.25.cloned.1.call-done = f32[256,4096]{1,0:T(8,128)} async-done(((f32[2048,4096]{1,0:T(8,128)}), f32[256,4096]{1,0:T(8,128)}) %reduce-scatter.25.cloned.1.call-update) | async-done | bytes 4194320 | tf_op jit(solution)/shard_map/reduce_scatter | solution.py:297
  3550.3 546.5 %reduce-scatter.27.cloned.1.call-done = f32[4096,256]{1,0:T(8,128)} async-done(((f32[4096,2048]{1,0:T(8,128)}), f32[4096,256]{1,0:T(8,128)}) %reduce-scatter.27.cloned.1.call-update) | async-done | bytes 4194320 | tf_op jit(solution)/shard_map/reduce_scatter | solution.py:308
  (398 shorter events, 137.9 us)
Async XLA Ops:
  7.2 90.8 %copy-start.6 = (bf16[100,1024]{1,0:T(8,128)(2,1)S(1)}, bf16[100,1024]{1,0:T(8,128)(2,1)}, u32[]{:S(2)}) copy-start(bf16[100,1024]{1,0:T(8,128)(2,1)} %param.25) | copy-start | bytes 614404
  7.2 94.6 %all-gather.17.cloned.1.call-start = ((), (), s32[]{:S(2)}) async-start(), calls=%async_computation.14 | async-start | bytes 1179648 | tf_op jit(solution)/shard_map/all_gather | solution.py:164
  8.0 96.2 %all-gather.19.cloned.1.call-start = ((), (), s32[]{:S(2)}) async-start(), calls=%async_computation.15 | async-start | bytes 1179648 | tf_op jit(solution)/shard_map/all_gather | solution.py:165
  8.7 131.7 %all-gather.31.cloned.1.call-start = ((), (), s32[]{:S(2)}) async-start(), calls=%async_computation.21 | async-start | bytes 1179648 | tf_op jit(solution)/shard_map/all_gather | solution.py:170
  9.5 170.5 %all-gather.33.cloned.1.call-start = ((), (), s32[]{:S(2)}) async-start(), calls=%async_computation.22 | async-start | bytes 1179648 | tf_op jit(solution)/shard_map/all_gather | solution.py:180
  10.0 221.5 %all-gather.21.cloned.1.call-start = ((), (), s32[]{:S(2)}) async-start(), calls=%async_computation.16 | async-start | bytes 2359296 | tf_op jit(solution)/shard_map/all_gather | solution.py:163
  10.6 272.9 %all-gather.23.cloned.1.call-start = ((), (), s32[]{:S(2)}) async-start(), calls=%async_computation.17 | async-start | bytes 2359296 | tf_op jit(solution)/shard_map/all_gather | solution.py:178
  11.2 375.2 %all-reduce.21.cloned.1.call-start = ((), (), s32[]{:S(2)}) async-start(), calls=%async_computation.42 | async-start | bytes 10027008 | tf_op jit(solution)/shard_map/psum | solution.py:218
  29.8 201.7 %copy-start.63 = (f32[8,1,256]{2,1,0:T(1,128)}, f32[8,1,256]{2,1,0:T(1,128)S(1)}, u32[]{:S(2)}) copy-start(f32[8,1,256]{2,1,0:T(1,128)S(1)} %convert_element_type.227) | copy-start | bytes 24580
  32.0 199.5 %copy-start.73 = (f32[560]{0:T(1024)}, f32[560]{0:T(1024)S(1)}, u32[]{:S(2)}) copy-start(f32[560]{0:T(1024)S(1)} %fusion.89) | copy-start | bytes 6724
  32.6 109.6 %copy-start.91 = (pred[2]{0:T(512)(128)(4,1)}, pred[2]{0:T(512)(128)(4,1)S(1)}, u32[]{:S(2)}) copy-start(pred[2]{0:T(512)(128)(4,1)S(1)} %get-tuple-element.71) | copy-start | bytes 10
  101.1 440.7 %copy-start.88 = (f32[100]{0:T(128)}, f32[100]{0:T(128)S(1)}, u32[]{:S(2)}) copy-start(f32[100]{0:T(128)S(1)} %mul.444) | copy-start | bytes 1204
  109.6 126.2 %copy-start.37 = (bf16[560,512]{1,0:T(8,128)(2,1)}, bf16[560,512]{1,0:T(8,128)(2,1)S(1)}, u32[]{:S(2)}) copy-start(bf16[560,512]{1,0:T(8,128)(2,1)S(1)} %convolution_convert_fusion.3) | copy-start | bytes 1720324
  109.6 32.5 collective-permute-start
  145.3 89.2 %copy-start.41 = (bf16[13,8,2,256]{3,1,2,0:T(8,128)(2,1)}, bf16[13,8,2,256]{3,1,2,0:T(8,128)(2,1)S(1)}, u32[]{:S(2)}) copy-start(bf16[13,8,2,256]{3,1,2,0:T(8,128)(2,1)S(1)} %copy.94) | copy-start | bytes 319492
  288.7 148.4 %all-gather.35.cloned.1.call-start = ((), (), s32[]{:S(2)}) async-start(), calls=%async_computation.23 | async-start | bytes 2359296 | tf_op jit(solution)/shard_map/all_gather | solution.py:174
  289.4 197.6 %all-gather.37.cloned.1.call-start = ((), (), s32[]{:S(2)}) async-start(), calls=%async_computation.24 | async-start | bytes 2359296 | tf_op jit(solution)/shard_map/all_gather | solution.py:175
  290.2 248.9 %all-gather.39.cloned.1.call-start = ((), (), s32[]{:S(2)}) async-start(), calls=%async_computation.25 | async-start | bytes 2359296 | tf_op jit(solution)/shard_map/all_gather | solution.py:181
  290.8 476.4 %all-gather.25.cloned.1.call-start = ((), (), s32[]{:S(2)}) async-start(), calls=%async_computation.18 | async-start | bytes 18874368 | tf_op jit(solution)/shard_map/all_gather | solution.py:167
  291.5 703.5 %all-gather.27.cloned.1.call-start = ((), (), s32[]{:S(2)}) async-start(), calls=%async_computation.19 | async-start | bytes 18874368 | tf_op jit(solution)/shard_map/all_gather | solution.py:168
  292.1 930.9 %all-gather.29.cloned.1.call-start = ((), (), s32[]{:S(2)}) async-start(), calls=%async_computation.20 | async-start | bytes 18874368 | tf_op jit(solution)/shard_map/all_gather | solution.py:179
  292.8 1085.7 %all-reduce.19.cloned.1.call-start = ((), (), s32[]{:S(2)}) async-start(), calls=%async_computation.41 | async-start | bytes 10027008 | tf_op jit(solution)/shard_map/psum | solution.py:238
  307.7 239.5 %copy-start.61 = (f32[8,1,256]{2,1,0:T(1,128)}, f32[8,1,256]{2,1,0:T(1,128)S(1)}, u32[]{:S(2)}) copy-start(f32[8,1,256]{2,1,0:T(1,128)S(1)} %convert_element_type.228) | copy-start | bytes 24580
  392.8 154.4 %copy-start.67 = (f32[560]{0:T(1024)}, f32[560]{0:T(1024)S(1)}, u32[]{:S(2)}) copy-start(f32[560]{0:T(1024)S(1)} %fusion.90) | copy-start | bytes 6724
  393.5 93.5 %copy-start.20 = (bf16[100,1024]{1,0:T(8,128)(2,1)}, bf16[100,1024]{1,0:T(8,128)(2,1)S(1)}, u32[]{:S(2)}) copy-start(bf16[100,1024]{1,0:T(8,128)(2,1)S(1)} %multiply_convert_fusion.7) | copy-start | bytes 614404
  393.5 145.5 %copy-start.46 = (bf16[100,1024]{1,0:T(8,128)(2,1)S(1)}, bf16[100,1024]{1,0:T(8,128)(2,1)}, u32[]{:S(2)}) copy-start(bf16[100,1024]{1,0:T(8,128)(2,1)} %param.45) | copy-start | bytes 614404
  547.7 219.5 %copy-start.29 = (bf16[560,2048]{1,0:T(8,128)(2,1)}, bf16[560,2048]{1,0:T(8,128)(2,1)S(1)}, u32[]{:S(2)}) copy-start(bf16[560,2048]{1,0:T(8,128)(2,1)S(1)} %multiply_convert_fusion.2) | copy-start | bytes 6881284
  782.5 440.5 %copy-start.28 = (bf16[560,2048]{1,0:T(8,128)(2,1)S(1)}, bf16[560,2048]{1,0:T(8,128)(2,1)}, u32[]{:S(2)}) copy-start(bf16[560,2048]{1,0:T(8,128)(2,1)} %param.44) | copy-start | bytes 6881284
  1280.9 159.2 %all-reduce.23.cloned.1.call-start = ((), (), s32[]{:S(2)}) async-start(), calls=%async_computation.43 | async-start | bytes 5013504 | tf_op jit(solution)/shard_map/psum | solution.py:225
  1281.0 97.5 %copy-start.15 = (f32[100,1024]{1,0:T(8,128)S(1)}, f32[100,1024]{1,0:T(8,128)}, u32[]{:S(2)}) copy-start(f32[100,1024]{1,0:T(8,128)} %copy-done.14) | copy-start | bytes 1228804
  1281.0 97.5 %copy-start.66 = (f32[8,1,128]{2,1,0:T(1,128)S(1)}, f32[8,1,128]{2,1,0:T(1,128)}, u32[]{:S(2)}) copy-start(f32[8,1,128]{2,1,0:T(1,128)} %copy-done.65) | copy-start | bytes 12292
  1281.0 97.5 %copy-start.94 = (f32[100]{0:T(128)S(1)}, f32[100]{0:T(128)}, u32[]{:S(2)}) copy-start(f32[100]{0:T(128)} %copy-done.93) | copy-start | bytes 1204
  1296.8 337.9 %all-reduce.17.cloned.1.call-start = ((), (), s32[]{:S(2)}) async-start(), calls=%async_computation.40 | async-start | bytes 10027008 | tf_op jit(solution)/shard_map/psum | solution.py:273
  1464.5 220.0 %reduce-scatter.37.cloned.1.call-start = ((), (), s32[]{:S(2)}) async-start(), calls=%async_computation.37 | async-start | bytes 4718592 | tf_op jit(solution)/shard_map/reduce_scatter | solution.py:303
  1468.3 294.1 %reduce-scatter.39.cloned.1.call-start = ((), (), s32[]{:S(2)}) async-start(), calls=%async_computation.38 | async-start | bytes 4718592 | tf_op jit(solution)/shard_map/reduce_scatter | solution.py:304
  1472.2 383.0 %reduce-scatter.41.cloned.1.call-start = ((), (), s32[]{:S(2)}) async-start(), calls=%async_computation.39 | async-start | bytes 4718592 | tf_op jit(solution)/shard_map/reduce_scatter | solution.py:310
  1476.1 444.6 %reduce-scatter.31.cloned.1.call-start = ((), (), s32[]{:S(2)}) async-start(), calls=%async_computation.34 | async-start | bytes 1179648 | tf_op jit(solution)/shard_map/reduce_scatter | solution.py:300
  1479.5 16.2 collective-permute-start.1
  1543.1 444.3 %reduce-scatter.33.cloned.1.call-start = ((), (), s32[]{:S(2)}) async-start(), calls=%async_computation.35 | async-start | bytes 1179648 | tf_op jit(solution)/shard_map/reduce_scatter | solution.py:301
  1543.8 514.3 %reduce-scatter.29.cloned.1.call-start = ((), (), s32[]{:S(2)}) async-start(), calls=%async_computation.33 | async-start | bytes 2359296 | tf_op jit(solution)/shard_map/reduce_scatter | solution.py:299
  1545.9 583.8 %reduce-scatter.35.cloned.1.call-start = ((), (), s32[]{:S(2)}) async-start(), calls=%async_computation.36 | async-start | bytes 2359296 | tf_op jit(solution)/shard_map/reduce_scatter | solution.py:309
  1547.8 653.3 %reduce-scatter.17.cloned.1.call-start = ((), (), s32[]{:S(2)}) async-start(), calls=%async_computation.27 | async-start | bytes 2359296 | tf_op jit(solution)/shard_map/reduce_scatter | solution.py:293
  1553.4 717.7 %reduce-scatter.19.cloned.1.call-start = ((), (), s32[]{:S(2)}) async-start(), calls=%async_computation.28 | async-start | bytes 2359296 | tf_op jit(solution)/shard_map/reduce_scatter | solution.py:294
  1554.2 809.8 %reduce-scatter.15.cloned.1.call-start = ((), (), s32[]{:S(2)}) async-start(), calls=%async_computation.26 | async-start | bytes 4718592 | tf_op jit(solution)/shard_map/reduce_scatter | solution.py:292
  1558.5 898.2 %reduce-scatter.21.cloned.1.call-start = ((), (), s32[]{:S(2)}) async-start(), calls=%async_computation.29 | async-start | bytes 4718592 | tf_op jit(solution)/shard_map/reduce_scatter | solution.py:307
  1565.8 1438.1 %reduce-scatter.23.cloned.1.call-start = ((), (), s32[]{:S(2)}) async-start(), calls=%async_computation.30 | async-start | bytes 37748736 | tf_op jit(solution)/shard_map/reduce_scatter | solution.py:296
  1587.8 1962.4 %reduce-scatter.25.cloned.1.call-start = ((), (), s32[]{:S(2)}) async-start(), calls=%async_computation.31 | async-start | bytes 37748736 | tf_op jit(solution)/shard_map/reduce_scatter | solution.py:297
  1610.2 2486.6 %reduce-scatter.27.cloned.1.call-start = ((), (), s32[]{:S(2)}) async-start(), calls=%async_computation.32 | async-start | bytes 37748736 | tf_op jit(solution)/shard_map/reduce_scatter | solution.py:308
  (94 other events, 1405.4 us)
Sparse Core Ops, SparseCore 0:
  10.2 45.0 all-gather.16
  57.4 38.8 all-gather.18
  98.4 41.9 all-gather.30
  142.4 37.6 all-gather.32
  182.0 49.4 all-gather.20
  233.4 50.0 all-gather.22
  288.8 97.5 all-reduce.20
  388.5 48.5 all-gather.34
  439.2 47.7 all-gather.36
  488.9 50.0 all-gather.38
  541.1 225.9 all-gather.24
  769.2 225.7 all-gather.26
  997.0 225.8 all-gather.28
  1281.1 97.4 all-reduce.18
  1381.4 58.7 all-reduce.22
  1464.6 112.6 all-reduce.16
  1581.8 88.6 reduce-scatter.36
  1674.6 87.7 reduce-scatter.38
  1767.0 88.0 reduce-scatter.40
  1859.0 61.5 reduce-scatter.30
  1925.0 62.3 reduce-scatter.32
  1991.5 66.5 reduce-scatter.28
  2062.3 67.3 reduce-scatter.34
  2133.7 67.4 reduce-scatter.16
  2205.2 65.8 reduce-scatter.18
  2275.2 88.7 reduce-scatter.14
  2368.5 88.1 reduce-scatter.20
  2461.1 542.7 reduce-scatter.22
  3008.2 542.0 reduce-scatter.24
  3554.5 542.2 reduce-scatter.26
where the time goes:
time: 4110 us; the launch traced here: 4100 us
  waiting for transfers between devices  3560 us (87%)
  matrix products  252 us (6%)
  blocking collectives  197 us (5%)
    reduce_scatter x1, waiting for transfers between devices, body(): lax.psum_scatter(dwg_p, 'seq', scatter_dimension=0, tiled=True)  547 us
    reduce_scatter x1, waiting for transfers between devices, body(): lax.psum_scatter(dwd_p, 'seq', scatter_dimension=1, tiled=True)  547 us
    reduce_scatter x1, waiting for transfers between devices, body(): lax.psum_scatter(dwu_p, 'seq', scatter_dimension=0, tiled=True)  546 us
    all_gather x1, waiting for transfers between devices, body(): lax.all_gather(gate_prefix, 'seq', axis=0, tiled=True)  220 us
    all_gather x1, waiting for transfers between devices, body(): lax.all_gather(up_prefix, 'seq', axis=0, tiled=True)  213 us
    all_gather x1, waiting for transfers between devices, body(): lax.all_gather(down_prefix, 'seq', axis=1, tiled=True)  212 us
    reduce_scatter x1, waiting for transfers between devices, body(): lax.psum_scatter(dwq_p, 'seq', scatter_dimension=0, tiled=True)  92.9 us
    reduce_scatter x1, waiting for transfers between devices, body(): lax.psum_scatter(dwd_a, 'seq', scatter_dimension=1, tiled=True)  92.8 us
  transfers between devices with their start and end apart: 32, of which 27 were waited for; matrix products, arithmetic and copies ran while one was open for 5% of the time, Pallas kernels for 0%

commit v1 on v0

v1 whole, which is shorter than its diff:
```python
import jax
import jax.numpy as jnp
from jax import lax
from jax.sharding import PartitionSpec as P

IMG = 512
EPS = 1e-06
MASKED = -1e30
BF = jnp.bfloat16
F32 = jnp.float32

SNAKE = (0, 2, 4, 6, 7, 5, 3, 1)


def dot(left, right, left_dim, right_dim):
    return lax.dot_general(
        left, right, (((left_dim,), (right_dim,)), ((), ())), preferred_element_type=F32
    )


def cat(parts, axis=0):
    return parts[0] if len(parts) == 1 else jnp.concatenate(parts, axis=axis)


def pad_rows(block, rows):
    missing = rows - block.shape[0]
    return jnp.pad(block, ((0, missing), (0, 0))) if missing else block


def shift(block, axis, distance):
    count = lax.axis_size(axis)
    return lax.ppermute(block, axis, [(i, (i + distance) % count) for i in range(count)])


def ring_step(block, step):
    pairs = [(SNAKE[i], SNAKE[(i + step) % len(SNAKE)]) for i in range(len(SNAKE))]
    return lax.ppermute(block, "seq", pairs)


def on_ring():
    return lax.axis_size("seq") == len(SNAKE)


def seq_gather(block):
    if not on_ring():
        return [lax.all_gather(block, "seq", axis=0, tiled=True)]
    count = len(SNAKE)
    ahead, behind = [block], [block]
    for _ in range(count // 2):
        ahead.append(ring_step(ahead[-1], -1))
    for _ in range((count - 1) // 2):
        behind.append(ring_step(behind[-1], 1))
    return [cat([behind[k], ahead[k + 1]]) for k in range(count // 2)]


def seq_reduce(groups):
    if not on_ring():
        return lax.psum_scatter(
            groups[0].astype(BF), "seq", scatter_dimension=0, tiled=True
        ).astype(F32)
    half = groups[0].shape[0] // 2
    top = len(groups)
    going = groups[top - 1][half:].astype(BF)
    back = groups[top - 1][:half].astype(BF)
    for k in range(top - 2, -1, -1):
        going = ring_step(going, 1).astype(F32) + groups[k][half:].astype(F32)
        going = going.astype(BF)
        back = ring_step(back, -1).astype(F32) + groups[k][:half].astype(F32)
        if k:
            back = back.astype(BF)
    return back + ring_step(going, 1).astype(F32)


def swap(block, axis):
    return shift(block, axis, 1)


def quad_gather_rel(block):
    across = swap(block, "mp")
    other = swap(jnp.stack([block, across]), "expert")
    return [block, across, other[0], other[1]]


def quad_gather(block):
    m, e = lax.axis_index("mp"), lax.axis_index("expert")
    across = swap(block, "mp")
    mine = jnp.where(m == 0, jnp.stack([block, across]), jnp.stack([across, block]))
    other = swap(mine, "expert")
    both = jnp.where(e == 0, jnp.stack([mine, other], 1), jnp.stack([other, mine], 1))
    return both.reshape((4,) + block.shape)


def quad_reduce(whole):
    m, e = lax.axis_index("mp"), lax.axis_index("expert")
    parts = whole.reshape((2, 2) + whole.shape[1:])
    give = lax.dynamic_index_in_dim(parts, 1 - e, 1, keepdims=False).astype(BF)
    keep = lax.dynamic_index_in_dim(parts, e, 1, keepdims=False).astype(F32)
    pair = keep + swap(give, "expert").astype(F32)
    give = lax.dynamic_index_in_dim(pair, 1 - m, 0, keepdims=False).astype(BF)
    keep = lax.dynamic_index_in_dim(pair, m, 0, keepdims=False)
    return keep + swap(give, "mp").astype(F32)


def quad_reduce_rel(whole):
    parts = whole.reshape((2, 2) + (whole.shape[0] // 4,) + whole.shape[1:])
    pair = parts[0].astype(F32) + swap(parts[1].astype(BF), "expert").astype(F32)
    return (pair[0] + swap(pair[1].astype(BF), "mp").astype(F32)).astype(BF)


def hidden_first(weight, from_rows):
    count = lax.axis_size("seq")
    if from_rows:
        depth, width = weight.shape
        parts = weight.reshape(depth, count, width // count).transpose(1, 2, 0)
    else:
        width, depth = weight.shape
        parts = weight.reshape(count, width // count, depth)
    parts = lax.all_to_all(parts, "seq", 0, 0, tiled=True)
    return parts.transpose(1, 0, 2).reshape(width // count, count * depth)


def hidden_back(grad, to_rows):
    count = lax.axis_size("seq")
    width, full = grad.shape
    depth = full // count
    parts = grad.reshape(width, count, depth).transpose(1, 0, 2)
    parts = lax.all_to_all(parts, "seq", 0, 0, tiled=True)
    if to_rows:
        return parts.transpose(2, 0, 1).reshape(depth, count * width).astype(F32)
    return parts.reshape(count * width, depth).astype(F32)


def spread(weight, from_rows):
    return cat(quad_gather_rel(hidden_first(weight, from_rows)))


def collect(grad, to_rows):
    return hidden_back(quad_reduce_rel(grad), to_rows)


def rms_norm(values, gain_vec):
    return values * lax.rsqrt(jnp.mean(values * values, axis=-1, keepdims=True) + EPS) * gain_vec


def norm_backward(values, gain_vec, grad_normed):
    return jax.vjp(rms_norm, values, gain_vec)[1](grad_normed)


def geglu_act(gate_pre, up_pre):
    return jax.nn.gelu(gate_pre, approximate=True) * up_pre


def attend_forward(query_flat, key_rows, value_rows, keep_mask):
    row_count = query_flat.shape[0]
    head_size = key_rows.shape[1]
    query_heads = query_flat.reshape(row_count, -1, head_size)
    scores = jnp.einsum(
        "qhd,kd->hqk", query_heads, key_rows, preferred_element_type=F32
    ) * (head_size ** (-0.5))
    scores = jnp.where(keep_mask[None, None, :], scores, MASKED)
    expo = jnp.exp(scores - jnp.max(scores, axis=-1, keepdims=True))
    probs = expo / jnp.sum(expo, axis=-1, keepdims=True)
    mixed_rows = jnp.einsum(
        "hqk,kd->qhd", probs.astype(BF), value_rows, preferred_element_type=F32
    )
    return mixed_rows.reshape(row_count, -1).astype(BF), probs


def attend_backward(query_flat, key_rows, value_rows, probs, grad_mixed):
    row_count = query_flat.shape[0]
    head_size = key_rows.shape[1]
    score_scale = head_size ** (-0.5)
    query_heads = query_flat.reshape(row_count, -1, head_size)
    grad_heads = grad_mixed.reshape(row_count, -1, head_size)
    grad_probs = jnp.einsum("qhd,kd->hqk", grad_heads, value_rows, preferred_element_type=F32)
    row_inner = jnp.sum(grad_probs * probs, axis=-1, keepdims=True)
    grad_scores = (probs * (grad_probs - row_inner)).astype(BF)
    grad_query = jnp.einsum("hqk,kd->qhd", grad_scores, key_rows, preferred_element_type=F32)
    grad_query = (grad_query * score_scale).reshape(row_count, -1).astype(BF)
    grad_keys = score_scale * jnp.einsum(
        "hqk,qhd->kd", grad_scores, query_heads, preferred_element_type=F32
    )
    grad_values = jnp.einsum(
        "hqk,qhd->kd", probs.astype(BF), grad_heads, preferred_element_type=F32
    )
    return grad_query, jnp.concatenate([grad_keys, grad_values], axis=1)


def feed_forward(normed_groups, cot_groups, w_gate, w_up, w_down):
    y_groups, gn_groups, mids, d_gates, d_ups = [], [], [], [], []
    for normed, cot in zip(normed_groups, cot_groups):
        gate_pre = dot(normed, w_gate, 1, 1)
        up_pre = dot(normed, w_up, 1, 1)
        grad_hidden = dot(cot, w_down, 1, 1)
        mid, pullback = jax.vjp(geglu_act, gate_pre, up_pre)
        d_gate, d_up = pullback(grad_hidden)
        mid, d_gate, d_up = mid.astype(BF), d_gate.astype(BF), d_up.astype(BF)
        gn_groups.append((dot(d_gate, w_gate, 1, 0) + dot(d_up, w_up, 1, 0)).astype(BF))
        y_groups.append(dot(mid, w_down, 1, 0).astype(BF))
        mids.append(mid)
        d_gates.append(d_gate)
        d_ups.append(d_up)
    return y_groups, gn_groups, cat(mids), cat(d_gates), cat(d_ups)


def weight_grad(left, right):
    return dot(left, right, 0, 0).astype(BF)


def body(
    hidden_prefix,
    hidden_action,
    norm1_prefix,
    query_prefix,
    key_prefix,
    value_prefix,
    out_prefix,
    norm2_prefix,
    gate_prefix,
    up_prefix,
    down_prefix,
    norm1_action,
    query_action,
    key_action,
    value_action,
    out_action,
    norm2_action,
    gate_action,
    up_action,
    down_action,
    cot_prefix,
    cot_action,
    instr_len,
    slot_source,
):
    seq_index = lax.axis_index("seq")
    episodes = lax.axis_size("seq")
    quad = lax.axis_size("mp") * lax.axis_size("expert")
    mine = lax.axis_index("mp") * lax.axis_size("expert") + lax.axis_index("expert")
    prefix_rows, action_rows_all = hidden_prefix.shape[0], hidden_action.shape[0]
    slot_count = slot_source.shape[0]
    action_rows = action_rows_all // slot_count
    head_size = key_prefix.shape[1]
    head_cols = query_prefix.shape[1]
    part_p = -(-prefix_rows // (16 * quad)) * 16
    part_a = -(-action_rows_all // (16 * quad)) * 16
    kv_cols = 2 * head_size // quad

    def quarter_kv(w_key, w_value):
        return lax.dynamic_slice_in_dim(
            jnp.concatenate([w_key, w_value], axis=1), mine * kv_cols, kv_cols, axis=1
        )

    early_cols = head_cols + kv_cols
    depth_p, depth_a = query_prefix.shape[0], query_action.shape[0]
    gains = jnp.concatenate([norm1_prefix, norm2_prefix, norm1_action, norm2_action])
    gain_rows = -(-gains.shape[0] // (16 * early_cols)) * 16
    gain_block = jnp.pad(gains, (0, gain_rows * early_cols - gains.shape[0]))
    early = jnp.concatenate(
        [
            jnp.concatenate([query_prefix, quarter_kv(key_prefix, value_prefix)], axis=1),
            jnp.concatenate([query_action, quarter_kv(key_action, value_action)], axis=1),
            gain_block.reshape(gain_rows, early_cols),
        ],
        axis=0,
    )
    early = lax.all_gather(early, "seq", axis=0, tiled=False)
    w_in_p = early[:, :depth_p].reshape(-1, early_cols)
    w_in_a = early[:, depth_p : depth_p + depth_a].reshape(-1, early_cols)
    gains = early[:, depth_p + depth_a :].reshape(episodes, -1)
    gain1_p = gains[:, :depth_p].reshape(-1).astype(F32)
    gain2_p = gains[:, depth_p : 2 * depth_p].reshape(-1).astype(F32)
    gain1_a = gains[:, 2 * depth_p : 2 * depth_p + depth_a].reshape(-1).astype(F32)
    gain2_a = gains[:, 2 * depth_p + depth_a : 2 * (depth_p + depth_a)].reshape(-1).astype(F32)

    w_gate_p, w_up_p = spread(gate_prefix, True), spread(up_prefix, True)
    w_gate_a, w_up_a = spread(gate_action, True), spread(up_action, True)
    late = jnp.concatenate([out_prefix, out_action], axis=1)
    late = lax.all_gather(late, "seq", axis=0, tiled=False)
    w_out_p = late[:, :, :depth_p].transpose(1, 0, 2).reshape(head_cols, -1)
    w_out_a = late[:, :, depth_p:].transpose(1, 0, 2).reshape(head_cols, -1)
    w_down_p, w_down_a = spread(down_prefix, False), spread(down_action, False)

    positions = jnp.arange(prefix_rows, dtype=jnp.int32)
    keep_prefix = positions < IMG + instr_len[seq_index]
    live_slot = slot_source >= 0
    offsets = jnp.where(live_slot, slot_source, 0)
    source_ep = (seq_index - offsets + episodes) % episodes
    keep_slots = (positions[None, :] < IMG + instr_len[source_ep][:, None]) & live_slot[:, None]
    keep_all = jnp.concatenate(
        [keep_slots, jnp.ones((slot_count, action_rows), dtype=bool)], axis=1
    )
    from_prev = slot_source == 1
    from_here = slot_source == 0
    live_rows = jnp.repeat(live_slot.astype(F32), action_rows)[:, None]

    def own_part(rows, part):
        return lax.dynamic_slice_in_dim(pad_rows(rows, quad * part), mine * part, part, axis=0)

    x_p, x_a = own_part(hidden_prefix, part_p), own_part(hidden_action, part_a)
    x_p, x_a = x_p.astype(F32), x_a.astype(F32)
    live_a = own_part(live_rows, part_a)
    cot_p, cot_a = own_part(cot_prefix, part_p), own_part(cot_action, part_a)
    cot_full_p = seq_gather(cot_p)
    cot_full_a = seq_gather((cot_a.astype(F32) * live_a).astype(BF))

    normed1_p = rms_norm(hidden_prefix.astype(F32), gain1_p).astype(BF)
    normed1_a = rms_norm(hidden_action.astype(F32), gain1_a).astype(BF)
    in_p, in_a = dot(normed1_p, w_in_p, 1, 0).astype(BF), dot(normed1_a, w_in_a, 1, 0).astype(BF)
    query_p, query_a = in_p[:, :head_cols], in_a[:, :head_cols]
    kv_both = quad_gather(jnp.concatenate([in_p[:, head_cols:], in_a[:, head_cols:]], axis=0))
    kv_both = kv_both.transpose(1, 0, 2).reshape(-1, 2 * head_size)
    kv_p, kv_a = kv_both[:prefix_rows], kv_both[prefix_rows:]
    kv_prev = shift(kv_p, "seq", 1)
    keys_p, values_p = kv_p[:, :head_size], kv_p[:, head_size:]
    mixed_p, probs_p = attend_forward(query_p, keys_p, values_p, keep_prefix)
    kv_slots = jnp.where(from_prev[:, None, None], kv_prev[None], kv_p[None])
    kv_slots = jnp.concatenate([kv_slots, kv_a.reshape(slot_count, action_rows, -1)], axis=1)
    keys_slots, values_slots = kv_slots[:, :, :head_size], kv_slots[:, :, head_size:]
    query_slots = query_a.reshape(slot_count, action_rows, -1)
    mixed_slots, probs_a = jax.vmap(attend_forward)(
        query_slots, keys_slots, values_slots, keep_all
    )
    mixed_a = mixed_slots.reshape(action_rows_all, -1)
    attn_p = dot(pad_rows(mixed_p, quad * part_p), w_out_p, 1, 0)
    attn_a = dot(pad_rows(mixed_a, quad * part_a), w_out_a, 1, 0)
    middle_p = x_p + quad_reduce(attn_p.reshape(quad, part_p, -1))
    middle_a = x_a + live_a * quad_reduce(attn_a.reshape(quad, part_a, -1))

    normed2_p = seq_gather(rms_norm(middle_p, gain2_p).astype(BF))
    normed2_a = seq_gather(rms_norm(middle_a, gain2_a).astype(BF))
    y_p, gn2_p, mid_p, d_gate_p, d_up_p = feed_forward(
        normed2_p, cot_full_p, w_gate_p, w_up_p, w_down_p
    )
    y_a, gn2_a, mid_a, d_gate_a, d_up_a = feed_forward(
        normed2_a, cot_full_a, w_gate_a, w_up_a, w_down_a
    )
    gn2_p, gn2_a = seq_reduce(gn2_p), seq_reduce(gn2_a)
    normed2_p, normed2_a = cat(normed2_p), cat(normed2_a)
    cot_full_p, cot_full_a = cat(cot_full_p), cat(cot_full_a)
    y_p = (middle_p + seq_reduce(y_p)).astype(BF)
    y_a = (middle_a + live_a * seq_reduce(y_a)).astype(BF)

    dmid_norm_p, dgain2_p = norm_backward(middle_p, gain2_p, gn2_p)
    dmid_norm_a, dgain2_a = norm_backward(middle_a, gain2_a, gn2_a)
    dmid_p = cot_p.astype(F32) + dmid_norm_p
    dmid_a = cot_a.astype(F32) + dmid_norm_a
    dao_p = quad_gather(dmid_p.astype(BF)).reshape(quad * part_p, -1)[:prefix_rows]
    dao_a = quad_gather((dmid_a * live_a).astype(BF)).reshape(quad * part_a, -1)
    dao_a = dao_a[:action_rows_all]

    dmix_p, dmix_a = dot(dao_p, w_out_p, 1, 1).astype(BF), dot(dao_a, w_out_a, 1, 1).astype(BF)
    dq_slots, dkv_slots = jax.vmap(attend_backward)(
        query_slots,
        keys_slots,
        values_slots,
        probs_a,
        dmix_a.reshape(slot_count, action_rows, -1),
    )
    dkv_pre = dkv_slots[:, :prefix_rows]
    dkv_a = dkv_slots[:, prefix_rows:].reshape(action_rows_all, -1)
    to_prev = jnp.sum(jnp.where(from_prev[:, None, None], dkv_pre, 0.0), axis=0)
    to_here = jnp.sum(jnp.where(from_here[:, None, None], dkv_pre, 0.0), axis=0)
    returned = shift(to_prev.astype(BF), "seq", -1).astype(F32)
    dq_p, dkv_p = attend_backward(query_p, keys_p, values_p, probs_p, dmix_p)
    dkv_p = dkv_p + to_here + returned
    dq_a = dq_slots.reshape(action_rows_all, -1)

    dkv_both = jnp.concatenate([dkv_p, dkv_a], axis=0)
    dkv_both = dkv_both.reshape(-1, quad, kv_cols).transpose(1, 0, 2)
    dkv_both = quad_reduce(dkv_both).astype(BF)
    din_p = jnp.concatenate([dq_p, dkv_both[:prefix_rows]], axis=1)
    din_a = jnp.concatenate([dq_a, dkv_both[prefix_rows:]], axis=1)
    gn1_p = dot(pad_rows(din_p, quad * part_p), w_in_p, 1, 1)
    gn1_a = dot(pad_rows(din_a, quad * part_a), w_in_a, 1, 1)
    gn1_p = quad_reduce(gn1_p.reshape(quad, part_p, -1))
    gn1_a = quad_reduce(gn1_a.reshape(quad, part_a, -1))
    dx_norm_p, dgain1_p = norm_backward(x_p, gain1_p, gn1_p)
    dx_norm_a, dgain1_a = norm_backward(x_a, gain1_a, gn1_a)
    dx_p = quad_gather((dmid_p + dx_norm_p).astype(BF)).reshape(quad * part_p, -1)
    dx_a = quad_gather((dmid_a + dx_norm_a).astype(BF)).reshape(quad * part_a, -1)
    dx_p = dx_p[:prefix_rows].astype(F32)
    dx_a = dx_a[:action_rows_all].astype(F32)
    y_p = quad_gather(y_p).reshape(quad * part_p, -1)[:prefix_rows]
    y_a = quad_gather(y_a).reshape(quad * part_a, -1)[:action_rows_all]

    dwd_p = collect(weight_grad(mid_p, cot_full_p), False)
    dwd_a = collect(weight_grad(mid_a, cot_full_a), False)
    dwg_p = collect(weight_grad(d_gate_p, normed2_p), True)
    dwg_a = collect(weight_grad(d_gate_a, normed2_a), True)
    dwu_p = collect(weight_grad(d_up_p, normed2_p), True)
    dwu_a = collect(weight_grad(d_up_a, normed2_a), True)

    dwo = jnp.concatenate(
        [
            weight_grad(mixed_p, dao_p).reshape(head_cols, episodes, -1),
            weight_grad(mixed_a, dao_a).reshape(head_cols, episodes, -1),
        ],
        axis=2,
    ).transpose(1, 0, 2)
    dwo = lax.psum_scatter(dwo, "seq", scatter_dimension=0, tiled=False).astype(F32)
    dw_in = jnp.concatenate(
        [
            weight_grad(normed1_p, din_p).reshape(episodes, -1, early_cols),
            weight_grad(normed1_a, din_a).reshape(episodes, -1, early_cols),
        ],
        axis=1,
    )
    dw_in = lax.psum_scatter(dw_in, "seq", scatter_dimension=0, tiled=False)
    dw_kv = quad_gather(dw_in[:, head_cols:]).transpose(1, 0, 2).reshape(-1, 2 * head_size)
    dw_kv = dw_kv.astype(F32)
    dw_in = dw_in.astype(F32)

    dgains = jnp.concatenate(
        [g.reshape(episodes, -1) for g in (dgain1_p, dgain2_p, dgain1_a, dgain2_a)], axis=1
    )
    dgains = lax.psum_scatter(dgains, "seq", scatter_dimension=0, tiled=False)
    dgains = lax.psum(dgains, ("mp", "expert"))
    return (
        y_p,
        y_a,
        dx_p,
        dx_a,
        dgains[:depth_p],
        dw_in[:depth_p, :head_cols],
        dw_kv[:depth_p, :head_size],
        dw_kv[:depth_p, head_size:],
        dwo[:, :depth_p],
        dgains[depth_p : 2 * depth_p],
        dwg_p,
        dwu_p,
        dwd_p,
        dgains[2 * depth_p : 2 * depth_p + depth_a],
        dw_in[depth_p:, :head_cols],
        dw_kv[depth_p:, :head_size],
        dw_kv[depth_p:, head_size:],
        dwo[:, depth_p:],
        dgains[2 * depth_p + depth_a :],
        dwg_a,
        dwu_a,
        dwd_a,
    )


def solution(mesh):
    rows, flat = P("seq", None), P("seq")
    wide, tall = P("seq", ("mp", "expert")), P(("mp", "expert"), "seq")
    one_expert = (flat, wide, rows, rows, tall, flat, wide, wide, tall)
    return jax.shard_map(
        body,
        mesh=mesh,
        in_specs=(rows, rows) + one_expert + one_expert + (rows, rows, P(), flat),
        out_specs=(rows, rows, rows, rows) + one_expert + one_expert,
        check_vma=False,
    )
```

time: 4110 us -> 1300 us (0.32)
  waiting for transfers between devices: 3560 us -> 400 us
  starting transfers between devices: 7.62 us -> 272 us
  local copies, waits for them, and re-layouts: 26.4 us -> 187 us
  blocking collectives: 197 us -> 80.5 us
  other arithmetic: 39.2 us -> 131 us
  matrix products: 252 us -> 204 us
    reduce_scatter x14 -> x2, waiting for transfers between devices: 2410 us -> 0.01 us  [the longest x1 0.01 us: body(): dw_in = lax.psum_scatter(dw_in, 'seq', scatter_dimension=0, tiled=False)]
    all_gather x12 -> x2, waiting for transfers between devices: 945 us -> 0.01 us  [the longest x1 0.01 us: body(): late = lax.all_gather(late, 'seq', axis=0, tiled=False)]
    ppermute x2 -> x108, waiting for transfers between devices: 6.76 us -> 300 us  [the longest x52 168 us: shift(): lax.ppermute(block, axis, [(i, (i + distance) % count) for i in range(cou...]
    ppermute x2 -> x108, starting transfers between devices: 5.68 us -> 213 us  [the longest x52 110 us: shift(): lax.ppermute(block, axis, [(i, (i + distance) % count) for i in range(cou...]
    psum x4 -> x0, waiting for transfers between devices: 190 us -> none  [the longest x1 81.4 us: body(): gn2_p, gn2_a = lax.psum((gn2_p, gn2_a), ('mp', 'expert'))]
    all_gather x6 -> x0, blocking collectives: 122 us -> none  [the longest x1 26.9 us: body(): lax.all_gather(key_action, 'seq', axis=0, tiled=True)]
    all_to_all x0 -> x11, waiting for transfers between devices: none -> 99.6 us  [the longest x5 80.2 us: hidden_first(): parts = lax.all_to_all(parts, 'seq', 0, 0, tiled=True)]
    unnamed x231 -> x352, local copies, waits for them, and re-layouts: 14.8 us -> 77.5 us
  transfers between devices with their start and end apart: 32 -> 123, of which waited for: 27 -> 50; matrix products, arithmetic and copies ran while one was open for 5% -> 39% of each run, Pallas kernels for 0% -> 0%
where the time goes in v1:
time: 1300 us; the launch traced here: 1290 us
  waiting for transfers between devices  400 us (31%)
  starting transfers between devices  272 us (21%)
  matrix products  204 us (16%)
  local copies, waits for them, and re-layouts  187 us (14%)
  other arithmetic  131 us (10%)
  blocking collectives  80.5 us (6%)
  between operations  17.7 us (1%)
    dot_general x66, matrix products, dot(): lax.dot_general(left, right, (((left_dim,), (right_dim,)), ((), ())), pre...  189 us
    ppermute x52, waiting for transfers between devices, shift(): lax.ppermute(block, axis, [(i, (i + distance) % count) for i in range(cou...  168 us
    ppermute x56, waiting for transfers between devices, ring_step(): return lax.ppermute(block, 'seq', pairs)  132 us
    ppermute x52, starting transfers between devices, shift(): lax.ppermute(block, axis, [(i, (i + distance) % count) for i in range(cou...  110 us
    ppermute x56, starting transfers between devices, ring_step(): return lax.ppermute(block, 'seq', pairs)  103 us
    all_to_all x5, waiting for transfers between devices, hidden_first(): parts = lax.all_to_all(parts, 'seq', 0, 0, tiled=True)  80.2 us
    unnamed x352, local copies, waits for them, and re-layouts  77.5 us
    unnamed x1, blocking collectives  55 us
  transfers between devices with their start and end apart: 123, of which 50 were waited for; matrix products, arithmetic and copies ran while one was open for 39% of the time, Pallas kernels for 0%

profile of v1, /device:TPU:1, one launch (start us, length us, event | category | flops | bytes accessed | tf_op | source)
XLA Modules:
  0.0 1291.8 jit_solution(15623483853370465023)
XLA Ops:
  9.2 6.4 all-to-all-start.3
  22.9 12.0 all_to_all.60
  34.8 8.0 all-to-all-start.5
  45.3 6.9 all-to-all-done.5
  60.5 68.0 %all-to-all-done = bf16[8,512,256]{2,1,0:T(8,128)(2,1)S(1)} async-done(((bf16[8,512,256]{2,1,0:T(8,128)(2,1)}), bf16[8,512,256]{2,1,0:T(8,128)(2,1)S(1)}, u32[]{:S(2)}, u32[]{:S(2)}) %all-to-all-start) | async-done | bytes 2097184 | tf_op jit(solution)/shard_map/all_to_all | solution.py:118
  146.3 50.6 %collective-permute-done.70 = bf16[32,1024]{1,0:T(8,128)(2,1)S(1)} collective-permute-done((bf16[32,1024]{1,0:T(8,128)(2,1)S(1)}, bf16[32,1024]{1,0:T(8,128)(2,1)S(1)}, u32[]{:S(2)}, u32[]{:S(2)}) %collective-permute-start.70) | collective-permute-done | bytes 65568 | tf_op jit(solution)/shard_map/ppermute | solution.py:37
  197.8 39.6 %collective-permute-start.68 = (bf16[32,1024]{1,0:T(8,128)(2,1)S(1)}, bf16[32,1024]{1,0:T(8,128)(2,1)S(1)}, u32[]{:S(2)}, u32[]{:S(2)}) collective-permute-start(bf16[32,1024]{1,0:T(8,128)(2,1)S(1)} %collective-permute-done.67), channel_id=1, source_target_pairs={{0,8},{8,16},{16,24},{24,28},{28,20},{20,12},{12,4},{4,0},{1,9},{9... | collective-permute-start | bytes 196616 | tf_op jit(solution)/shard_map/ppermute | solution.py:37
  262.7 6.3 collective-permute-start.37
  275.5 14.5 %collective-permute-done.55 = bf16[144,2048]{1,0:T(8,128)(2,1)} collective-permute-done((bf16[144,2048]{1,0:T(8,128)(2,1)}, bf16[144,2048]{1,0:T(8,128)(2,1)}, u32[]{:S(2)}, u32[]{:S(2)}) %collective-permute-start.55) | collective-permute-done | bytes 589856 | tf_op jit(solution)/shard_map/ppermute | solution.py:37
  290.0 5.5 collective-permute-start.56
  295.5 14.8 %collective-permute-start.53 = (bf16[144,2048]{1,0:T(8,128)(2,1)}, bf16[144,2048]{1,0:T(8,128)(2,1)}, u32[]{:S(2)}, u32[]{:S(2)}) collective-permute-start(bf16[144,2048]{1,0:T(8,128)(2,1)} %collective-permute-done.52), channel_id=1, source_target_pairs={{0,8},{8,16},{16,24},{24,28},{28,20},{20,12},{12,4},{4,0},{1,9},{9... | collective-permute-start | bytes 1769480 | tf_op jit(solution)/shard_map/ppermute | solution.py:37
  330.8 6.4 collective-permute-done.57
  385.9 18.7 %collective-permute-done.13 = bf16[512,2048]{0,1:T(8,128)(2,1)} collective-permute-done((bf16[512,2048]{0,1:T(8,128)(2,1)}, bf16[512,2048]{0,1:T(8,128)(2,1)}, u32[]{:S(2)}, u32[]{:S(2)}) %collective-permute-start.13) | collective-permute-done | bytes 2097184 | tf_op jit(solution)/shard_map/ppermute | solution.py:32
  408.7 11.8 collective-permute-start.14
  420.5 32.7 %collective-permute-done = bf16[660,128]{1,0:T(8,128)(2,1)S(1)} collective-permute-done((bf16[660,128]{1,0:T(8,128)(2,1)S(1)}, bf16[660,128]{1,0:T(8,128)(2,1)S(1)}, u32[]{:S(2)}, u32[]{:S(2)}) %collective-permute-start) | collective-permute-done | bytes 168992 | tf_op jit(solution)/shard_map/ppermute | solution.py:32
  454.0 6.0 collective-permute-start.1
  483.5 6.3 collective-permute-done.26
  541.8 10.2 collective-permute-start.16
  562.6 5.6 collective-permute-start.102
  598.6 10.4 collective-permute-done.3
  650.4 7.2 fusion.68
  684.4 6.7 fusion.61
  691.0 5.9 fusion.361
  719.8 6.6 fusion.54
  726.5 8.3 fusion.360
  748.8 6.6 fusion.47
  755.4 5.5 fusion.359
  780.0 9.4 collective-permute-done.17
  792.5 15.6 %convolution_convert_fusion.2 = bf16[2048,2048]{1,0:T(8,128)(2,1)} fusion(bf16[1152,2048]{1,0:T(8,128)(2,1)} %get-tuple-element.164, bf16[288,2048]{1,0:T(8,128)(2,1)S(1)} %copy-done.138, bf16[288,2048]{1,0:T(8,128)(2,1)S(1)} %copy-done.137, bf16[288,2048]{1,0:T(8,128)(2,1)S(1)} %copy-done.135, bf16[288,2048]{1,0:T(8,128)(2,1)S(1)} %copy-done.133), kind=kOutput, calls=%fused_computation.11 | convolution fusion | flops 9686745088 | bytes 17825792 | tf_op jit(solution)/shard_map/dot_general | solution.py:16
  809.0 5.7 collective-permute-done.18
  816.9 14.2 %convolution_convert_fusion.1 = bf16[2048,2048]{1,0:T(8,128)(2,1)S(1)} fusion(bf16[1152,2048]{1,0:T(8,128)(2,1)} %get-tuple-element.164, bf16[288,2048]{1,0:T(8,128)(2,1)} %copy-done.144, bf16[288,2048]{1,0:T(8,128)(2,1)} %copy-done.143, bf16[288,2048]{1,0:T(8,128)(2,1)S(1)} %copy-done.142, bf16[288,2048]{1,0:T(8,128)(2,1)S(1)} %copy-done.140), kind=kOutput, calls=%fused_computation.10 | convolution fusion | flops 9686745088 | bytes 17825792 | tf_op jit(solution)/shard_map/dot_general | solution.py:16
  834.0 7.2 collective-permute-done.22
  855.5 10.2 collective-permute-start.96
  869.6 16.4 %convolution_convert_fusion = bf16[2048,2048]{1,0:T(8,128)(2,1)} fusion(bf16[1152,2048]{1,0:T(8,128)(2,1)} %constant_dynamic-update-slice_fusion.20, bf16[288,2048]{1,0:T(8,128)(2,1)} %get-tuple-element.131, bf16[288,2048]{1,0:T(8,128)(2,1)} %get-tuple-element.128, bf16[288,2048]{1,0:T(8,128)(2,1)} %get-tuple-element.125, ...), kind=kOutput, calls=%fused_computation.9 | convolution fusion | flops 9686745088 | bytes 17825792 | tf_op jit(solution)/shard_map/dot_general | solution.py:16
  886.2 8.7 collective-permute-start.66
  947.2 5.4 all-to-all-start.11
  970.2 18.4 %collective-permute-done.24 = bf16[144,2048]{1,0:T(8,128)(2,1)} collective-permute-done((bf16[144,2048]{1,0:T(8,128)(2,1)S(1)}, bf16[144,2048]{1,0:T(8,128)(2,1)}, u32[]{:S(2)}, u32[]{:S(2)}) %collective-permute-start.24) | collective-permute-done | bytes 589856 | tf_op jit(solution)/shard_map/ppermute | solution.py:32
  1006.4 5.4 convert_add_fusion.1
  1031.4 29.6 %collective-permute-done.99 = bf16[512,2048]{1,0:T(8,128)(2,1)} collective-permute-done((bf16[512,2048]{1,0:T(8,128)(2,1)}, bf16[512,2048]{1,0:T(8,128)(2,1)}, u32[]{:S(2)}, u32[]{:S(2)}) %collective-permute-start.99) | collective-permute-done | bytes 2097184 | tf_op jit(solution)/shard_map/ppermute | solution.py:32
  1084.9 22.4 %collective-permute-done.91 = bf16[32,1024]{1,0:T(8,128)(2,1)S(1)} collective-permute-done((bf16[32,1024]{1,0:T(8,128)(2,1)S(1)}, bf16[32,1024]{1,0:T(8,128)(2,1)S(1)}, u32[]{:S(2)}, u32[]{:S(2)}) %collective-permute-start.91) | collective-permute-done | bytes 65568 | tf_op jit(solution)/shard_map/ppermute | solution.py:32
  1115.8 8.5 collective-permute-done.87
  1125.7 16.8 %all-to-all-done.7 = bf16[8,512,256]{1,2,0:T(8,128)(2,1)} async-done(((bf16[8,512,256]{1,2,0:T(8,128)(2,1)}), bf16[8,512,256]{1,2,0:T(8,128)(2,1)}, u32[]{:S(2)}, u32[]{:S(2)}) %all-to-all-start.7) | async-done | bytes 2097184 | tf_op jit(solution)/shard_map/all_to_all | solution.py:127
  1142.5 9.7 all-to-all-start.8
  1160.1 9.5 collective-permute-done.92
  1174.0 55.0 %all-reduce.11 = f32[8,768]{1,0:T(8,128)S(1)} all-reduce(f32[8,768]{1,0:T(8,128)S(1)} %pad_maximum_fusion.27), channel_id=4, replica_groups=mesh['seq'=8,'mp'=2,'expert'=2] {'seq'}, use_global_device_ids=true, to_apply=%region_22.23.clone | all-reduce | flops 6144 | bytes 49152
  1229.6 13.5 %psum.7 = f32[768]{0:T(1024)S(1)} all-reduce(f32[768]{0:T(1024)S(1)} %dynamic-slice_reduce_fusion), channel_id=1, replica_groups=mesh['seq'=8,'mp'=2,'expert'=2] {'mp','expert'}, use_global_device_ids=true, to_apply=%region_23.24 | all-reduce | flops 768 | bytes 6144 | tf_op jit(solution)/shard_map/psum | solution.py:418
  1252.9 5.6 copy.304
  1263.7 5.6 copy.305
  (876 shorter events, 593.8 us)
Async XLA Ops:
  15.5 332.7 %all-gather.7.cloned.1.call-start = ((), (), s32[]{:S(2)}) async-start(), calls=%async_computation.17 | async-start | bytes 3538944 | tf_op jit(solution)/shard_map/all_gather | solution.py:279
  52.3 76.2 %all-to-all-start = ((bf16[8,512,256]{2,1,0:T(8,128)(2,1)}), bf16[8,512,256]{2,1,0:T(8,128)(2,1)S(1)}, u32[]{:S(2)}, u32[]{:S(2)}) async-start(bf16[8,512,256]{2,1,0:T(8,128)(2,1)} %bitcast.656), calls=%async_computation | async-start | bytes 4194304 | tf_op jit(solution)/shard_map/all_to_all | solution.py:118
  128.5 119.1 %all-to-all-start.1 = ((bf16[8,512,256]{2,1,0:T(8,128)(2,1)}), bf16[8,512,256]{2,1,0:T(8,128)(2,1)}, u32[]{:S(2)}, u32[]{:S(2)}) async-start(bf16[8,512,256]{2,1,0:T(8,128)(2,1)} %bitcast.652), calls=%async_computation.1 | async-start | bytes 4194304 | tf_op jit(solution)/shard_map/all_to_all | solution.py:118
  132.9 243.2 %all-gather.5.cloned.1.call-start = ((), (), s32[]{:S(2)}) async-start(), calls=%async_computation.16 | async-start | bytes 4608000 | tf_op jit(solution)/shard_map/all_gather | solution.py:267
  135.1 122.2 %collective-permute-start.54 = (bf16[144,2048]{1,0:T(8,128)(2,1)S(1)}, bf16[144,2048]{1,0:T(8,128)(2,1)}, u32[]{:S(2)}, u32[]{:S(2)}) collective-permute-start(bf16[144,2048]{1,0:T(8,128)(2,1)S(1)} %get-tuple-element.103), channel_id=1, source_target_pairs={{0,4},{8,0},{16,8},{24,16},{28,24},{20,28},{12,20},{4,12},{1,5},{9... | collective-permute-start | bytes 1769480 | tf_op jit(solution)/shard_map/ppermute | solution.py:37
  136.7 122.0 %collective-permute-start.51 = (bf16[144,2048]{1,0:T(8,128)(2,1)S(1)}, bf16[144,2048]{1,0:T(8,128)(2,1)}, u32[]{:S(2)}, u32[]{:S(2)}) collective-permute-start(bf16[144,2048]{1,0:T(8,128)(2,1)S(1)} %get-tuple-element.103), channel_id=1, source_target_pairs={{0,8},{8,16},{16,24},{24,28},{28,20},{20,12},{12,4},{4,0},{1,9},{9... | collective-permute-start | bytes 1769480 | tf_op jit(solution)/shard_map/ppermute | solution.py:37
  141.0 56.0 %collective-permute-start.70 = (bf16[32,1024]{1,0:T(8,128)(2,1)S(1)}, bf16[32,1024]{1,0:T(8,128)(2,1)S(1)}, u32[]{:S(2)}, u32[]{:S(2)}) collective-permute-start(bf16[32,1024]{1,0:T(8,128)(2,1)S(1)} %get-tuple-element.99), channel_id=1, source_target_pairs={{0,4},{8,0},{16,8},{24,16},{28,24},{20,28},{12,20},{4,12},{1,5},{9... | collective-permute-start | bytes 196616 | tf_op jit(solution)/shard_map/ppermute | solution.py:37
  142.4 55.4 %collective-permute-start.67 = (bf16[32,1024]{1,0:T(8,128)(2,1)S(1)}, bf16[32,1024]{1,0:T(8,128)(2,1)S(1)}, u32[]{:S(2)}, u32[]{:S(2)}) collective-permute-start(bf16[32,1024]{1,0:T(8,128)(2,1)S(1)} %get-tuple-element.99), channel_id=1, source_target_pairs={{0,8},{8,16},{16,24},{24,28},{28,20},{20,12},{12,4},{4,0},{1,9},{9... | collective-permute-start | bytes 196616 | tf_op jit(solution)/shard_map/ppermute | solution.py:37
  196.9 41.8 %collective-permute-start.71 = (bf16[32,1024]{1,0:T(8,128)(2,1)S(1)}, bf16[32,1024]{1,0:T(8,128)(2,1)S(1)}, u32[]{:S(2)}, u32[]{:S(2)}) collective-permute-start(bf16[32,1024]{1,0:T(8,128)(2,1)S(1)} %collective-permute-done.70), channel_id=1, source_target_pairs={{0,4},{8,0},{16,8},{24,16},{28,24},{20,28},{12,20},{4,12},{1,5},{9... | collective-permute-start | bytes 196616 | tf_op jit(solution)/shard_map/ppermute | solution.py:37
  197.8 41.0 %collective-permute-start.68 = (bf16[32,1024]{1,0:T(8,128)(2,1)S(1)}, bf16[32,1024]{1,0:T(8,128)(2,1)S(1)}, u32[]{:S(2)}, u32[]{:S(2)}) collective-permute-start(bf16[32,1024]{1,0:T(8,128)(2,1)S(1)} %collective-permute-done.67), channel_id=1, source_target_pairs={{0,8},{8,16},{16,24},{24,28},{28,20},{20,12},{12,4},{4,0},{1,9},{9... | collective-permute-start | bytes 196616 | tf_op jit(solution)/shard_map/ppermute | solution.py:37
  247.6 95.7 %all-to-all-start.2 = ((bf16[8,512,256]{2,1,0:T(8,128)(2,1)}), bf16[8,512,256]{2,1,0:T(8,128)(2,1)}, u32[]{:S(2)}, u32[]{:S(2)}) async-start(bf16[8,512,256]{2,1,0:T(8,128)(2,1)} %bitcast.700), calls=%async_computation.2 | async-start | bytes 4194304 | tf_op jit(solution)/shard_map/all_to_all | solution.py:118
  257.3 32.7 %collective-permute-start.55 = (bf16[144,2048]{1,0:T(8,128)(2,1)}, bf16[144,2048]{1,0:T(8,128)(2,1)}, u32[]{:S(2)}, u32[]{:S(2)}) collective-permute-start(bf16[144,2048]{1,0:T(8,128)(2,1)} %collective-permute-done.54), channel_id=1, source_target_pairs={{0,4},{8,0},{16,8},{24,16},{28,24},{20,28},{12,20},{4,12},{1,5},{9... | collective-permute-start | bytes 1769480 | tf_op jit(solution)/shard_map/ppermute | solution.py:37
  258.6 36.9 %collective-permute-start.52 = (bf16[144,2048]{1,0:T(8,128)(2,1)}, bf16[144,2048]{1,0:T(8,128)(2,1)}, u32[]{:S(2)}, u32[]{:S(2)}) collective-permute-start(bf16[144,2048]{1,0:T(8,128)(2,1)} %collective-permute-done.51), channel_id=1, source_target_pairs={{0,8},{8,16},{16,24},{24,28},{28,20},{20,12},{12,4},{4,0},{1,9},{9... | collective-permute-start | bytes 1769480 | tf_op jit(solution)/shard_map/ppermute | solution.py:37
  262.7 51.5 %collective-permute-start.37 = (bf16[2,128,1024]{1,2,0:T(8,128)(2,1)S(1)}, bf16[2,128,1024]{1,2,0:T(8,128)(2,1)S(1)}, u32[]{:S(2)}, u32[]{:S(2)}) collective-permute-start(bf16[2,128,1024]{1,2,0:T(8,128)(2,1)S(1)} %pad_maximum_fusion.16), channel_id=1, source_target_pairs={{0,1},{1,0},{2,3},{3,2},{4,5},{5,4},{6,7},{7,6},{8,9},{9,8},{10,11... | collective-permute-start | bytes 1572872 | tf_op jit(solution)/shard_map/ppermute | solution.py:32
  270.6 52.1 %collective-permute-start.39 = (bf16[2,128,1024]{1,2,0:T(8,128)(2,1)}, bf16[2,128,1024]{1,2,0:T(8,128)(2,1)}, u32[]{:S(2)}, u32[]{:S(2)}) collective-permute-start(bf16[2,128,1024]{1,2,0:T(8,128)(2,1)} %pad_maximum_fusion.17), channel_id=1, source_target_pairs={{0,1},{1,0},{2,3},{3,2},{4,5},{5,4},{6,7},{7,6},{8,9},{9,8},{10,11... | collective-permute-start | bytes 1572872 | tf_op jit(solution)/shard_map/ppermute | solution.py:32
  274.3 44.2 %collective-permute-start.41 = (bf16[2,128,1024]{1,2,0:T(8,128)(2,1)}, bf16[2,128,1024]{1,2,0:T(8,128)(2,1)}, u32[]{:S(2)}, u32[]{:S(2)}) collective-permute-start(bf16[2,128,1024]{1,2,0:T(8,128)(2,1)} %pad_maximum_fusion.18), channel_id=1, source_target_pairs={{0,1},{1,0},{2,3},{3,2},{4,5},{5,4},{6,7},{7,6},{8,9},{9,8},{10,11... | collective-permute-start | bytes 1572872 | tf_op jit(solution)/shard_map/ppermute | solution.py:32
  290.0 33.8 %collective-permute-start.56 = (bf16[144,2048]{1,0:T(8,128)(2,1)}, bf16[144,2048]{1,0:T(8,128)(2,1)}, u32[]{:S(2)}, u32[]{:S(2)}) collective-permute-start(bf16[144,2048]{1,0:T(8,128)(2,1)} %collective-permute-done.55), channel_id=1, source_target_pairs={{0,4},{8,0},{16,8},{24,16},{28,24},{20,28},{12,20},{4,12},{1,5},{9... | collective-permute-start | bytes 1769480 | tf_op jit(solution)/shard_map/ppermute | solution.py:37
  295.5 33.3 %collective-permute-start.53 = (bf16[144,2048]{1,0:T(8,128)(2,1)}, bf16[144,2048]{1,0:T(8,128)(2,1)}, u32[]{:S(2)}, u32[]{:S(2)}) collective-permute-start(bf16[144,2048]{1,0:T(8,128)(2,1)} %collective-permute-done.52), channel_id=1, source_target_pairs={{0,8},{8,16},{16,24},{24,28},{28,20},{20,12},{12,4},{4,0},{1,9},{9... | collective-permute-start | bytes 1769480 | tf_op jit(solution)/shard_map/ppermute | solution.py:37
  317.4 50.1 %collective-permute-start.11 = (bf16[512,2048]{0,1:T(8,128)(2,1)}, bf16[512,2048]{0,1:T(8,128)(2,1)}, u32[]{:S(2)}, u32[]{:S(2)}) collective-permute-start(bf16[512,2048]{0,1:T(8,128)(2,1)} %bitcast.27), channel_id=1, source_target_pairs={{0,2},{2,0},{1,3},{3,1},{4,6},{6,4},{5,7},{7,5},{8,10},{10,8},{9,1... | collective-permute-start | bytes 6291464 | tf_op jit(solution)/shard_map/ppermute | solution.py:32
  342.8 61.8 %collective-permute-start.13 = (bf16[512,2048]{0,1:T(8,128)(2,1)}, bf16[512,2048]{0,1:T(8,128)(2,1)}, u32[]{:S(2)}, u32[]{:S(2)}) collective-permute-start(bf16[512,2048]{0,1:T(8,128)(2,1)} %bitcast.628), channel_id=1, source_target_pairs={{0,2},{2,0},{1,3},{3,1},{4,6},{6,4},{5,7},{7,5},{8,10},{10,8},{9,1... | collective-permute-start | bytes 6291464 | tf_op jit(solution)/shard_map/ppermute | solution.py:32
  347.2 112.8 %collective-permute-start.15 = (bf16[512,2048]{0,1:T(8,128)(2,1)}, bf16[512,2048]{0,1:T(8,128)(2,1)}, u32[]{:S(2)}, u32[]{:S(2)}) collective-permute-start(bf16[512,2048]{0,1:T(8,128)(2,1)} %bitcast.631), channel_id=1, source_target_pairs={{0,2},{2,0},{1,3},{3,1},{4,6},{6,4},{5,7},{7,5},{8,10},{10,8},{9,1... | collective-permute-start | bytes 6291464 | tf_op jit(solution)/shard_map/ppermute | solution.py:32
  372.1 252.0 %collective-permute-start.12 = (bf16[2,512,2048]{1,2,0:T(8,128)(2,1)}, bf16[2,512,2048]{1,2,0:T(8,128)(2,1)}, u32[]{:S(2)}, u32[]{:S(2)}) collective-permute-start(bf16[2,512,2048]{1,2,0:T(8,128)(2,1)} %pad_maximum_fusion.3), channel_id=1, source_target_pairs={{0,1},{1,0},{2,3},{3,2},{4,5},{5,4},{6,7},{7,6},{8,9},{9,8},{10,11... | collective-permute-start | bytes 12582920 | tf_op jit(solution)/shard_map/ppermute | solution.py:32
  384.8 68.3 %collective-permute-start = (bf16[660,128]{1,0:T(8,128)(2,1)S(1)}, bf16[660,128]{1,0:T(8,128)(2,1)S(1)}, u32[]{:S(2)}, u32[]{:S(2)}) collective-permute-start(bf16[660,128]{1,0:T(8,128)(2,1)S(1)} %get-tuple-element.200), channel_id=1, source_target_pairs={{0,2},{2,0},{1,3},{3,1},{4,6},{6,4},{5,7},{7,5},{8,10},{10,8},{9,1... | collective-permute-start | bytes 506888 | tf_op jit(solution)/shard_map/ppermute | solution.py:32
  408.7 218.1 %collective-permute-start.14 = (bf16[2,512,2048]{1,2,0:T(8,128)(2,1)}, bf16[2,512,2048]{1,2,0:T(8,128)(2,1)}, u32[]{:S(2)}, u32[]{:S(2)}) collective-permute-start(bf16[2,512,2048]{1,2,0:T(8,128)(2,1)} %pad_maximum_fusion.4), channel_id=1, source_target_pairs={{0,1},{1,0},{2,3},{3,2},{4,5},{5,4},{6,7},{7,6},{8,9},{9,8},{10,11... | collective-permute-start | bytes 12582920 | tf_op jit(solution)/shard_map/ppermute | solution.py:32
  500.8 51.2 %collective-permute-start.2 = (bf16[2,144,2048]{2,1,0:T(8,128)(2,1)S(1)}, bf16[2,144,2048]{2,1,0:T(8,128)(2,1)S(1)}, u32[]{:S(2)}, u32[]{:S(2)}) collective-permute-start(bf16[2,144,2048]{2,1,0:T(8,128)(2,1)S(1)} %fusion.103), channel_id=1, source_target_pairs={{0,1},{1,0},{2,3},{3,2},{4,5},{5,4},{6,7},{7,6},{8,9},{9,8},{10,11... | collective-permute-start | bytes 3538952 | tf_op jit(solution)/shard_map/ppermute | solution.py:32
  541.8 87.5 %collective-permute-start.16 = (bf16[2,512,2048]{1,2,0:T(8,128)(2,1)}, bf16[2,512,2048]{1,2,0:T(8,128)(2,1)}, u32[]{:S(2)}, u32[]{:S(2)}) collective-permute-start(bf16[2,512,2048]{1,2,0:T(8,128)(2,1)} %pad_maximum_fusion.5), channel_id=1, source_target_pairs={{0,1},{1,0},{2,3},{3,2},{4,5},{5,4},{6,7},{7,6},{8,9},{9,8},{10,11... | collective-permute-start | bytes 12582920 | tf_op jit(solution)/shard_map/ppermute | solution.py:32
  614.6 338.0 %collective-permute-start.50 = (bf16[2,32,1024]{2,1,0:T(8,128)(2,1)}, bf16[2,32,1024]{2,1,0:T(8,128)(2,1)}, u32[]{:S(2)}, u32[]{:S(2)}) collective-permute-start(bf16[2,32,1024]{2,1,0:T(8,128)(2,1)} %maximum_select_fusion.18), channel_id=1, source_target_pairs={{0,1},{1,0},{2,3},{3,2},{4,5},{5,4},{6,7},{7,6},{8,9},{9,8},{10,11... | collective-permute-start | bytes 393224 | tf_op jit(solution)/shard_map/ppermute | solution.py:32
  616.7 319.3 %all-to-all-start.9 = ((bf16[8,128,128]{1,2,0:T(8,128)(2,1)}), bf16[8,128,128]{1,2,0:T(8,128)(2,1)}, u32[]{:S(2)}, u32[]{:S(2)}) async-start(bf16[8,128,128]{1,2,0:T(8,128)(2,1)} %bitcast.203), calls=%async_computation.11 | async-start | bytes 524288 | tf_op jit(solution)/shard_map/all_to_all | solution.py:127
  624.1 45.7 %collective-permute-start.4 = (bf16[144,2048]{1,0:T(8,128)(2,1)S(1)}, bf16[144,2048]{1,0:T(8,128)(2,1)S(1)}, u32[]{:S(2)}, u32[]{:S(2)}) collective-permute-start(bf16[144,2048]{1,0:T(8,128)(2,1)S(1)} %get-tuple-element.105), channel_id=1, source_target_pairs={{0,8},{8,16},{16,24},{24,28},{28,20},{20,12},{12,4},{4,0},{1,9},{9... | collective-permute-start | bytes 1769480 | tf_op jit(solution)/shard_map/ppermute | solution.py:37
  669.8 31.2 %collective-permute-start.5 = (bf16[144,2048]{1,0:T(8,128)(2,1)S(1)}, bf16[144,2048]{1,0:T(8,128)(2,1)S(1)}, u32[]{:S(2)}, u32[]{:S(2)}) collective-permute-start(bf16[144,2048]{1,0:T(8,128)(2,1)S(1)} %collective-permute-done.4), channel_id=1, source_target_pairs={{0,8},{8,16},{16,24},{24,28},{28,20},{20,12},{12,4},{4,0},{1,9},{9... | collective-permute-start | bytes 1769480 | tf_op jit(solution)/shard_map/ppermute | solution.py:37
  701.0 33.8 %collective-permute-start.6 = (bf16[144,2048]{1,0:T(8,128)(2,1)S(1)}, bf16[144,2048]{1,0:T(8,128)(2,1)S(1)}, u32[]{:S(2)}, u32[]{:S(2)}) collective-permute-start(bf16[144,2048]{1,0:T(8,128)(2,1)S(1)} %collective-permute-done.5), channel_id=1, source_target_pairs={{0,8},{8,16},{16,24},{24,28},{28,20},{20,12},{12,4},{4,0},{1,9},{9... | collective-permute-start | bytes 1769480 | tf_op jit(solution)/shard_map/ppermute | solution.py:37
  778.5 29.7 %collective-permute-start.59 = (bf16[144,2048]{1,0:T(8,128)(2,1)S(1)}, bf16[144,2048]{1,0:T(8,128)(2,1)S(1)}, u32[]{:S(2)}, u32[]{:S(2)}) collective-permute-start(bf16[144,2048]{1,0:T(8,128)(2,1)S(1)} %get-tuple-element.142), channel_id=1, source_target_pairs={{0,4},{8,0},{16,8},{24,16},{28,24},{20,28},{12,20},{4,12},{1,5},{9... | collective-permute-start | bytes 1769480 | tf_op jit(solution)/shard_map/ppermute | solution.py:37
  847.0 68.8 %collective-permute-start.83 = (bf16[560,512]{1,0:T(8,128)(2,1)}, bf16[560,512]{1,0:T(8,128)(2,1)}, u32[]{:S(2)}, u32[]{:S(2)}) collective-permute-start(bf16[560,512]{1,0:T(8,128)(2,1)} %get-tuple-element.92), channel_id=1, source_target_pairs={{0,28},{4,0},{8,4},{12,8},{16,12},{20,16},{24,20},{28,24},{1,29},{... | collective-permute-start | bytes 1720328 | tf_op jit(solution)/shard_map/ppermute | solution.py:32
  853.8 90.2 %collective-permute-start.107 = (bf16[128,1024]{1,0:T(8,128)(2,1)}, bf16[128,1024]{1,0:T(8,128)(2,1)}, u32[]{:S(2)}, u32[]{:S(2)}) collective-permute-start(bf16[128,1024]{1,0:T(8,128)(2,1)} %fusion.170), channel_id=1, source_target_pairs={{0,2},{2,0},{1,3},{3,1},{4,6},{6,4},{5,7},{7,5},{8,10},{10,8},{9,1... | collective-permute-start | bytes 786440 | tf_op jit(solution)/shard_map/ppermute | solution.py:32
  855.5 62.5 %collective-permute-start.96 = (bf16[2,512,2048]{2,1,0:T(8,128)(2,1)}, bf16[2,512,2048]{2,1,0:T(8,128)(2,1)}, u32[]{:S(2)}, u32[]{:S(2)}) collective-permute-start(bf16[2,512,2048]{2,1,0:T(8,128)(2,1)} %bitcast.176), channel_id=1, source_target_pairs={{0,1},{1,0},{2,3},{3,2},{4,5},{5,4},{6,7},{7,6},{8,9},{9,8},{10,11... | collective-permute-start | bytes 12582920 | tf_op jit(solution)/shard_map/ppermute | solution.py:32
  902.9 103.4 %collective-permute-start.98 = (bf16[2,512,2048]{2,1,0:T(8,128)(2,1)}, bf16[2,512,2048]{2,1,0:T(8,128)(2,1)}, u32[]{:S(2)}, u32[]{:S(2)}) collective-permute-start(bf16[2,512,2048]{2,1,0:T(8,128)(2,1)} %bitcast.184), channel_id=1, source_target_pairs={{0,1},{1,0},{2,3},{3,2},{4,5},{5,4},{6,7},{7,6},{8,9},{9,8},{10,11... | collective-permute-start | bytes 12582920 | tf_op jit(solution)/shard_map/ppermute | solution.py:32
  915.8 100.6 %collective-permute-start.100 = (bf16[2,512,2048]{2,1,0:T(8,128)(2,1)}, bf16[2,512,2048]{2,1,0:T(8,128)(2,1)}, u32[]{:S(2)}, u32[]{:S(2)}) collective-permute-start(bf16[2,512,2048]{2,1,0:T(8,128)(2,1)} %bitcast.192), channel_id=1, source_target_pairs={{0,1},{1,0},{2,3},{3,2},{4,5},{5,4},{6,7},{7,6},{8,9},{9,8},{10,11... | collective-permute-start | bytes 12582920 | tf_op jit(solution)/shard_map/ppermute | solution.py:32
  929.5 63.6 %collective-permute-start.97 = (bf16[512,2048]{1,0:T(8,128)(2,1)}, bf16[512,2048]{1,0:T(8,128)(2,1)}, u32[]{:S(2)}, u32[]{:S(2)}) collective-permute-start(bf16[512,2048]{1,0:T(8,128)(2,1)} %fusion.72), channel_id=1, source_target_pairs={{0,2},{2,0},{1,3},{3,1},{4,6},{6,4},{5,7},{7,5},{8,10},{10,8},{9,1... | collective-permute-start | bytes 6291464 | tf_op jit(solution)/shard_map/ppermute | solution.py:32
  939.4 333.9 %reduce-scatter.3.cloned.1.call-start = ((), (), s32[]{:S(2)}) async-start(), calls=%async_computation.14 | async-start | bytes 4423680 | tf_op jit(solution)/shard_map/reduce_scatter | solution.py:409
  954.7 33.9 %collective-permute-start.24 = (bf16[144,2048]{1,0:T(8,128)(2,1)S(1)}, bf16[144,2048]{1,0:T(8,128)(2,1)}, u32[]{:S(2)}, u32[]{:S(2)}) collective-permute-start(bf16[144,2048]{1,0:T(8,128)(2,1)S(1)} %get-tuple-element.139), channel_id=1, source_target_pairs={{0,2},{2,0},{1,3},{3,1},{4,6},{6,4},{5,7},{7,5},{8,10},{10,8},{9,1... | collective-permute-start | bytes 1769480 | tf_op jit(solution)/shard_map/ppermute | solution.py:32
  991.2 165.1 %collective-permute-start.25 = (bf16[2,144,2048]{2,1,0:T(8,128)(2,1)}, bf16[2,144,2048]{2,1,0:T(8,128)(2,1)}, u32[]{:S(2)}, u32[]{:S(2)}) collective-permute-start(bf16[2,144,2048]{2,1,0:T(8,128)(2,1)} %maximum_select_fusion.4), channel_id=1, source_target_pairs={{0,1},{1,0},{2,3},{3,2},{4,5},{5,4},{6,7},{7,6},{8,9},{9,8},{10,11... | collective-permute-start | bytes 3538952 | tf_op jit(solution)/shard_map/ppermute | solution.py:32
  1002.0 68.5 %all-to-all-start.6 = ((bf16[8,512,256]{1,2,0:T(8,128)(2,1)}), bf16[8,512,256]{1,2,0:T(8,128)(2,1)}, u32[]{:S(2)}, u32[]{:S(2)}) async-start(bf16[8,512,256]{1,2,0:T(8,128)(2,1)} %bitcast.655), calls=%async_computation.8 | async-start | bytes 4194304 | tf_op jit(solution)/shard_map/all_to_all | solution.py:127
  1013.4 47.6 %collective-permute-start.99 = (bf16[512,2048]{1,0:T(8,128)(2,1)}, bf16[512,2048]{1,0:T(8,128)(2,1)}, u32[]{:S(2)}, u32[]{:S(2)}) collective-permute-start(bf16[512,2048]{1,0:T(8,128)(2,1)} %fusion.73), channel_id=1, source_target_pairs={{0,2},{2,0},{1,3},{3,1},{4,6},{6,4},{5,7},{7,5},{8,10},{10,8},{9,1... | collective-permute-start | bytes 6291464 | tf_op jit(solution)/shard_map/ppermute | solution.py:32
  1023.4 87.0 %collective-permute-start.101 = (bf16[512,2048]{1,0:T(8,128)(2,1)}, bf16[512,2048]{1,0:T(8,128)(2,1)}, u32[]{:S(2)}, u32[]{:S(2)}) collective-permute-start(bf16[512,2048]{1,0:T(8,128)(2,1)} %fusion.74), channel_id=1, source_target_pairs={{0,2},{2,0},{1,3},{3,1},{4,6},{6,4},{5,7},{7,5},{8,10},{10,8},{9,1... | collective-permute-start | bytes 6291464 | tf_op jit(solution)/shard_map/ppermute | solution.py:32
  1070.5 72.0 %all-to-all-start.7 = ((bf16[8,512,256]{1,2,0:T(8,128)(2,1)}), bf16[8,512,256]{1,2,0:T(8,128)(2,1)}, u32[]{:S(2)}, u32[]{:S(2)}) async-start(bf16[8,512,256]{1,2,0:T(8,128)(2,1)} %bitcast.654), calls=%async_computation.9 | async-start | bytes 4194304 | tf_op jit(solution)/shard_map/all_to_all | solution.py:127
  1074.9 199.9 %reduce-scatter.5.cloned.1.call-start = ((), (), s32[]{:S(2)}) async-start(), calls=%async_computation.15 | async-start | bytes 3538944 | tf_op jit(solution)/shard_map/reduce_scatter | solution.py:401
  1142.5 126.8 %all-to-all-start.8 = ((bf16[8,512,256]{2,1,0:T(8,128)(2,1)}), bf16[8,512,256]{2,1,0:T(8,128)(2,1)}, u32[]{:S(2)}, u32[]{:S(2)}) async-start(bf16[8,512,256]{2,1,0:T(8,128)(2,1)} %bitcast.653), calls=%async_computation.10 | async-start | bytes 4194304 | tf_op jit(solution)/shard_map/all_to_all | solution.py:127
  1173.1 71.2 %collective-permute-start.89 = (bf16[2,144,2048]{2,1,0:T(8,128)(2,1)}, bf16[2,144,2048]{2,1,0:T(8,128)(2,1)S(1)}, u32[]{:S(2)}, u32[]{:S(2)}) collective-permute-start(bf16[2,144,2048]{2,1,0:T(8,128)(2,1)} %maximum_select_fusion.7), channel_id=1, source_target_pairs={{0,1},{1,0},{2,3},{3,2},{4,5},{5,4},{6,7},{7,6},{8,9},{9,8},{10,11... | collective-permute-start | bytes 3538952 | tf_op jit(solution)/shard_map/ppermute | solution.py:32
  (226 other events, 2747.3 us)
Sparse Core Ops, SparseCore 0:
  19.1 100.5 all-gather.6
  139.6 107.8 all-gather.4
  944.1 123.4 reduce-scatter.2
  1085.0 125.8 reduce-scatter.4

commit v2 on v1

--- a/solution.py
+++ b/solution.py
@@ -4,6 +4,7 @@
 from jax.sharding import PartitionSpec as P
 
 IMG = 512
+LANES = 128
 EPS = 1e-06
 MASKED = -1e30
 BF = jnp.bfloat16
@@ -18,6 +19,18 @@
     )
 
 
+def fence(*values):
+    return lax.optimization_barrier(values)
+
+
+def fold(block, width):
+    return cat([block[:, k : k + width] for k in range(0, block.shape[1], width)])
+
+
+def unfold(block, rows):
+    return cat([block[..., k : k + rows, :] for k in range(0, block.shape[-2], rows)], -1)
+
+
 def cat(parts, axis=0):
     return parts[0] if len(parts) == 1 else jnp.concatenate(parts, axis=axis)
 
@@ -41,44 +54,57 @@
     return lax.axis_size("seq") == len(SNAKE)
 
 
+def ring_gather(block):
+    ahead, behind, order = [block], [block], [block]
+    for k in range(1, len(SNAKE)):
+        if k % 2:
+            ahead.append(ring_step(ahead[-1], -1))
+            order.append(ahead[-1])
+        else:
+            behind.append(ring_step(behind[-1], 1))
+            order.append(behind[-1])
+    return order
+
+
 def seq_gather(block):
+    if on_ring():
+        return ring_gather(block)
+    whole = lax.all_gather(block, "seq", axis=0, tiled=False)
+    return [whole[k] for k in range(whole.shape[0])]
+
+
+def seq_reduce(blocks):
     if not on_ring():
-        return [lax.all_gather(block, "seq", axis=0, tiled=True)]
-    count = len(SNAKE)
-    ahead, behind = [block], [block]
-    for _ in range(count // 2):
-        ahead.append(ring_step(ahead[-1], -1))
-    for _ in range((count - 1) // 2):
-        behind.append(ring_step(behind[-1], 1))
-    return [cat([behind[k], ahead[k + 1]]) for k in range(count // 2)]
-
-
-def seq_reduce(groups):
-    if not on_ring():
-        return lax.psum_scatter(
-            groups[0].astype(BF), "seq", scatter_dimension=0, tiled=True
-        ).astype(F32)
-    half = groups[0].shape[0] // 2
-    top = len(groups)
-    going = groups[top - 1][half:].astype(BF)
-    back = groups[top - 1][:half].astype(BF)
-    for k in range(top - 2, -1, -1):
-        going = ring_step(going, 1).astype(F32) + groups[k][half:].astype(F32)
-        going = going.astype(BF)
-        back = ring_step(back, -1).astype(F32) + groups[k][:half].astype(F32)
-        if k:
+        return lax.psum_scatter(jnp.stack(blocks), "seq", scatter_dimension=0).astype(F32)
+    going, back = blocks[-1], blocks[-2]
+    for k in range(len(blocks) - 3, 0, -2):
+        going = (ring_step(going, 1).astype(F32) + blocks[k].astype(F32)).astype(BF)
+        back = ring_step(back, -1).astype(F32) + blocks[k - 1].astype(F32)
+        if k > 1:
             back = back.astype(BF)
     return back + ring_step(going, 1).astype(F32)
 
 
+def seq_halve(rows):
+    count, index = rows.shape[0], lax.axis_index("seq")
+    while count > 1:
+        count //= 2
+        bit = (index // count) % 2
+        halves = rows.reshape(2, count, -1)
+        keep = lax.dynamic_index_in_dim(halves, bit, 0, keepdims=False)
+        give = lax.dynamic_index_in_dim(halves, 1 - bit, 0, keepdims=False)
+        pairs = [(i, i ^ count) for i in range(lax.axis_size("seq"))]
+        rows = keep + lax.ppermute(give, "seq", pairs)
+    rows = rows + shift(rows, "expert", 1)
+    return (rows + shift(rows, "mp", 1)).reshape(-1)
+
+
 def swap(block, axis):
     return shift(block, axis, 1)
 
 
-def quad_gather_rel(block):
-    across = swap(block, "mp")
-    other = swap(jnp.stack([block, across]), "expert")
-    return [block, across, other[0], other[1]]
+def quad_join(block, across, axis):
+    return cat([block, across, swap(block, "expert"), swap(across, "expert")], axis)
 
 
 def quad_gather(block):
@@ -101,41 +127,48 @@
     return keep + swap(give, "mp").astype(F32)
 
 
-def quad_reduce_rel(whole):
-    parts = whole.reshape((2, 2) + (whole.shape[0] // 4,) + whole.shape[1:])
-    pair = parts[0].astype(F32) + swap(parts[1].astype(BF), "expert").astype(F32)
-    return (pair[0] + swap(pair[1].astype(BF), "mp").astype(F32)).astype(BF)
-
-
-def hidden_first(weight, from_rows):
+def quad_reduce_rel(parts):
+    give = parts[1].astype(F32) + swap(parts[3].astype(BF), "expert").astype(F32)
+    keep = parts[0].astype(F32) + swap(parts[2].astype(BF), "expert").astype(F32)
+    return (keep + swap(give.astype(BF), "mp").astype(F32)).astype(BF)
+
+
+def pack(prefix, action):
+    fold = prefix.shape[-1] // action.shape[-1]
+    rows = action.shape[-2] // fold
+    parts = [action[..., k * rows : (k + 1) * rows, :] for k in range(fold)]
+    return jnp.concatenate([prefix, jnp.concatenate(parts, axis=-1)], axis=-2)
+
+
+def action_of(block, part_p, width):
+    folded = block[..., part_p:, :]
+    fold = folded.shape[-1] // width
+    parts = [folded[..., k * width : (k + 1) * width] for k in range(fold)]
+    return jnp.concatenate(parts, axis=-2)
+
+
+def a2a(parts):
+    return lax.all_to_all(parts, "seq", 0, 0, tiled=True)
+
+
+def split_columns(weight):
+    depth, width = weight.shape
     count = lax.axis_size("seq")
-    if from_rows:
-        depth, width = weight.shape
-        parts = weight.reshape(depth, count, width // count).transpose(1, 2, 0)
-    else:
-        width, depth = weight.shape
-        parts = weight.reshape(count, width // count, depth)
-    parts = lax.all_to_all(parts, "seq", 0, 0, tiled=True)
-    return parts.transpose(1, 0, 2).reshape(width // count, count * depth)
-
-
-def hidden_back(grad, to_rows):
+    return weight.reshape(depth, count, width // count).transpose(1, 0, 2)
+
+
+def split_rows(weight):
+    width, depth = weight.shape
     count = lax.axis_size("seq")
-    width, full = grad.shape
-    depth = full // count
-    parts = grad.reshape(width, count, depth).transpose(1, 0, 2)
-    parts = lax.all_to_all(parts, "seq", 0, 0, tiled=True)
-    if to_rows:
-        return parts.transpose(2, 0, 1).reshape(depth, count * width).astype(F32)
-    return parts.reshape(count * width, depth).astype(F32)
-
-
-def spread(weight, from_rows):
-    return cat(quad_gather_rel(hidden_first(weight, from_rows)))
-
-
-def collect(grad, to_rows):
-    return hidden_back(quad_reduce_rel(grad), to_rows)
+    return weight.reshape(count, width // count, depth)
+
+
+def join_rows(parts):
+    return parts.reshape(-1, parts.shape[-1])
+
+
+def join_columns(parts):
+    return parts.transpose(1, 0, 2).reshape(parts.shape[1], -1)
 
 
 def rms_norm(values, gain_vec):
@@ -187,24 +220,27 @@
 
 
 def feed_forward(normed_groups, cot_groups, w_gate, w_up, w_down):
-    y_groups, gn_groups, mids, d_gates, d_ups = [], [], [], [], []
+    gn_groups, mids, d_gates, d_ups = [], [], [], []
     for normed, cot in zip(normed_groups, cot_groups):
-        gate_pre = dot(normed, w_gate, 1, 1)
-        up_pre = dot(normed, w_up, 1, 1)
+        gate_pre = dot(normed, w_gate, 1, 0)
+        up_pre = dot(normed, w_up, 1, 0)
         grad_hidden = dot(cot, w_down, 1, 1)
         mid, pullback = jax.vjp(geglu_act, gate_pre, up_pre)
         d_gate, d_up = pullback(grad_hidden)
-        mid, d_gate, d_up = mid.astype(BF), d_gate.astype(BF), d_up.astype(BF)
-        gn_groups.append((dot(d_gate, w_gate, 1, 0) + dot(d_up, w_up, 1, 0)).astype(BF))
-        y_groups.append(dot(mid, w_down, 1, 0).astype(BF))
-        mids.append(mid)
+        d_gate, d_up = d_gate.astype(BF), d_up.astype(BF)
+        gn_groups.append((dot(d_gate, w_gate, 1, 1) + dot(d_up, w_up, 1, 1)).astype(BF))
+        mids.append(mid.astype(BF))
         d_gates.append(d_gate)
         d_ups.append(d_up)
-    return y_groups, gn_groups, cat(mids), cat(d_gates), cat(d_ups)
+    return gn_groups, mids, d_gates, d_ups
 
 
 def weight_grad(left, right):
     return dot(left, right, 0, 0).astype(BF)
+
+
+def quarters(array, axis):
+    return jnp.split(array, 4, axis=axis)
 
 
 def body(
@@ -246,41 +282,6 @@
     part_a = -(-action_rows_all // (16 * quad)) * 16
     kv_cols = 2 * head_size // quad
 
-    def quarter_kv(w_key, w_value):
-        return lax.dynamic_slice_in_dim(
-            jnp.concatenate([w_key, w_value], axis=1), mine * kv_cols, kv_cols, axis=1
-        )
-
-    early_cols = head_cols + kv_cols
-    depth_p, depth_a = query_prefix.shape[0], query_action.shape[0]
-    gains = jnp.concatenate([norm1_prefix, norm2_prefix, norm1_action, norm2_action])
-    gain_rows = -(-gains.shape[0] // (16 * early_cols)) * 16
-    gain_block = jnp.pad(gains, (0, gain_rows * early_cols - gains.shape[0]))
-    early = jnp.concatenate(
-        [
-            jnp.concatenate([query_prefix, quarter_kv(key_prefix, value_prefix)], axis=1),
-            jnp.concatenate([query_action, quarter_kv(key_action, value_action)], axis=1),
-            gain_block.reshape(gain_rows, early_cols),
-        ],
-        axis=0,
-    )
-    early = lax.all_gather(early, "seq", axis=0, tiled=False)
-    w_in_p = early[:, :depth_p].reshape(-1, early_cols)
-    w_in_a = early[:, depth_p : depth_p + depth_a].reshape(-1, early_cols)
-    gains = early[:, depth_p + depth_a :].reshape(episodes, -1)
-    gain1_p = gains[:, :depth_p].reshape(-1).astype(F32)
-    gain2_p = gains[:, depth_p : 2 * depth_p].reshape(-1).astype(F32)
-    gain1_a = gains[:, 2 * depth_p : 2 * depth_p + depth_a].reshape(-1).astype(F32)
-    gain2_a = gains[:, 2 * depth_p + depth_a : 2 * (depth_p + depth_a)].reshape(-1).astype(F32)
-
-    w_gate_p, w_up_p = spread(gate_prefix, True), spread(up_prefix, True)
-    w_gate_a, w_up_a = spread(gate_action, True), spread(up_action, True)
-    late = jnp.concatenate([out_prefix, out_action], axis=1)
-    late = lax.all_gather(late, "seq", axis=0, tiled=False)
-    w_out_p = late[:, :, :depth_p].transpose(1, 0, 2).reshape(head_cols, -1)
-    w_out_a = late[:, :, depth_p:].transpose(1, 0, 2).reshape(head_cols, -1)
-    w_down_p, w_down_a = spread(down_prefix, False), spread(down_action, False)
-
     positions = jnp.arange(prefix_rows, dtype=jnp.int32)
     keep_prefix = positions < IMG + instr_len[seq_index]
     live_slot = slot_source >= 0
@@ -301,8 +302,62 @@
     x_p, x_a = x_p.astype(F32), x_a.astype(F32)
     live_a = own_part(live_rows, part_a)
     cot_p, cot_a = own_part(cot_prefix, part_p), own_part(cot_action, part_a)
-    cot_full_p = seq_gather(cot_p)
-    cot_full_a = seq_gather((cot_a.astype(F32) * live_a).astype(BF))
+    cot_live_a = (cot_a.astype(F32) * live_a).astype(BF)
+
+    def quarter_kv(w_key, w_value):
+        return lax.dynamic_slice_in_dim(
+            jnp.concatenate([w_key, w_value], axis=1), mine * kv_cols, kv_cols, axis=1
+        )
+
+    early_cols = head_cols + kv_cols
+    depth_p, depth_a = query_prefix.shape[0], query_action.shape[0]
+    gains = jnp.concatenate([norm1_prefix, norm2_prefix, norm1_action, norm2_action])
+    gain_rows = -(-gains.shape[0] // (16 * LANES)) * 16
+    gain_block = jnp.pad(gains, (0, gain_rows * LANES - gains.shape[0]))
+    out_both = jnp.concatenate([out_prefix, out_action], axis=1)
+    out_both = jnp.pad(out_both, ((0, 0), (0, -out_both.shape[1] % LANES)))
+    pieces = [
+        fold(query_prefix, LANES),
+        fold(quarter_kv(key_prefix, value_prefix), LANES),
+        fold(query_action, LANES),
+        fold(quarter_kv(key_action, value_action), LANES),
+        fold(out_both, LANES),
+        gain_block.reshape(gain_rows, LANES),
+    ]
+    early = lax.all_gather(jnp.concatenate(pieces, axis=0), "seq", axis=0, tiled=False)
+
+    gate_p = a2a(split_columns(gate_prefix))
+    gate_p, up_send = fence(gate_p, split_columns(up_prefix))
+    up_p = a2a(up_send)
+    gate_p = join_rows(gate_p)
+    gate_far_p = swap(gate_p, "mp")
+
+    cot_chunks = pack(cot_p, cot_live_a)
+    in_action = [split_columns(gate_action), split_columns(up_action), split_rows(down_action)]
+    in_action = jnp.concatenate(in_action, axis=1)
+    early, up_p, gate_far_p, down_send, in_action, cot_chunks = fence(
+        early, up_p, gate_far_p, split_rows(down_prefix), in_action, cot_chunks
+    )
+    down_p, in_action = a2a(down_send), a2a(in_action)
+    up_p = join_rows(up_p)
+    up_far_p = swap(up_p, "mp")
+    cot_chunks = seq_gather(cot_chunks)
+
+    starts, w_in = [0], []
+    for piece in pieces:
+        starts.append(starts[-1] + piece.shape[0])
+    parts = [early[:, a:b] for a, b in zip(starts[:-1], starts[1:])]
+    for rows, (query, kv) in ((depth_p, parts[:2]), (depth_a, parts[2:4])):
+        w_in.append(join_rows(unfold(jnp.concatenate([query, kv], axis=1), rows)))
+    w_in_p, w_in_a = w_in
+    w_out = unfold(parts[4], head_cols)
+    w_out_p = join_columns(w_out[:, :, :depth_p])
+    w_out_a = join_columns(w_out[:, :, depth_p : depth_p + depth_a])
+    gains = parts[5].reshape(episodes, -1)
+    gain1_p = gains[:, :depth_p].reshape(-1).astype(F32)
+    gain2_p = gains[:, depth_p : 2 * depth_p].reshape(-1).astype(F32)
+    gain1_a = gains[:, 2 * depth_p : 2 * depth_p + depth_a].reshape(-1).astype(F32)
+    gain2_a = gains[:, 2 * depth_p + depth_a : 2 * (depth_p + depth_a)].reshape(-1).astype(F32)
 
     normed1_p = rms_norm(hidden_prefix.astype(F32), gain1_p).astype(BF)
     normed1_a = rms_norm(hidden_action.astype(F32), gain1_a).astype(BF)
@@ -322,32 +377,77 @@
         query_slots, keys_slots, values_slots, keep_all
     )
     mixed_a = mixed_slots.reshape(action_rows_all, -1)
-    attn_p = dot(pad_rows(mixed_p, quad * part_p), w_out_p, 1, 0)
-    attn_a = dot(pad_rows(mixed_a, quad * part_a), w_out_a, 1, 0)
-    middle_p = x_p + quad_reduce(attn_p.reshape(quad, part_p, -1))
-    middle_a = x_a + live_a * quad_reduce(attn_a.reshape(quad, part_a, -1))
-
-    normed2_p = seq_gather(rms_norm(middle_p, gain2_p).astype(BF))
-    normed2_a = seq_gather(rms_norm(middle_a, gain2_a).astype(BF))
-    y_p, gn2_p, mid_p, d_gate_p, d_up_p = feed_forward(
+    attn_p = dot(pad_rows(mixed_p, quad * part_p), w_out_p, 1, 0).reshape(quad, part_p, -1)
+    attn_a = dot(pad_rows(mixed_a, quad * part_a), w_out_a, 1, 0).reshape(quad, part_a, -1)
+    attn = quad_reduce(pack(attn_p, attn_a))
+    middle_p = x_p + attn[:part_p]
+    middle_a = x_a + live_a * action_of(attn, part_p, x_a.shape[1])
+    normed2 = pack(
+        rms_norm(middle_p, gain2_p).astype(BF), rms_norm(middle_a, gain2_a).astype(BF)
+    )
+
+    normed2, down_p, in_action, up_far_p = fence(normed2, down_p, in_action, up_far_p)
+    down_p = join_columns(down_p)
+    down_far_p, far_action = swap(down_p, "mp"), swap(in_action, "mp")
+    w_gate_p, w_up_p = quad_join(gate_p, gate_far_p, 1), quad_join(up_p, up_far_p, 1)
+    w_down_p = quad_join(down_p, down_far_p, 0)
+    in_action = [in_action, far_action, swap(in_action, "expert"), swap(far_action, "expert")]
+    w_gate_a = cat([join_rows(part[:, :depth_a]) for part in in_action], 1)
+    w_up_a = cat([join_rows(part[:, depth_a : 2 * depth_a]) for part in in_action], 1)
+    w_down_a = cat([join_columns(part[:, 2 * depth_a :]) for part in in_action], 0)
+
+    normed2_chunks = seq_gather(normed2)
+    pair = 4 if on_ring() else episodes
+
+    def prefix_groups(chunks):
+        rows = [chunk[:part_p] for chunk in chunks]
+        return [cat(rows[k : k + pair]) for k in range(0, episodes, pair)]
+
+    def action_group(chunks):
+        return cat([action_of(chunk, part_p, x_a.shape[1]) for chunk in chunks])
+
+    normed2_p, normed2_a = prefix_groups(normed2_chunks), action_group(normed2_chunks)
+    cot_full_p, cot_full_a = prefix_groups(cot_chunks), action_group(cot_chunks)
+    gn2_p, mid_p, d_gate_p, d_up_p = feed_forward(
         normed2_p, cot_full_p, w_gate_p, w_up_p, w_down_p
     )
-    y_a, gn2_a, mid_a, d_gate_a, d_up_a = feed_forward(
-        normed2_a, cot_full_a, w_gate_a, w_up_a, w_down_a
-    )
-    gn2_p, gn2_a = seq_reduce(gn2_p), seq_reduce(gn2_a)
-    normed2_p, normed2_a = cat(normed2_p), cat(normed2_a)
-    cot_full_p, cot_full_a = cat(cot_full_p), cat(cot_full_a)
-    y_p = (middle_p + seq_reduce(y_p)).astype(BF)
-    y_a = (middle_a + live_a * seq_reduce(y_a)).astype(BF)
-
-    dmid_norm_p, dgain2_p = norm_backward(middle_p, gain2_p, gn2_p)
-    dmid_norm_a, dgain2_a = norm_backward(middle_a, gain2_a, gn2_a)
+    gn2_a, mid_a, d_gate_a, d_up_a = feed_forward(
+        [normed2_a], [cot_full_a], w_gate_a, w_up_a, w_down_a
+    )
+    gn2_a, mid_a, d_gate_a, d_up_a = gn2_a[0], mid_a[0], d_gate_a[0], d_up_a[0]
+
+    def chunks_of(groups, action):
+        groups = [group.reshape(pair, part_p, -1) for group in groups]
+        action = action.reshape(episodes, part_a, -1)
+        return [pack(groups[k // pair][k % pair], action[k]) for k in range(episodes)]
+
+    gn2, mid_p, d_gate_p, d_up_p = fence(chunks_of(gn2_p, gn2_a), mid_p, d_gate_p, d_up_p)
+    gn2 = seq_reduce(gn2)
+    normed2_p, cot_full_p = cat(normed2_p), cat(cot_full_p)
+    dwd_p = quad_reduce_rel(quarters(weight_grad(cat(mid_p), cot_full_p), 0))
+    y_p = [dot(mid, w_down_p, 1, 0).astype(BF) for mid in mid_p]
+    y_a = dot(mid_a, w_down_a, 1, 0).astype(BF)
+    y_chunks = chunks_of(y_p, y_a)
+    d_gate_p, d_up_p = cat(d_gate_p), cat(d_up_p)
+    dwg_p = quad_reduce_rel([weight_grad(normed2_p, g) for g in quarters(d_gate_p, 1)])
+    dwu_p = quad_reduce_rel([weight_grad(normed2_p, g) for g in quarters(d_up_p, 1)])
+    gn2, dwd_p, y_chunks = fence(gn2, dwd_p, y_chunks)
+    dwd_p = a2a(split_columns(dwd_p))
+    y_sum = seq_reduce(y_chunks)
+    dmid_norm_p, dgain2_p = norm_backward(middle_p, gain2_p, gn2[:part_p])
+    dmid_norm_a, dgain2_a = norm_backward(
+        middle_a, gain2_a, action_of(gn2, part_p, x_a.shape[1])
+    )
     dmid_p = cot_p.astype(F32) + dmid_norm_p
     dmid_a = cot_a.astype(F32) + dmid_norm_a
-    dao_p = quad_gather(dmid_p.astype(BF)).reshape(quad * part_p, -1)[:prefix_rows]
-    dao_a = quad_gather((dmid_a * live_a).astype(BF)).reshape(quad * part_a, -1)
-    dao_a = dao_a[:action_rows_all]
+    dao = quad_gather(pack(dmid_p.astype(BF), (dmid_a * live_a).astype(BF)))
+
+    def whole_rows(block):
+        prefix = block[:, :part_p].reshape(quad * part_p, -1)[:prefix_rows]
+        action = action_of(block, part_p, x_a.shape[1]).reshape(quad * part_a, -1)
+        return prefix, action[:action_rows_all]
+
+    dao_p, dao_a = whole_rows(dao)
 
     dmix_p, dmix_a = dot(dao_p, w_out_p, 1, 1).astype(BF), dot(dao_a, w_out_a, 1, 1).astype(BF)
     dq_slots, dkv_slots = jax.vmap(attend_backward)(
@@ -367,29 +467,44 @@
     dq_a = dq_slots.reshape(action_rows_all, -1)
 
     dkv_both = jnp.concatenate([dkv_p, dkv_a], axis=0)
+    dkv_both, dwd_p, dwg_p, y_sum = fence(dkv_both, dwd_p, dwg_p, y_sum)
+    dwg_p = a2a(split_rows(dwg_p))
     dkv_both = dkv_both.reshape(-1, quad, kv_cols).transpose(1, 0, 2)
     dkv_both = quad_reduce(dkv_both).astype(BF)
     din_p = jnp.concatenate([dq_p, dkv_both[:prefix_rows]], axis=1)
     din_a = jnp.concatenate([dq_a, dkv_both[prefix_rows:]], axis=1)
-    gn1_p = dot(pad_rows(din_p, quad * part_p), w_in_p, 1, 1)
-    gn1_a = dot(pad_rows(din_a, quad * part_a), w_in_a, 1, 1)
-    gn1_p = quad_reduce(gn1_p.reshape(quad, part_p, -1))
-    gn1_a = quad_reduce(gn1_a.reshape(quad, part_a, -1))
-    dx_norm_p, dgain1_p = norm_backward(x_p, gain1_p, gn1_p)
-    dx_norm_a, dgain1_a = norm_backward(x_a, gain1_a, gn1_a)
-    dx_p = quad_gather((dmid_p + dx_norm_p).astype(BF)).reshape(quad * part_p, -1)
-    dx_a = quad_gather((dmid_a + dx_norm_a).astype(BF)).reshape(quad * part_a, -1)
-    dx_p = dx_p[:prefix_rows].astype(F32)
-    dx_a = dx_a[:action_rows_all].astype(F32)
-    y_p = quad_gather(y_p).reshape(quad * part_p, -1)[:prefix_rows]
-    y_a = quad_gather(y_a).reshape(quad * part_a, -1)[:action_rows_all]
-
-    dwd_p = collect(weight_grad(mid_p, cot_full_p), False)
-    dwd_a = collect(weight_grad(mid_a, cot_full_a), False)
-    dwg_p = collect(weight_grad(d_gate_p, normed2_p), True)
-    dwg_a = collect(weight_grad(d_gate_a, normed2_a), True)
-    dwu_p = collect(weight_grad(d_up_p, normed2_p), True)
-    dwu_a = collect(weight_grad(d_up_a, normed2_a), True)
+    gn1_p = dot(pad_rows(din_p, quad * part_p), w_in_p, 1, 1).reshape(quad, part_p, -1)
+    gn1_a = dot(pad_rows(din_a, quad * part_a), w_in_a, 1, 1).reshape(quad, part_a, -1)
+    gn1 = quad_reduce(pack(gn1_p, gn1_a))
+    gn1, dwg_p, dwu_p = fence(gn1, dwg_p, dwu_p)
+    dx_norm_p, dgain1_p = norm_backward(x_p, gain1_p, gn1[:part_p])
+    dx_norm_a, dgain1_a = norm_backward(x_a, gain1_a, action_of(gn1, part_p, x_a.shape[1]))
+    dx = quad_gather(pack((dmid_p + dx_norm_p).astype(BF), (dmid_a + dx_norm_a).astype(BF)))
+    dx_p, dx_a = whole_rows(dx)
+    dx_p, dx_a = dx_p.astype(F32), dx_a.astype(F32)
+    y_p = middle_p + y_sum[:part_p]
+    y_a = middle_a + live_a * action_of(y_sum, part_p, x_a.shape[1])
+    y_out = quad_gather(pack(y_p.astype(BF), y_a.astype(BF)))
+    y_p, y_a = whole_rows(y_out)
+
+    dwd_p = join_rows(dwd_p).astype(F32)
+    dwg_p = join_columns(dwg_p).astype(F32)
+    dwu_p = join_columns(a2a(split_rows(dwu_p))).astype(F32)
+    d_action = zip(
+        quarters(weight_grad(normed2_a, d_gate_a), 1),
+        quarters(weight_grad(normed2_a, d_up_a), 1),
+        quarters(weight_grad(mid_a, cot_full_a), 0),
+    )
+    d_action = quad_reduce_rel(
+        [
+            jnp.concatenate([split_rows(g), split_rows(u), split_columns(d)], axis=1)
+            for g, u, d in d_action
+        ]
+    )
+    d_action = a2a(d_action).astype(F32)
+    dwg_a = join_columns(d_action[:, :depth_a])
+    dwu_a = join_columns(d_action[:, depth_a : 2 * depth_a])
+    dwd_a = join_rows(d_action[:, 2 * depth_a :])
 
     dwo = jnp.concatenate(
         [
@@ -414,8 +529,7 @@
     dgains = jnp.concatenate(
         [g.reshape(episodes, -1) for g in (dgain1_p, dgain2_p, dgain1_a, dgain2_a)], axis=1
     )
-    dgains = lax.psum_scatter(dgains, "seq", scatter_dimension=0, tiled=False)
-    dgains = lax.psum(dgains, ("mp", "expert"))
+    dgains = seq_halve(dgains)
     return (
         y_p,
         y_a,

time: 1300 us -> 1190 us (0.915)
  starting transfers between devices: 272 us -> 163 us
  blocking collectives: 80.5 us -> 0 us
  waiting for transfers between devices: 400 us -> 436 us
  local copies, waits for them, and re-layouts: 187 us -> 213 us
    unnamed x1 -> x0, blocking collectives: 55 us -> none
    ppermute x56 -> x28, waiting for transfers between devices: 132 us -> 77.7 us  [ring_step(): return lax.ppermute(block, 'seq', pairs)]
    all_to_all x11 -> x8, waiting for transfers between devices: 99.6 us -> 152 us  [a2a(): return lax.all_to_all(parts, 'seq', 0, 0, tiled=True)]
    ppermute x56 -> x28, starting transfers between devices: 103 us -> 52.8 us  [ring_step(): return lax.ppermute(block, 'seq', pairs)]
    ppermute x52 -> x44, starting transfers between devices: 110 us -> 61.7 us  [shift(): lax.ppermute(block, axis, [(i, (i + distance) % count) for i in range(cou...]
    unnamed x352 -> x466, local copies, waits for them, and re-layouts: 77.5 us -> 109 us
    optimization_barrier x0 -> x3, local copies, waits for them, and re-layouts: none -> 23.4 us  [fence(): return lax.optimization_barrier(values)]
    reduce_scatter x1, waiting for transfers between devices: 0.01 us -> 22 us  [body(): dw_in = lax.psum_scatter(dw_in, 'seq', scatter_dimension=0, tiled=False)]
  transfers between devices with their start and end apart: 123 -> 86, of which waited for: 50 -> 32; matrix products, arithmetic and copies ran while one was open for 39% -> 44% of each run, Pallas kernels for 0% -> 0%
where the time goes in v2:
time: 1190 us; the launch traced here: 1170 us
  waiting for transfers between devices  436 us (37%)
  local copies, waits for them, and re-layouts  213 us (18%)
  matrix products  207 us (17%)
  starting transfers between devices  163 us (14%)
  other arithmetic  135 us (11%)
  between operations  18 us (2%)
    dot_general x42, matrix products, dot(): lax.dot_general(left, right, (((left_dim,), (right_dim,)), ((), ())), pre...  194 us
    ppermute x44, waiting for transfers between devices, shift(): lax.ppermute(block, axis, [(i, (i + distance) % count) for i in range(cou...  181 us
    all_to_all x8, waiting for transfers between devices, a2a(): return lax.all_to_all(parts, 'seq', 0, 0, tiled=True)  152 us
    unnamed x466, local copies, waits for them, and re-layouts  109 us
    ppermute x28, waiting for transfers between devices, ring_step(): return lax.ppermute(block, 'seq', pairs)  77.7 us
    ppermute x44, starting transfers between devices, shift(): lax.ppermute(block, axis, [(i, (i + distance) % count) for i in range(cou...  61.7 us
    ppermute x28, starting transfers between devices, ring_step(): return lax.ppermute(block, 'seq', pairs)  52.8 us
    all_to_all x8, starting transfers between devices, a2a(): return lax.all_to_all(parts, 'seq', 0, 0, tiled=True)  42 us
  transfers between devices with their start and end apart: 86, of which 32 were waited for; matrix products, arithmetic and copies ran while one was open for 44% of the time, Pallas kernels for 0%

profile of v2, /device:TPU:1, one launch (start us, length us, event | category | flops | bytes accessed | tf_op | source)
XLA Modules:
  0.0 1172.7 jit_solution(13416793224746015102)
XLA Ops:
  22.5 6.4 all-to-all-start
  33.0 71.7 %all-to-all-done = bf16[8,256,512]{1,2,0:T(8,128)(2,1)S(1)} async-done(((bf16[8,256,512]{1,2,0:T(8,128)(2,1)}), bf16[8,256,512]{1,2,0:T(8,128)(2,1)S(1)}, u32[]{:S(2)}, u32[]{:S(2)}) %all-to-all-start) | async-done | bytes 2097184 | tf_op jit(solution)/shard_map/all_to_all | solution.py:151
  106.1 4.8 all-to-all-start.1
  125.5 39.1 %collective-permute-done = bf16[2048,512]{1,0:T(8,128)(2,1)} collective-permute-done((bf16[2048,512]{1,0:T(8,128)(2,1)}, bf16[2048,512]{1,0:T(8,128)(2,1)}, u32[]{:S(2)}, u32[]{:S(2)}) %collective-permute-start) | collective-permute-done | bytes 2097184 | tf_op jit(solution)/shard_map/ppermute | solution.py:45
  164.5 40.9 %all-to-all-done.1 = bf16[8,256,512]{1,2,0:T(8,128)(2,1)} async-done(((bf16[8,256,512]{1,2,0:T(8,128)(2,1)}), bf16[8,256,512]{1,2,0:T(8,128)(2,1)}, u32[]{:S(2)}, u32[]{:S(2)}) %all-to-all-start.1) | async-done | bytes 2097184 | tf_op jit(solution)/shard_map/all_to_all | solution.py:151
  223.6 15.4 %copy.243 = bf16[8,3472,128]{2,0,1:T(8,128)(2,1)S(1)} copy(bf16[8,3472,128]{2,1,0:T(8,128)(2,1)S(1)} %bitcast.464) | data formatting | bytes 14221312 | tf_op jit(solution)/shard_map/optimization_barrier | solution.py:23
  261.8 4.5 all-to-all-start.3
  283.0 5.2 fusion.257
  301.1 4.4 collective-permute-done.3
  349.9 8.5 all-to-all-start.2
  364.4 39.8 %all-to-all-done.2 = bf16[8,512,256]{2,1,0:T(8,128)(2,1)} async-done(((bf16[8,512,256]{2,1,0:T(8,128)(2,1)}), bf16[8,512,256]{2,1,0:T(8,128)(2,1)}, u32[]{:S(2)}, u32[]{:S(2)}) %all-to-all-start.2) | async-done | bytes 2097184 | tf_op jit(solution)/shard_map/all_to_all | solution.py:151
  417.1 5.7 collective-permute-done.13
  448.0 10.7 fusion.121
  472.2 5.7 collective-permute-done.28
  482.2 9.4 collective-permute-start.30
  500.0 9.6 fusion.122
  518.4 9.5 fusion.119
  527.9 9.5 fusion.120
  543.1 15.5 %multiply_convert_fusion = (bf16[576,2048]{1,0:T(8,128)(2,1)}, bf16[576,2048]{1,0:T(8,128)(2,1)}, bf16[576,2048]{1,0:T(8,128)(2,1)S(1)}) fusion(f32[576,2048]{1,0:T(8,128)} %fusion.120, f32[576,2048]{1,0:T(8,128)} %fusion.119, bf16[512,2048]{0,1:T(8,128)(2,1)} %collective-permute-done.12, bf16[512,2048]{0,1:T(8,128)(2,1)} %collective-permute-done.11, ...), kind=kOutput, calls=%fused_computation.32 | convolution fusion | flops 4905500672 | bytes 27262976 | tf_op jit(solution)/shard_map/dot_general | solution.py:17
  558.6 8.4 fusion.218
  567.0 7.5 add_convert_fusion
  575.8 16.0 %multiply_convert_fusion.1 = (bf16[576,2048]{1,0:T(8,128)(2,1)}, bf16[576,2048]{1,0:T(8,128)(2,1)}, bf16[576,2048]{1,0:T(8,128)(2,1)}) fusion(f32[576,2048]{1,0:T(8,128)} %fusion.122, f32[576,2048]{1,0:T(8,128)} %fusion.121, bf16[512,2048]{0,1:T(8,128)(2,1)} %collective-permute-done.12, bf16[512,2048]{0,1:T(8,128)(2,1)} %collective-permute-done.11, ...), kind=kOutput, calls=%fused_computation.33 | convolution fusion | flops 4905500672 | bytes 27262976 | tf_op jit(solution)/shard_map/dot_general | solution.py:17
  591.8 8.4 fusion.219
  600.2 7.5 add_convert_fusion.1
  614.9 6.7 convolution_convert_fusion.11
  621.6 4.5 convolution_convert_fusion.10
  653.8 7.4 convolution_convert_fusion.2
  662.9 7.2 convolution_convert_fusion.3
  671.9 13.3 %convolution_convert_fusion = bf16[2048,2048]{1,0:T(8,128)(2,1)S(1)} fusion(bf16[1152,2048]{1,0:T(8,128)(2,1)} %get-tuple-element.295, bf16[576,2048]{1,0:T(8,128)(2,1)S(1)} %copy-done.185, bf16[576,2048]{1,0:T(8,128)(2,1)S(1)} %copy-done.186), kind=kOutput, calls=%fused_computation.6 | convolution fusion | flops 9677307904 | bytes 17825792 | tf_op jit(solution)/shard_map/dot_general | solution.py:17
  716.3 18.0 %collective-permute-done.32 = bf16[160,2048]{1,0:T(8,128)(2,1)S(1)} collective-permute-done((bf16[160,2048]{1,0:T(8,128)(2,1)S(1)}, bf16[160,2048]{1,0:T(8,128)(2,1)S(1)}, u32[]{:S(2)}, u32[]{:S(2)}) %collective-permute-start.32) | collective-permute-done | bytes 655392 | tf_op jit(solution)/shard_map/ppermute | solution.py:50
  739.5 5.6 collective-permute-start.36
  748.7 9.2 collective-permute-done.36
  769.6 5.4 collective-permute-done.37
  778.6 15.0 %collective-permute-done.40 = bf16[512,2048]{1,0:T(8,128)(2,1)S(1)} collective-permute-done((bf16[512,2048]{1,0:T(8,128)(2,1)S(1)}, bf16[512,2048]{1,0:T(8,128)(2,1)S(1)}, u32[]{:S(2)}, u32[]{:S(2)}) %collective-permute-start.40) | collective-permute-done | bytes 2097184 | tf_op jit(solution)/shard_map/ppermute | solution.py:45
  808.4 30.2 %collective-permute-done.46 = bf16[2048,512]{1,0:T(8,128)(2,1)} collective-permute-done((bf16[2048,512]{1,0:T(8,128)(2,1)}, bf16[2048,512]{1,0:T(8,128)(2,1)}, u32[]{:S(2)}, u32[]{:S(2)}) %collective-permute-start.46) | collective-permute-done | bytes 2097184 | tf_op jit(solution)/shard_map/ppermute | solution.py:45
  840.8 5.0 add_convert_fusion.4
  845.9 6.8 collective-permute-done.41
  857.6 9.3 collective-permute-start.51
  868.5 8.1 collective-permute-done.48
  877.6 5.5 collective-permute-start.49
  905.1 5.4 collective-permute-start.43
  920.3 32.4 %collective-permute-done.43 = bf16[560,512]{1,0:T(8,128)(2,1)} collective-permute-done((bf16[560,512]{1,0:T(8,128)(2,1)}, bf16[560,512]{1,0:T(8,128)(2,1)}, u32[]{:S(2)}, u32[]{:S(2)}) %collective-permute-start.43) | collective-permute-done | bytes 573472 | tf_op jit(solution)/shard_map/ppermute | solution.py:45
  976.3 6.3 all-to-all-start.5
  982.9 38.7 %collective-permute-done.57 = bf16[660,128]{1,0:T(8,128)(2,1)S(1)} collective-permute-done((bf16[660,128]{1,0:T(8,128)(2,1)S(1)}, bf16[660,128]{1,0:T(8,128)(2,1)S(1)}, u32[]{:S(2)}, u32[]{:S(2)}) %collective-permute-start.57) | collective-permute-done | bytes 168992 | tf_op jit(solution)/shard_map/ppermute | solution.py:45
  1029.8 4.5 add_convert_fusion.2
  1044.5 9.2 collective-permute-done.59
  1097.8 5.0 collective-permute-done.54
  1132.1 22.0 %reduce-scatter.3.cloned.1.call-done = bf16[1,384,640]{2,1,0:T(8,128)(2,1)} async-done(((bf16[8,384,640]{2,1,0:T(8,128)(2,1)}), bf16[1,384,640]{2,1,0:T(8,128)(2,1)}) %reduce-scatter.3.cloned.1.call-update) | async-done | bytes 491536 | tf_op jit(solution)/shard_map/reduce_scatter | solution.py:524
  (908 shorter events, 510.3 us)
Async XLA Ops:
  7.2 201.5 %all-gather.3.cloned.1.call-start = ((), (), s32[]{:S(2)}) async-start(), calls=%async_computation.12 | async-start | bytes 7999488 | tf_op jit(solution)/shard_map/all_gather | solution.py:327
  22.5 82.3 %all-to-all-start = ((bf16[8,256,512]{1,2,0:T(8,128)(2,1)}), bf16[8,256,512]{1,2,0:T(8,128)(2,1)S(1)}, u32[]{:S(2)}, u32[]{:S(2)}) async-start(bf16[8,256,512]{1,2,0:T(8,128)(2,1)} %bitcast.484), calls=%async_computation | async-start | bytes 4194304 | tf_op jit(solution)/shard_map/all_to_all | solution.py:151
  106.1 99.3 %all-to-all-start.1 = ((bf16[8,256,512]{1,2,0:T(8,128)(2,1)}), bf16[8,256,512]{1,2,0:T(8,128)(2,1)}, u32[]{:S(2)}, u32[]{:S(2)}) async-start(bf16[8,256,512]{1,2,0:T(8,128)(2,1)} %bitcast.5), calls=%async_computation.1 | async-start | bytes 4194304 | tf_op jit(solution)/shard_map/all_to_all | solution.py:151
  118.8 45.7 %collective-permute-start = (bf16[2048,512]{1,0:T(8,128)(2,1)}, bf16[2048,512]{1,0:T(8,128)(2,1)}, u32[]{:S(2)}, u32[]{:S(2)}) collective-permute-start(bf16[2048,512]{1,0:T(8,128)(2,1)} %bitcast.6), channel_id=1, source_target_pairs={{0,2},{2,0},{1,3},{3,1},{4,6},{6,4},{5,7},{7,5},{8,10},{10,8},{9,1... | collective-permute-start | bytes 6291464 | tf_op jit(solution)/shard_map/ppermute | solution.py:45
  123.5 323.0 %collective-permute-start.18 = (bf16[2048,512]{1,0:T(8,128)(2,1)}, bf16[2048,512]{1,0:T(8,128)(2,1)}, u32[]{:S(2)}, u32[]{:S(2)}) collective-permute-start(bf16[2048,512]{1,0:T(8,128)(2,1)} %bitcast.6), channel_id=1, source_target_pairs={{0,1},{1,0},{2,3},{3,2},{4,5},{5,4},{6,7},{7,6},{8,9},{9,8},{10,11... | collective-permute-start | bytes 6291464 | tf_op jit(solution)/shard_map/ppermute | solution.py:45
  208.7 79.5 %collective-permute-start.6 = (bf16[160,2048]{1,0:T(8,128)(2,1)}, bf16[160,2048]{1,0:T(8,128)(2,1)}, u32[]{:S(2)}, u32[]{:S(2)}) collective-permute-start(bf16[160,2048]{1,0:T(8,128)(2,1)} %maximum_maximum_fusion.2), channel_id=1, source_target_pairs={{0,4},{8,0},{16,8},{24,16},{28,24},{20,28},{12,20},{4,12},{1,5},{9... | collective-permute-start | bytes 1966088 | tf_op jit(solution)/shard_map/ppermute | solution.py:50
  209.9 84.9 %collective-permute-start.7 = (bf16[160,2048]{1,0:T(8,128)(2,1)}, bf16[160,2048]{1,0:T(8,128)(2,1)}, u32[]{:S(2)}, u32[]{:S(2)}) collective-permute-start(bf16[160,2048]{1,0:T(8,128)(2,1)} %maximum_maximum_fusion.2), channel_id=1, source_target_pairs={{0,8},{8,16},{16,24},{24,28},{28,20},{20,12},{12,4},{4,0},{1,9},{9... | collective-permute-start | bytes 1966088 | tf_op jit(solution)/shard_map/ppermute | solution.py:50
  244.5 26.8 %collective-permute-start.1 = (bf16[660,128]{1,0:T(8,128)(2,1)}, bf16[660,128]{1,0:T(8,128)(2,1)}, u32[]{:S(2)}, u32[]{:S(2)}) collective-permute-start(bf16[660,128]{1,0:T(8,128)(2,1)} %get-tuple-element.353), channel_id=1, source_target_pairs={{0,2},{2,0},{1,3},{3,1},{4,6},{6,4},{5,7},{7,5},{8,10},{10,8},{9,1... | collective-permute-start | bytes 506888 | tf_op jit(solution)/shard_map/ppermute | solution.py:45
  261.5 102.9 %collective-permute-start.9 = (bf16[2048,512]{1,0:T(8,128)(2,1)}, bf16[2048,512]{1,0:T(8,128)(2,1)}, u32[]{:S(2)}, u32[]{:S(2)}) collective-permute-start(bf16[2048,512]{1,0:T(8,128)(2,1)} %bitcast.511), channel_id=1, source_target_pairs={{0,2},{2,0},{1,3},{3,1},{4,6},{6,4},{5,7},{7,5},{8,10},{10,8},{9,1... | collective-permute-start | bytes 6291464 | tf_op jit(solution)/shard_map/ppermute | solution.py:45
  261.8 88.1 %all-to-all-start.3 = ((bf16[8,384,128]{1,2,0:T(8,128)(2,1)}), bf16[8,384,128]{1,2,0:T(8,128)(2,1)}, u32[]{:S(2)}, u32[]{:S(2)}) async-start(bf16[8,384,128]{1,2,0:T(8,128)(2,1)} %pad_maximum_fusion.11), calls=%async_computation.3 | async-start | bytes 1572864 | tf_op jit(solution)/shard_map/all_to_all | solution.py:151
  276.8 169.8 %collective-permute-start.19 = (bf16[2048,512]{1,0:T(8,128)(2,1)}, bf16[2048,512]{1,0:T(8,128)(2,1)}, u32[]{:S(2)}, u32[]{:S(2)}) collective-permute-start(bf16[2048,512]{1,0:T(8,128)(2,1)} %collective-permute-done), channel_id=1, source_target_pairs={{0,1},{1,0},{2,3},{3,2},{4,5},{5,4},{6,7},{7,6},{8,9},{9,8},{10,11... | collective-permute-start | bytes 6291464 | tf_op jit(solution)/shard_map/ppermute | solution.py:45
  349.9 54.2 %all-to-all-start.2 = ((bf16[8,512,256]{2,1,0:T(8,128)(2,1)}), bf16[8,512,256]{2,1,0:T(8,128)(2,1)}, u32[]{:S(2)}, u32[]{:S(2)}) async-start(bf16[8,512,256]{2,1,0:T(8,128)(2,1)} %bitcast.509), calls=%async_computation.2 | async-start | bytes 4194304 | tf_op jit(solution)/shard_map/all_to_all | solution.py:151
  404.2 30.7 %collective-permute-start.24 = (bf16[8,384,128]{1,2,0:T(8,128)(2,1)}, bf16[8,384,128]{1,2,0:T(8,128)(2,1)}, u32[]{:S(2)}, u32[]{:S(2)}) collective-permute-start(bf16[8,384,128]{1,2,0:T(8,128)(2,1)} %all-to-all-done.3), channel_id=1, source_target_pairs={{0,2},{2,0},{1,3},{3,1},{4,6},{6,4},{5,7},{7,5},{8,10},{10,8},{9,1... | collective-permute-start | bytes 2359304 | tf_op jit(solution)/shard_map/ppermute | solution.py:45
  434.9 65.0 %collective-permute-start.16 = (bf16[2048,512]{1,0:T(8,128)(2,1)S(1)}, bf16[2048,512]{1,0:T(8,128)(2,1)}, u32[]{:S(2)}, u32[]{:S(2)}) collective-permute-start(bf16[2048,512]{1,0:T(8,128)(2,1)S(1)} %bitcast.514), channel_id=1, source_target_pairs={{0,1},{1,0},{2,3},{3,2},{4,5},{5,4},{6,7},{7,6},{8,9},{9,8},{10,11... | collective-permute-start | bytes 6291464 | tf_op jit(solution)/shard_map/ppermute | solution.py:45
  438.0 62.0 %collective-permute-start.17 = (bf16[2048,512]{1,0:T(8,128)(2,1)}, bf16[2048,512]{1,0:T(8,128)(2,1)}, u32[]{:S(2)}, u32[]{:S(2)}) collective-permute-start(bf16[2048,512]{1,0:T(8,128)(2,1)} %collective-permute-done.9), channel_id=1, source_target_pairs={{0,1},{1,0},{2,3},{3,2},{4,5},{5,4},{6,7},{7,6},{8,9},{9,8},{10,11... | collective-permute-start | bytes 6291464 | tf_op jit(solution)/shard_map/ppermute | solution.py:45
  444.2 53.0 %collective-permute-start.10 = (bf16[512,2048]{0,1:T(8,128)(2,1)}, bf16[512,2048]{0,1:T(8,128)(2,1)}, u32[]{:S(2)}, u32[]{:S(2)}) collective-permute-start(bf16[512,2048]{0,1:T(8,128)(2,1)} %bitcast.517), channel_id=1, source_target_pairs={{0,2},{2,0},{1,3},{3,1},{4,6},{6,4},{5,7},{7,5},{8,10},{10,8},{9,1... | collective-permute-start | bytes 6291464 | tf_op jit(solution)/shard_map/ppermute | solution.py:45
  477.9 65.2 %collective-permute-start.11 = (bf16[512,2048]{0,1:T(8,128)(2,1)S(1)}, bf16[512,2048]{0,1:T(8,128)(2,1)}, u32[]{:S(2)}, u32[]{:S(2)}) collective-permute-start(bf16[512,2048]{0,1:T(8,128)(2,1)S(1)} %bitcast.520), channel_id=1, source_target_pairs={{0,1},{1,0},{2,3},{3,2},{4,5},{5,4},{6,7},{7,6},{8,9},{9,8},{10,11... | collective-permute-start | bytes 6291464 | tf_op jit(solution)/shard_map/ppermute | solution.py:45
  482.2 27.3 %collective-permute-start.30 = (bf16[160,2048]{1,0:T(8,128)(2,1)}, bf16[160,2048]{1,0:T(8,128)(2,1)S(1)}, u32[]{:S(2)}, u32[]{:S(2)}) collective-permute-start(bf16[160,2048]{1,0:T(8,128)(2,1)} %collective-permute-done.28), channel_id=1, source_target_pairs={{0,4},{8,0},{16,8},{24,16},{28,24},{20,28},{12,20},{4,12},{1,5},{9... | collective-permute-start | bytes 1966088 | tf_op jit(solution)/shard_map/ppermute | solution.py:50
  497.3 45.8 %collective-permute-start.12 = (bf16[512,2048]{0,1:T(8,128)(2,1)}, bf16[512,2048]{0,1:T(8,128)(2,1)}, u32[]{:S(2)}, u32[]{:S(2)}) collective-permute-start(bf16[512,2048]{0,1:T(8,128)(2,1)} %collective-permute-done.10), channel_id=1, source_target_pairs={{0,1},{1,0},{2,3},{3,2},{4,5},{5,4},{6,7},{7,6},{8,9},{9,8},{10,11... | collective-permute-start | bytes 6291464 | tf_op jit(solution)/shard_map/ppermute | solution.py:45
  516.7 181.5 %collective-permute-start.72 = (bf16[8,384,128]{2,1,0:T(8,128)(2,1)}, bf16[8,384,128]{2,1,0:T(8,128)(2,1)}, u32[]{:S(2)}, u32[]{:S(2)}) collective-permute-start(bf16[8,384,128]{2,1,0:T(8,128)(2,1)} %pad_maximum_fusion.12), channel_id=1, source_target_pairs={{0,1},{1,0},{2,3},{3,2},{4,5},{5,4},{6,7},{7,6},{8,9},{9,8},{10,11... | collective-permute-start | bytes 2359304 | tf_op jit(solution)/shard_map/ppermute | solution.py:45
  516.9 23.8 %collective-permute-start.73 = (bf16[8,384,128]{2,1,0:T(8,128)(2,1)S(1)}, bf16[8,384,128]{2,1,0:T(8,128)(2,1)S(1)}, u32[]{:S(2)}, u32[]{:S(2)}) collective-permute-start(bf16[8,384,128]{2,1,0:T(8,128)(2,1)S(1)} %pad_maximum_fusion.13), channel_id=1, source_target_pairs={{0,1},{1,0},{2,3},{3,2},{4,5},{5,4},{6,7},{7,6},{8,9},{9,8},{10,11... | collective-permute-start | bytes 2359304 | tf_op jit(solution)/shard_map/ppermute | solution.py:45
  541.9 156.3 %collective-permute-start.74 = (bf16[8,384,128]{2,1,0:T(8,128)(2,1)}, bf16[8,384,128]{2,1,0:T(8,128)(2,1)}, u32[]{:S(2)}, u32[]{:S(2)}) collective-permute-start(bf16[8,384,128]{2,1,0:T(8,128)(2,1)} %add_convert_fusion.9), channel_id=1, source_target_pairs={{0,2},{2,0},{1,3},{3,1},{4,6},{6,4},{5,7},{7,5},{8,10},{10,8},{9,1... | collective-permute-start | bytes 2359304 | tf_op jit(solution)/shard_map/ppermute | solution.py:45
  689.7 55.5 %collective-permute-start.39 = (bf16[512,2048]{1,0:T(8,128)(2,1)}, bf16[512,2048]{1,0:T(8,128)(2,1)}, u32[]{:S(2)}, u32[]{:S(2)}) collective-permute-start(bf16[512,2048]{1,0:T(8,128)(2,1)} %get-tuple-element.197), channel_id=1, source_target_pairs={{0,1},{1,0},{2,3},{3,2},{4,5},{5,4},{6,7},{7,6},{8,9},{9,8},{10,11... | collective-permute-start | bytes 6291464 | tf_op jit(solution)/shard_map/ppermute | solution.py:45
  690.3 88.0 %collective-permute-start.38 = (bf16[512,2048]{1,0:T(8,128)(2,1)}, bf16[512,2048]{1,0:T(8,128)(2,1)}, u32[]{:S(2)}, u32[]{:S(2)}) collective-permute-start(bf16[512,2048]{1,0:T(8,128)(2,1)} %get-tuple-element.196), channel_id=1, source_target_pairs={{0,1},{1,0},{2,3},{3,2},{4,5},{5,4},{6,7},{7,6},{8,9},{9,8},{10,11... | collective-permute-start | bytes 6291464 | tf_op jit(solution)/shard_map/ppermute | solution.py:45
  698.2 65.1 %collective-permute-start.45 = (bf16[2048,512]{1,0:T(8,128)(2,1)}, bf16[2048,512]{1,0:T(8,128)(2,1)}, u32[]{:S(2)}, u32[]{:S(2)}) collective-permute-start(bf16[2048,512]{1,0:T(8,128)(2,1)} %convolution_convert_fusion.8), channel_id=1, source_target_pairs={{0,1},{1,0},{2,3},{3,2},{4,5},{5,4},{6,7},{7,6},{8,9},{9,8},{10,11... | collective-permute-start | bytes 6291464 | tf_op jit(solution)/shard_map/ppermute | solution.py:45
  701.8 43.3 %all-to-all-start.7 = ((bf16[8,384,128]{2,1,0:T(8,128)(2,1)}), bf16[8,384,128]{2,1,0:T(8,128)(2,1)S(1)}, u32[]{:S(2)}, u32[]{:S(2)}) async-start(bf16[8,384,128]{2,1,0:T(8,128)(2,1)} %add_convert_fusion.8), calls=%async_computation.9 | async-start | bytes 1572864 | tf_op jit(solution)/shard_map/all_to_all | solution.py:151
  708.0 26.3 %collective-permute-start.32 = (bf16[160,2048]{1,0:T(8,128)(2,1)S(1)}, bf16[160,2048]{1,0:T(8,128)(2,1)S(1)}, u32[]{:S(2)}, u32[]{:S(2)}) collective-permute-start(bf16[160,2048]{1,0:T(8,128)(2,1)S(1)} %add_convert_fusion.19), channel_id=1, source_target_pairs={{0,4},{8,0},{16,8},{24,16},{28,24},{20,28},{12,20},{4,12},{1,5},{9... | collective-permute-start | bytes 1966088 | tf_op jit(solution)/shard_map/ppermute | solution.py:50
  735.4 34.3 %collective-permute-start.33 = (bf16[160,2048]{1,0:T(8,128)(2,1)}, bf16[160,2048]{1,0:T(8,128)(2,1)S(1)}, u32[]{:S(2)}, u32[]{:S(2)}) collective-permute-start(bf16[160,2048]{1,0:T(8,128)(2,1)} %add_convert_fusion.18), channel_id=1, source_target_pairs={{0,4},{8,0},{16,8},{24,16},{28,24},{20,28},{12,20},{4,12},{1,5},{9... | collective-permute-start | bytes 1966088 | tf_op jit(solution)/shard_map/ppermute | solution.py:50
  748.3 45.3 %collective-permute-start.40 = (bf16[512,2048]{1,0:T(8,128)(2,1)S(1)}, bf16[512,2048]{1,0:T(8,128)(2,1)S(1)}, u32[]{:S(2)}, u32[]{:S(2)}) collective-permute-start(bf16[512,2048]{1,0:T(8,128)(2,1)S(1)} %add_convert_fusion.7), channel_id=1, source_target_pairs={{0,2},{2,0},{1,3},{3,1},{4,6},{6,4},{5,7},{7,5},{8,10},{10,8},{9,1... | collective-permute-start | bytes 6291464 | tf_op jit(solution)/shard_map/ppermute | solution.py:45
  763.3 43.6 %collective-permute-start.44 = (bf16[2048,512]{1,0:T(8,128)(2,1)}, bf16[2048,512]{1,0:T(8,128)(2,1)}, u32[]{:S(2)}, u32[]{:S(2)}) collective-permute-start(bf16[2048,512]{1,0:T(8,128)(2,1)} %convolution_convert_fusion.10), channel_id=1, source_target_pairs={{0,1},{1,0},{2,3},{3,2},{4,5},{5,4},{6,7},{7,6},{8,9},{9,8},{10,11... | collective-permute-start | bytes 6291464 | tf_op jit(solution)/shard_map/ppermute | solution.py:45
  769.6 259.7 %collective-permute-start.60 = (bf16[2048,512]{1,0:T(8,128)(2,1)}, bf16[2048,512]{1,0:T(8,128)(2,1)}, u32[]{:S(2)}, u32[]{:S(2)}) collective-permute-start(bf16[2048,512]{1,0:T(8,128)(2,1)} %convolution_convert_fusion.6), channel_id=1, source_target_pairs={{0,1},{1,0},{2,3},{3,2},{4,5},{5,4},{6,7},{7,6},{8,9},{9,8},{10,11... | collective-permute-start | bytes 6291464 | tf_op jit(solution)/shard_map/ppermute | solution.py:45
  775.0 192.0 %collective-permute-start.61 = (bf16[2048,512]{1,0:T(8,128)(2,1)}, bf16[2048,512]{1,0:T(8,128)(2,1)}, u32[]{:S(2)}, u32[]{:S(2)}) collective-permute-start(bf16[2048,512]{1,0:T(8,128)(2,1)} %convolution_convert_fusion.4), channel_id=1, source_target_pairs={{0,1},{1,0},{2,3},{3,2},{4,5},{5,4},{6,7},{7,6},{8,9},{9,8},{10,11... | collective-permute-start | bytes 6291464 | tf_op jit(solution)/shard_map/ppermute | solution.py:45
  778.3 60.3 %collective-permute-start.46 = (bf16[2048,512]{1,0:T(8,128)(2,1)}, bf16[2048,512]{1,0:T(8,128)(2,1)}, u32[]{:S(2)}, u32[]{:S(2)}) collective-permute-start(bf16[2048,512]{1,0:T(8,128)(2,1)} %add_convert_fusion.5), channel_id=1, source_target_pairs={{0,2},{2,0},{1,3},{3,1},{4,6},{6,4},{5,7},{7,5},{8,10},{10,8},{9,1... | collective-permute-start | bytes 6291464 | tf_op jit(solution)/shard_map/ppermute | solution.py:45
  801.0 51.6 %collective-permute-start.41 = (bf16[160,2048]{1,0:T(8,128)(2,1)}, bf16[160,2048]{1,0:T(8,128)(2,1)}, u32[]{:S(2)}, u32[]{:S(2)}) collective-permute-start(bf16[160,2048]{1,0:T(8,128)(2,1)} %get-tuple-element.294), channel_id=1, source_target_pairs={{0,2},{2,0},{1,3},{3,1},{4,6},{6,4},{5,7},{7,5},{8,10},{10,8},{9,1... | collective-permute-start | bytes 1966088 | tf_op jit(solution)/shard_map/ppermute | solution.py:45
  802.8 155.2 %all-to-all-start.4 = ((bf16[8,512,256]{2,1,0:T(8,128)(2,1)}), bf16[8,512,256]{2,1,0:T(8,128)(2,1)S(1)}, u32[]{:S(2)}, u32[]{:S(2)}) async-start(bf16[8,512,256]{2,1,0:T(8,128)(2,1)} %bitcast.483), calls=%async_computation.4 | async-start | bytes 4194304 | tf_op jit(solution)/shard_map/all_to_all | solution.py:151
  806.9 310.9 %reduce-scatter.5.cloned.1.call-start = ((), (), s32[]{:S(2)}) async-start(), calls=%async_computation.11 | async-start | bytes 3538944 | tf_op jit(solution)/shard_map/reduce_scatter | solution.py:516
  807.0 50.1 %collective-permute-start.47 = (bf16[160,2048]{1,0:T(8,128)(2,1)}, bf16[160,2048]{1,0:T(8,128)(2,1)S(1)}, u32[]{:S(2)}, u32[]{:S(2)}) collective-permute-start(bf16[160,2048]{1,0:T(8,128)(2,1)} %maximum_maximum_fusion.18), channel_id=1, source_target_pairs={{0,4},{8,0},{16,8},{24,16},{28,24},{20,28},{12,20},{4,12},{1,5},{9... | collective-permute-start | bytes 1966088 | tf_op jit(solution)/shard_map/ppermute | solution.py:50
  854.2 30.2 %collective-permute-start.42 = (bf16[2,160,2048]{2,1,0:T(8,128)(2,1)S(1)}, bf16[2,160,2048]{2,1,0:T(8,128)(2,1)S(1)}, u32[]{:S(2)}, u32[]{:S(2)}) collective-permute-start(bf16[2,160,2048]{2,1,0:T(8,128)(2,1)S(1)} %maximum_select_fusion.4), channel_id=1, source_target_pairs={{0,1},{1,0},{2,3},{3,2},{4,5},{5,4},{6,7},{7,6},{8,9},{9,8},{10,11... | collective-permute-start | bytes 3932168 | tf_op jit(solution)/shard_map/ppermute | solution.py:45
  857.6 25.6 %collective-permute-start.51 = (bf16[160,2048]{1,0:T(8,128)(2,1)S(1)}, bf16[160,2048]{1,0:T(8,128)(2,1)S(1)}, u32[]{:S(2)}, u32[]{:S(2)}) collective-permute-start(bf16[160,2048]{1,0:T(8,128)(2,1)S(1)} %add_convert_fusion.12), channel_id=1, source_target_pairs={{0,8},{8,16},{16,24},{24,28},{28,20},{20,12},{12,4},{4,0},{1,9},{9... | collective-permute-start | bytes 1966088 | tf_op jit(solution)/shard_map/ppermute | solution.py:50
  877.6 77.6 %collective-permute-start.49 = (bf16[160,2048]{1,0:T(8,128)(2,1)}, bf16[160,2048]{1,0:T(8,128)(2,1)}, u32[]{:S(2)}, u32[]{:S(2)}) collective-permute-start(bf16[160,2048]{1,0:T(8,128)(2,1)} %add_convert_fusion.13), channel_id=1, source_target_pairs={{0,4},{8,0},{16,8},{24,16},{28,24},{20,28},{12,20},{4,12},{1,5},{9... | collective-permute-start | bytes 1966088 | tf_op jit(solution)/shard_map/ppermute | solution.py:50
  902.0 53.3 %collective-permute-start.53 = (bf16[160,2048]{1,0:T(8,128)(2,1)}, bf16[160,2048]{1,0:T(8,128)(2,1)}, u32[]{:S(2)}, u32[]{:S(2)}) collective-permute-start(bf16[160,2048]{1,0:T(8,128)(2,1)} %add_convert_fusion.10), channel_id=1, source_target_pairs={{0,8},{8,16},{16,24},{24,28},{28,20},{20,12},{12,4},{4,0},{1,9},{9... | collective-permute-start | bytes 1966088 | tf_op jit(solution)/shard_map/ppermute | solution.py:50
  905.1 47.7 %collective-permute-start.43 = (bf16[560,512]{1,0:T(8,128)(2,1)}, bf16[560,512]{1,0:T(8,128)(2,1)}, u32[]{:S(2)}, u32[]{:S(2)}) collective-permute-start(bf16[560,512]{1,0:T(8,128)(2,1)} %get-tuple-element.176), channel_id=1, source_target_pairs={{0,28},{4,0},{8,4},{12,8},{16,12},{20,16},{24,20},{28,24},{1,29},{... | collective-permute-start | bytes 1720328 | tf_op jit(solution)/shard_map/ppermute | solution.py:45
  970.5 58.8 %collective-permute-start.62 = (bf16[2048,512]{1,0:T(8,128)(2,1)}, bf16[2048,512]{1,0:T(8,128)(2,1)}, u32[]{:S(2)}, u32[]{:S(2)}) collective-permute-start(bf16[2048,512]{1,0:T(8,128)(2,1)} %add_convert_fusion.3), channel_id=1, source_target_pairs={{0,2},{2,0},{1,3},{3,1},{4,6},{6,4},{5,7},{7,5},{8,10},{10,8},{9,1... | collective-permute-start | bytes 6291464 | tf_op jit(solution)/shard_map/ppermute | solution.py:45
  974.1 47.5 %collective-permute-start.57 = (bf16[660,128]{1,0:T(8,128)(2,1)S(1)}, bf16[660,128]{1,0:T(8,128)(2,1)S(1)}, u32[]{:S(2)}, u32[]{:S(2)}) collective-permute-start(bf16[660,128]{1,0:T(8,128)(2,1)S(1)} %fusion.131), channel_id=1, source_target_pairs={{0,2},{2,0},{1,3},{3,1},{4,6},{6,4},{5,7},{7,5},{8,10},{10,8},{9,1... | collective-permute-start | bytes 506888 | tf_op jit(solution)/shard_map/ppermute | solution.py:45
  976.3 80.3 %all-to-all-start.5 = ((bf16[8,256,512]{2,1,0:T(8,128)(2,1)}), bf16[8,256,512]{2,1,0:T(8,128)(2,1)}, u32[]{:S(2)}, u32[]{:S(2)}) async-start(bf16[8,256,512]{2,1,0:T(8,128)(2,1)} %bitcast.110), calls=%async_computation.5 | async-start | bytes 4194304 | tf_op jit(solution)/shard_map/all_to_all | solution.py:151
  982.6 171.5 %reduce-scatter.3.cloned.1.call-start = ((), (), s32[]{:S(2)}) async-start(), calls=%async_computation.10 | async-start | bytes 4423680 | tf_op jit(solution)/shard_map/reduce_scatter | solution.py:524
  1086.7 69.6 %all-to-all-start.6 = ((bf16[8,256,512]{2,1,0:T(8,128)(2,1)}), bf16[8,256,512]{2,1,0:T(8,128)(2,1)S(1)}, u32[]{:S(2)}, u32[]{:S(2)}) async-start(bf16[8,256,512]{2,1,0:T(8,128)(2,1)} %bitcast.485), calls=%async_computation.8 | async-start | bytes 4194304 | tf_op jit(solution)/shard_map/all_to_all | solution.py:151
  1094.6 26.0 %collective-permute-start.64 = (bf16[2,160,2048]{2,1,0:T(8,128)(2,1)}, bf16[2,160,2048]{2,1,0:T(8,128)(2,1)}, u32[]{:S(2)}, u32[]{:S(2)}) collective-permute-start(bf16[2,160,2048]{2,1,0:T(8,128)(2,1)} %maximum_select_fusion.7), channel_id=1, source_target_pairs={{0,1},{1,0},{2,3},{3,2},{4,5},{5,4},{6,7},{7,6},{8,9},{9,8},{10,11... | collective-permute-start | bytes 3932168 | tf_op jit(solution)/shard_map/ppermute | solution.py:45
  (230 other events, 2151.9 us)
Sparse Core Ops, SparseCore 0:
  20.1 188.5 all-gather.2
  891.9 106.6 reduce-scatter.4
  1044.6 109.4 reduce-scatter.2

commit v3 on v2

v3 whole, which is shorter than its diff:
```python
import math

import jax
import jax.numpy as jnp
from jax import lax
from jax.experimental import pallas as pl
from jax.experimental.pallas import tpu as pltpu
from jax.sharding import PartitionSpec as P

IMG = 512
EPS = 1e-06
MASKED = -1e30
GELU_A = (2.0 / math.pi) ** 0.5
GELU_B = 0.044715
TILE = 256
VMEM_BYTES = 60 * 2**20
BF = jnp.bfloat16
F32 = jnp.float32

SNAKE = (0, 2, 4, 6, 7, 5, 3, 1)


def dot(left, right, left_dim, right_dim):
    return lax.dot_general(
        left, right, (((left_dim,), (right_dim,)), ((), ())), preferred_element_type=F32
    )


def fence(*values):
    return lax.optimization_barrier(values)


def cat(parts, axis=0):
    return parts[0] if len(parts) == 1 else jnp.concatenate(parts, axis=axis)


def pad_rows(block, rows):
    missing = rows - block.shape[0]
    return jnp.pad(block, ((0, missing), (0, 0))) if missing else block


def shift(block, axis, distance):
    count = lax.axis_size(axis)
    return lax.ppermute(block, axis, [(i, (i + distance) % count) for i in range(count)])


def ring_step(block, step):
    pairs = [(SNAKE[i], SNAKE[(i + step) % len(SNAKE)]) for i in range(len(SNAKE))]
    return lax.ppermute(block, "seq", pairs)


def ring_owners():
    count = len(SNAKE)
    place = jnp.array([SNAKE.index(i) for i in range(count)], jnp.int32)[lax.axis_index("seq")]
    steps = [(k + 1) // 2 if k % 2 else -(k // 2) for k in range(count)]
    return jnp.array(SNAKE, jnp.int32)[(place + jnp.array(steps, jnp.int32) + count) % count]


def on_ring():
    return lax.axis_size("seq") == len(SNAKE)


class Gathered:
    def __init__(self, block):
        self.ahead, self.behind = [block], [block]

    def hop(self):
        if on_ring():
            if len(self.ahead) <= len(SNAKE) // 2:
                self.ahead.append(ring_step(self.ahead[-1], -1))
            if len(self.behind) <= (len(SNAKE) - 1) // 2:
                self.behind.append(ring_step(self.behind[-1], 1))

    def meet(self, *values):
        self.ahead[-1], self.behind[-1], *values = fence(self.ahead[-1], self.behind[-1], *values)
        return values

    def blocks_and_owners(self):
        if not on_ring():
            whole = lax.all_gather(self.ahead[0], "seq", axis=0, tiled=False)
            return [whole[k] for k in range(whole.shape[0])], None
        order = [self.ahead[0]]
        for k in range(1, len(SNAKE)):
            order.append(self.ahead[(k + 1) // 2] if k % 2 else self.behind[k // 2])
        return order, ring_owners()


class Summed:
    def __init__(self, blocks):
        self.blocks, self.left, self.done = blocks, len(blocks) - 3, False
        self.going, self.back = blocks[-1], blocks[-2]

    def hop(self):
        if not on_ring():
            return
        going = ring_step(self.going, 1).astype(F32)
        if self.left < 0:
            self.back, self.done = self.back + going, True
            return
        self.going = (going + self.blocks[self.left].astype(F32)).astype(BF)
        back = ring_step(self.back, -1).astype(F32) + self.blocks[self.left - 1].astype(F32)
        self.back = back if self.left == 1 else back.astype(BF)
        self.left -= 2

    def meet(self, *values):
        self.going, self.back, *values = fence(self.going, self.back, *values)
        return values

    def total(self):
        if on_ring():
            assert self.done
            return self.back
        return lax.psum_scatter(jnp.stack(self.blocks), "seq", scatter_dimension=0).astype(F32)


def seq_halve(rows):
    count, index = rows.shape[0], lax.axis_index("seq")
    while count > 1:
        count //= 2
        bit = (index // count) % 2
        halves = rows.reshape(2, count, -1)
        keep = lax.dynamic_index_in_dim(halves, bit, 0, keepdims=False)
        give = lax.dynamic_index_in_dim(halves, 1 - bit, 0, keepdims=False)
        pairs = [(i, i ^ count) for i in range(lax.axis_size("seq"))]
        rows = keep + lax.ppermute(give, "seq", pairs)
    rows = rows + shift(rows, "expert", 1)
    return (rows + shift(rows, "mp", 1)).reshape(-1)


def swap(block, axis):
    return shift(block, axis, 1)


def quad_join(block, across, axis):
    return cat([block, across, swap(block, "expert"), swap(across, "expert")], axis)


def quad_gather(block):
    m, e = lax.axis_index("mp"), lax.axis_index("expert")
    across = swap(block, "mp")
    mine = jnp.where(m == 0, jnp.stack([block, across]), jnp.stack([across, block]))
    other = swap(mine, "expert")
    both = jnp.where(e == 0, jnp.stack([mine, other], 1), jnp.stack([other, mine], 1))
    return both.reshape((4,) + block.shape)


def quad_reduce(whole):
    m, e = lax.axis_index("mp"), lax.axis_index("expert")
    parts = whole.reshape((2, 2) + whole.shape[1:])
    give = lax.dynamic_index_in_dim(parts, 1 - e, 1, keepdims=False).astype(BF)
    keep = lax.dynamic_index_in_dim(parts, e, 1, keepdims=False).astype(F32)
    pair = keep + swap(give, "expert").astype(F32)
    give = lax.dynamic_index_in_dim(pair, 1 - m, 0, keepdims=False).astype(BF)
    keep = lax.dynamic_index_in_dim(pair, m, 0, keepdims=False)
    return keep + swap(give, "mp").astype(F32)


def pair_reduce_rel(parts):
    keep = parts[0].astype(F32) + swap(parts[2].astype(BF), "expert").astype(F32)
    give = parts[1].astype(F32) + swap(parts[3].astype(BF), "expert").astype(F32)
    return keep.astype(BF), give.astype(BF)


def across_reduce(keep, give):
    return (keep.astype(F32) + swap(give, "mp").astype(F32)).astype(BF)


def pack(prefix, action):
    fold = prefix.shape[-1] // action.shape[-1]
    rows = action.shape[-2] // fold
    parts = [action[..., k * rows : (k + 1) * rows, :] for k in range(fold)]
    return jnp.concatenate([prefix, jnp.concatenate(parts, axis=-1)], axis=-2)


def action_of(block, part_p, width):
    folded = block[..., part_p:, :]
    fold = folded.shape[-1] // width
    parts = [folded[..., k * width : (k + 1) * width] for k in range(fold)]
    return jnp.concatenate(parts, axis=-2)


def a2a(parts):
    return lax.all_to_all(parts, "seq", 0, 0, tiled=True)


def split_columns(weight):
    depth, width = weight.shape
    count = lax.axis_size("seq")
    return weight.reshape(depth, count, width // count).transpose(1, 0, 2)


def split_rows(weight):
    width, depth = weight.shape
    count = lax.axis_size("seq")
    return weight.reshape(count, width // count, depth)


def join_rows(parts):
    return parts.reshape(-1, parts.shape[-1])


def join_columns(parts):
    return parts.transpose(1, 0, 2).reshape(parts.shape[1], -1)


def rms_norm(values, gain_vec):
    return values * lax.rsqrt(jnp.mean(values * values, axis=-1, keepdims=True) + EPS) * gain_vec


def norm_backward(values, gain_vec, grad_normed):
    return jax.vjp(rms_norm, values, gain_vec)[1](grad_normed)


def geglu_act(gate_pre, up_pre):
    return jax.nn.gelu(gate_pre, approximate=True) * up_pre


def attend_forward(query_flat, key_rows, value_rows, keep_mask):
    row_count = query_flat.shape[0]
    head_size = key_rows.shape[1]
    query_heads = query_flat.reshape(row_count, -1, head_size)
    scores = jnp.einsum(
        "qhd,kd->hqk", query_heads, key_rows, preferred_element_type=F32
    ) * (head_size ** (-0.5))
    scores = jnp.where(keep_mask[None, None, :], scores, MASKED)
    expo = jnp.exp(scores - jnp.max(scores, axis=-1, keepdims=True))
    probs = expo / jnp.sum(expo, axis=-1, keepdims=True)
    mixed_rows = jnp.einsum(
        "hqk,kd->qhd", probs.astype(BF), value_rows, preferred_element_type=F32
    )
    return mixed_rows.reshape(row_count, -1).astype(BF), probs


def attend_backward(query_flat, key_rows, value_rows, probs, grad_mixed):
    row_count = query_flat.shape[0]
    head_size = key_rows.shape[1]
    score_scale = head_size ** (-0.5)
    query_heads = query_flat.reshape(row_count, -1, head_size)
    grad_heads = grad_mixed.reshape(row_count, -1, head_size)
    grad_probs = jnp.einsum("qhd,kd->hqk", grad_heads, value_rows, preferred_element_type=F32)
    row_inner = jnp.sum(grad_probs * probs, axis=-1, keepdims=True)
    grad_scores = (probs * (grad_probs - row_inner)).astype(BF)
    grad_query = jnp.einsum("hqk,kd->qhd", grad_scores, key_rows, preferred_element_type=F32)
    grad_query = (grad_query * score_scale).reshape(row_count, -1).astype(BF)
    grad_keys = score_scale * jnp.einsum(
        "hqk,qhd->kd", grad_scores, query_heads, preferred_element_type=F32
    )
    grad_values = jnp.einsum(
        "hqk,qhd->kd", probs.astype(BF), grad_heads, preferred_element_type=F32
    )
    return grad_query, jnp.concatenate([grad_keys, grad_values], axis=1)


def gelu_parts(gate):
    square = gate * gate
    bend = jnp.tanh(gate * (GELU_A + (GELU_A * GELU_B) * square))
    half = 0.5 + 0.5 * bend
    act = gate * half
    return act, half + act * (1.0 - bend) * (GELU_A + (3.0 * GELU_A * GELU_B) * square)


def feed_back(normed, cot, w_gate, w_up, w_down):
    gate, up, grad = dot(normed, w_gate, 1, 0), dot(normed, w_up, 1, 0), dot(cot, w_down, 1, 1)
    act, slope = gelu_parts(gate)
    return (act * up).astype(BF), (grad * up * slope).astype(BF), (grad * act).astype(BF)


def whole_block(shape):
    return pl.BlockSpec(shape, lambda j, *_: (0,) * len(shape), pipeline_mode=pl.Buffered(1))


def column_block(rows, tile):
    return pl.BlockSpec((rows, tile), lambda j, *_: (0, j))


def row_block(tile, columns):
    return pl.BlockSpec((tile, columns), lambda j, *_: (j, 0))


def row_kernel(body, count, ins, outs, flops, name, order=(), scratch=()):
    moved = sum(math.prod(a.shape) * a.dtype.itemsize for a, _ in ins + outs)
    return pl.pallas_call(
        body,
        grid_spec=pltpu.PrefetchScalarGridSpec(
            num_scalar_prefetch=len(order),
            grid=(count,),
            in_specs=[spec for _, spec in ins],
            out_specs=[spec for _, spec in outs],
            scratch_shapes=scratch,
        ),
        out_shape=[shape for shape, _ in outs],
        compiler_params=pltpu.CompilerParams(vmem_limit_bytes=VMEM_BYTES),
        cost_estimate=pl.CostEstimate(flops=flops, transcendentals=0, bytes_accessed=moved),
        name=name,
    )(*order, *[a for a, _ in ins])


def like(rows, columns):
    return jax.ShapeDtypeStruct((rows, columns), BF)


def feed_inner(normed, cots, part, w_gate, w_up, w_down, width_a):
    depth, width = w_gate[0].shape[0], 4 * w_gate[0].shape[1]
    normed, order = normed.blocks_and_owners()
    count, packed = cots.shape[0], cots.shape[1]
    rows, part_a = count * part, (packed - part) * depth // width_a
    if not on_ring():
        whole = jnp.stack(normed)
        joined = [block[:, :part].reshape(rows, depth) for block in (whole, cots)]
        action = [action_of(block, part, width_a).reshape(-1, width_a) for block in (whole, cots)]
        weights = cat(w_gate, 1), cat(w_up, 1), cat(w_down, 0)
        return feed_back(*joined, *weights), joined, action

    def place(block, owner, out_ref, action_ref):
        out_ref[pl.ds(pl.multiple_of(owner * part, 16), part), :] = block[:part, :]
        for k in range(depth // width_a):
            at = pl.multiple_of(owner * part_a + k * (packed - part), 16)
            columns = pl.ds(k * width_a, width_a)
            action_ref[pl.ds(at, packed - part), :] = block[part:packed, columns]

    steps = width // 4 // TILE

    def body(order_ref, *refs):
        cot_ref, weights = refs[count], refs[count + 1 : count + 13]
        mid_ref, dg_ref, du_ref, n_ref, c_ref, na_ref, ca_ref = refs[count + 13 : count + 20]
        chosen = refs[count + 20 :]

        @pl.when(pl.program_id(0) == 0)
        def _():
            for k in range(count):
                place(refs[k], order_ref[k], n_ref, na_ref)
                place(cot_ref.at[k], k, c_ref, ca_ref)

        for q in range(4):

            @pl.when(pl.program_id(0) // steps == q)
            def _():
                for k in range(3):
                    chosen[k][...] = weights[4 * k + q][...]

        mid_ref[...], dg_ref[...], du_ref[...] = feed_back(
            n_ref[...], c_ref[...], *[ref[...] for ref in chosen]
        )

    def part_of(q, axis):
        def index(j, *_):
            at = jnp.clip(j - q * steps, 0, steps - 1)
            return (0, at) if axis else (at, 0)

        return pl.BlockSpec((depth, TILE) if axis else (TILE, depth), index)

    ins = [(block, whole_block((packed, depth))) for block in normed]
    ins += [(cots, whole_block((count, packed, depth)))]
    ins += [(w_gate[q], part_of(q, 1)) for q in range(4)]
    ins += [(w_up[q], part_of(q, 1)) for q in range(4)]
    ins += [(w_down[q], part_of(q, 0)) for q in range(4)]
    outs = [(like(rows, width), column_block(rows, TILE))] * 3
    outs += [(like(rows, depth), whole_block((rows, depth)))] * 2
    outs += [(like(count * part_a, width_a), whole_block((count * part_a, width_a)))] * 2
    scratch = [pltpu.VMEM((depth, TILE), BF)] * 2 + [pltpu.VMEM((TILE, depth), BF)]
    flops = 6 * rows * depth * width
    out = row_kernel(body, width // TILE, ins, outs, flops, "feed_inner", (order,), scratch)
    return out[:3], out[3:5], out[5:]


def feed_outer(d_gate, d_up, w_gate, w_up):
    if not on_ring():
        return (dot(d_gate, cat(w_gate, 1), 1, 1) + dot(d_up, cat(w_up, 1), 1, 1)).astype(BF)
    (rows, width), depth = d_gate.shape, w_gate[0].shape[0]

    def body(dg_ref, du_ref, *refs):
        gate, up = (cat([ref[...] for ref in refs[k : k + 4]], 1) for k in (0, 4))
        total = dot(dg_ref[...], gate, 1, 1) + dot(du_ref[...], up, 1, 1)
        refs[8][...] = total.astype(BF)

    ins = [(d_gate, whole_block((rows, width))), (d_up, whole_block((rows, width)))]
    ins += [(part, row_block(TILE, width // 4)) for part in list(w_gate) + list(w_up)]
    outs = [(like(rows, depth), column_block(rows, TILE))]
    return row_kernel(body, depth // TILE, ins, outs, 4 * rows * depth * width, "feed_outer")[0]


def feed_down(mid, w_down):
    if not on_ring():
        return dot(mid, cat(w_down, 0), 1, 0).astype(BF)
    (rows, width), depth = mid.shape, w_down[0].shape[1]

    def body(mid_ref, *refs):
        weight = cat([ref[...] for ref in refs[:4]], 0)
        refs[4][...] = dot(mid_ref[...], weight, 1, 0).astype(BF)

    ins = [(mid, whole_block((rows, width)))]
    ins += [(part, column_block(width // 4, TILE)) for part in w_down]
    outs = [(like(rows, depth), column_block(rows, TILE))]
    return row_kernel(body, depth // TILE, ins, outs, 2 * rows * depth * width, "feed_down")[0]


def weight_grad(left, right):
    return dot(left, right, 0, 0).astype(BF)


def quarters(array, axis):
    return jnp.split(array, 4, axis=axis)


def quarter_grads(left, right):
    if not on_ring():
        return quarters(weight_grad(left, right), 1)
    (rows, depth), width = left.shape, right.shape[1]

    def body(left_ref, right_ref, *out_refs):
        out = dot(left_ref[...], right_ref[...], 0, 0).astype(BF)
        for k, out_ref in enumerate(out_refs):
            out_ref[...] = out[:, k * (width // 4) : (k + 1) * (width // 4)]

    ins = [(left, column_block(rows, TILE)), (right, whole_block((rows, width)))]
    outs = [(like(depth, width // 4), row_block(TILE, width // 4))] * 4
    return row_kernel(body, depth // TILE, ins, outs, 2 * rows * depth * width, "feed_grads")


def body(
    hidden_prefix,
    hidden_action,
    norm1_prefix,
    query_prefix,
    key_prefix,
    value_prefix,
    out_prefix,
    norm2_prefix,
    gate_prefix,
    up_prefix,
    down_prefix,
    norm1_action,
    query_action,
    key_action,
    value_action,
    out_action,
    norm2_action,
    gate_action,
    up_action,
    down_action,
    cot_prefix,
    cot_action,
    instr_len,
    slot_source,
):
    seq_index = lax.axis_index("seq")
    episodes = lax.axis_size("seq")
    quad = lax.axis_size("mp") * lax.axis_size("expert")
    mine = lax.axis_index("mp") * lax.axis_size("expert") + lax.axis_index("expert")
    prefix_rows, action_rows_all = hidden_prefix.shape[0], hidden_action.shape[0]
    slot_count = slot_source.shape[0]
    action_rows = action_rows_all // slot_count
    head_size = key_prefix.shape[1]
    head_cols = query_prefix.shape[1]
    part_p = -(-prefix_rows // (16 * quad)) * 16
    part_a = -(-action_rows_all // (16 * quad)) * 16
    kv_cols = 2 * head_size // quad

    positions = jnp.arange(prefix_rows, dtype=jnp.int32)
    keep_prefix = positions < IMG + instr_len[seq_index]
    live_slot = slot_source >= 0
    offsets = jnp.where(live_slot, slot_source, 0)
    source_ep = (seq_index - offsets + episodes) % episodes
    keep_slots = (positions[None, :] < IMG + instr_len[source_ep][:, None]) & live_slot[:, None]
    keep_all = jnp.concatenate(
        [keep_slots, jnp.ones((slot_count, action_rows), dtype=bool)], axis=1
    )
    from_prev = slot_source == 1
    from_here = slot_source == 0
    live_rows = jnp.repeat(live_slot.astype(F32), action_rows)[:, None]

    def own_part(rows, part):
        return lax.dynamic_slice_in_dim(pad_rows(rows, quad * part), mine * part, part, axis=0)

    x_p, x_a = own_part(hidden_prefix, part_p), own_part(hidden_action, part_a)
    x_p, x_a = x_p.astype(F32), x_a.astype(F32)
    live_a = own_part(live_rows, part_a)
    cot_p, cot_a = own_part(cot_prefix, part_p), own_part(cot_action, part_a)
    cot_block = pack(cot_p, (cot_a.astype(F32) * live_a).astype(BF))

    def quarter_kv(w_key, w_value):
        return lax.dynamic_slice_in_dim(
            jnp.concatenate([w_key, w_value], axis=1), mine * kv_cols, kv_cols, axis=1
        )

    early_cols = head_cols + kv_cols
    depth_p, depth_a = query_prefix.shape[0], query_action.shape[0]
    gains = jnp.concatenate([norm1_prefix, norm2_prefix, norm1_action, norm2_action])
    gain_rows = -(-gains.shape[0] // (16 * early_cols)) * 16
    gain_block = jnp.pad(gains, (0, gain_rows * early_cols - gains.shape[0]))
    early = jnp.concatenate(
        [
            jnp.concatenate([query_prefix, quarter_kv(key_prefix, value_prefix)], axis=1),
            jnp.concatenate([query_action, quarter_kv(key_action, value_action)], axis=1),
            gain_block.reshape(gain_rows, early_cols),
        ],
        axis=0,
    )
    early = lax.all_gather(early, "seq", axis=0, tiled=False)
    in_action = [split_columns(gate_action), split_columns(up_action), split_rows(down_action)]
    in_action = jnp.concatenate(in_action, axis=1)
    late = jnp.concatenate([out_prefix, out_action], axis=1)
    late = lax.all_gather(late, "seq", axis=0, tiled=False)

    gate_p = join_rows(a2a(split_columns(gate_prefix)))
    gate_other = swap(gate_p, "expert")
    early, gate_other = fence(early, gate_other)
    w_in_p = early[:, :depth_p].reshape(-1, early_cols)
    w_in_a = early[:, depth_p : depth_p + depth_a].reshape(-1, early_cols)
    gains = early[:, depth_p + depth_a :].reshape(episodes, -1)
    gain1_p = gains[:, :depth_p].reshape(-1).astype(F32)
    gain2_p = gains[:, depth_p : 2 * depth_p].reshape(-1).astype(F32)
    gain1_a = gains[:, 2 * depth_p : 2 * depth_p + depth_a].reshape(-1).astype(F32)
    gain2_a = gains[:, 2 * depth_p + depth_a : 2 * (depth_p + depth_a)].reshape(-1).astype(F32)

    normed1_p = rms_norm(hidden_prefix.astype(F32), gain1_p).astype(BF)
    normed1_a = rms_norm(hidden_action.astype(F32), gain1_a).astype(BF)
    in_p, in_a = dot(normed1_p, w_in_p, 1, 0).astype(BF), dot(normed1_a, w_in_a, 1, 0).astype(BF)
    kv_prev = shift(in_p[:, head_cols:], "seq", 1)
    kv_own = jnp.concatenate([in_p[:, head_cols:], in_a[:, head_cols:]], axis=0)

    def whole_kv(quarter):
        return quad_gather(quarter).transpose(1, 0, 2).reshape(-1, 2 * head_size)

    kv_own = whole_kv(kv_own)
    in_p, in_a, kv_own, kv_prev, gate_p, up_p, cot_block = fence(
        in_p, in_a, kv_own, kv_prev, gate_p, split_columns(up_prefix), cot_block
    )
    gate_far = swap(gate_p, "mp")
    query_p, query_a = in_p[:, :head_cols], in_a[:, :head_cols]
    up_p = a2a(up_p)
    cots = lax.all_gather(cot_block, "seq", axis=0, tiled=False)
    kv_prev = whole_kv(kv_prev)
    kv_p, kv_a = kv_own[:prefix_rows], kv_own[prefix_rows:]
    keys_p, values_p = kv_p[:, :head_size], kv_p[:, head_size:]
    mixed_p, probs_p = attend_forward(query_p, keys_p, values_p, keep_prefix)
    kv_slots = jnp.where(from_prev[:, None, None], kv_prev[None], kv_p[None])
    kv_slots = jnp.concatenate([kv_slots, kv_a.reshape(slot_count, action_rows, -1)], axis=1)
    keys_slots, values_slots = kv_slots[:, :, :head_size], kv_slots[:, :, head_size:]
    query_slots = query_a.reshape(slot_count, action_rows, -1)
    mixed_slots, probs_a = jax.vmap(attend_forward)(
        query_slots, keys_slots, values_slots, keep_all
    )
    mixed_a = mixed_slots.reshape(action_rows_all, -1)
    mixed_p, mixed_a, up_p, gate_far, down_p = fence(
        mixed_p, mixed_a, up_p, gate_far, split_rows(down_prefix)
    )
    down_p, up_p = a2a(down_p), join_rows(up_p)
    gate_far_other = swap(gate_far, "expert")
    up_far, up_other = swap(up_p, "mp"), swap(up_p, "expert")
    w_gate_p = [gate_p, gate_far, gate_other, gate_far_other]
    w_out_p = join_columns(late[:, :, :depth_p])
    w_out_a = join_columns(late[:, :, depth_p:])
    attn_p = dot(pad_rows(mixed_p, quad * part_p), w_out_p, 1, 0).reshape(quad, part_p, -1)
    attn_a = dot(pad_rows(mixed_a, quad * part_a), w_out_a, 1, 0).reshape(quad, part_a, -1)
    attn, up_far, up_other = fence(pack(attn_p, attn_a), up_far, up_other)
    attn, down_p = fence(quad_reduce(attn), down_p)
    down_p = join_columns(down_p)
    down_far, down_other = swap(down_p, "mp"), swap(down_p, "expert")
    middle_p = x_p + attn[:part_p]
    middle_a = x_a + live_a * action_of(attn, part_p, x_a.shape[1])
    normed2 = Gathered(
        pack(rms_norm(middle_p, gain2_p).astype(BF), rms_norm(middle_a, gain2_a).astype(BF))
    )
    normed2.hop()
    w_up_p = [up_p, up_far, up_other, swap(up_far, "expert")]
    w_up_p = normed2.meet(w_up_p)[0]
    normed2.hop()
    normed2.meet()
    normed2.hop()
    down_far, down_other = normed2.meet(down_far, down_other)
    normed2.hop()
    w_down_p = [down_p, down_far, down_other, swap(down_far, "expert")]
    w_down_p, cots, in_action = normed2.meet(w_down_p, cots, in_action)
    in_action = a2a(in_action)

    inner, (normed2_p, cots_p), (normed2_a, cots_a) = feed_inner(
        normed2, cots, part_p, w_gate_p, w_up_p, w_down_p, x_a.shape[1]
    )
    mid_p, d_gate_p, d_up_p = inner
    mid_p, d_gate_p, d_up_p, in_action = fence(mid_p, d_gate_p, d_up_p, in_action)
    far_action = swap(in_action, "mp")
    dwd_p = quarters(weight_grad(mid_p, cots_p), 0)
    dwd_p, mid_p, far_action = fence(dwd_p, mid_p, far_action)
    dwd_p, y_sum = pair_reduce_rel(dwd_p), feed_down(mid_p, w_down_p)
    in_action = [in_action, far_action, swap(in_action, "expert"), swap(far_action, "expert")]
    dwd_p, y_sum, d_gate_p, in_action = fence(dwd_p, y_sum, d_gate_p, in_action)
    y_sum = y_sum.reshape(episodes, part_p, -1)
    y_sum = lax.psum_scatter(y_sum, "seq", scatter_dimension=0).astype(F32)
    dwd_p, dwg_p = across_reduce(*dwd_p), quarter_grads(normed2_p, d_gate_p)
    w_gate_a = cat([join_rows(part[:, :depth_a]) for part in in_action], 1)
    w_up_a = cat([join_rows(part[:, depth_a : 2 * depth_a]) for part in in_action], 1)
    w_down_a = cat([join_columns(part[:, 2 * depth_a :]) for part in in_action], 0)
    mid_a, d_gate_a, d_up_a = feed_back(normed2_a, cots_a, w_gate_a, w_up_a, w_down_a)
    gn2_a = (dot(d_gate_a, w_gate_a, 1, 1) + dot(d_up_a, w_up_a, 1, 1)).astype(BF)
    y_a = dot(mid_a, w_down_a, 1, 0).astype(BF)
    d_action = zip(
        quarters(weight_grad(normed2_a, d_gate_a), 1),
        quarters(weight_grad(normed2_a, d_up_a), 1),
        quarters(weight_grad(mid_a, cots_a), 0),
    )
    d_action = [
        jnp.concatenate([split_rows(g), split_rows(u), split_columns(d)], axis=1)
        for g, u, d in d_action
    ]
    dwd_p, dwg_p, d_gate_p, d_up_p, d_action = fence(dwd_p, dwg_p, d_gate_p, d_up_p, d_action)
    dwd_p, dwg_p = a2a(split_columns(dwd_p)), pair_reduce_rel(dwg_p)
    dwu_p, d_action = quarter_grads(normed2_p, d_up_p), pair_reduce_rel(d_action)
    dwg_p, dwu_p, d_gate_p, d_up_p, d_action = fence(dwg_p, dwu_p, d_gate_p, d_up_p, d_action)
    dwg_p, dwu_p = across_reduce(*dwg_p), pair_reduce_rel(dwu_p)
    d_action = across_reduce(*d_action)
    gn2_p = feed_outer(d_gate_p, d_up_p, w_gate_p, w_up_p).reshape(episodes, part_p, -1)
    gn2_a, y_a = gn2_a.reshape(episodes, part_a, -1), y_a.reshape(episodes, part_a, -1)
    owners = ring_owners() if on_ring() else range(episodes)
    chunks = [pack(pack(gn2_p[k], gn2_a[k]), y_a[k]) for k in [owners[k] for k in range(episodes)]]
    chunks, dwd_p, dwg_p, dwu_p, y_sum, d_action = fence(
        chunks, dwd_p, dwg_p, dwu_p, y_sum, d_action
    )
    gn2 = Summed(chunks)
    gn2.hop()
    dwu_p = across_reduce(*dwu_p)
    gn2.meet()
    gn2.hop()
    gn2.meet()
    gn2.hop()
    dwu_p = gn2.meet(dwu_p)[0]
    gn2.hop()
    gn2, dwg_p, d_action = fence(gn2.total(), dwg_p, d_action)
    d_action = a2a(d_action).astype(F32)
    packed = x_p.shape[0] + x_a.shape[0] * x_a.shape[1] // x_p.shape[1]
    y_a = action_of(gn2, packed, x_a.shape[1])
    gn2 = gn2[:packed]

    dmid_norm_p, dgain2_p = norm_backward(middle_p, gain2_p, gn2[:part_p])
    dmid_norm_a, dgain2_a = norm_backward(
        middle_a, gain2_a, action_of(gn2, part_p, x_a.shape[1])
    )
    dmid_p = cot_p.astype(F32) + dmid_norm_p
    dmid_a = cot_a.astype(F32) + dmid_norm_a
    dao = quad_gather(pack(dmid_p.astype(BF), (dmid_a * live_a).astype(BF)))

    def whole_rows(block):
        prefix = block[:, :part_p].reshape(quad * part_p, -1)[:prefix_rows]
        action = action_of(block, part_p, x_a.shape[1]).reshape(quad * part_a, -1)
        return prefix, action[:action_rows_all]

    dao_p, dao_a = whole_rows(dao)
    dao_p, dao_a, dwg_p, d_action = fence(dao_p, dao_a, dwg_p, d_action)
    dwg_p = a2a(split_rows(dwg_p))

    dwo = jnp.concatenate(
        [
            weight_grad(mixed_p, dao_p).reshape(head_cols, episodes, -1),
            weight_grad(mixed_a, dao_a).reshape(head_cols, episodes, -1),
        ],
        axis=2,
    ).transpose(1, 0, 2)
    dwo = lax.psum_scatter(dwo, "seq", scatter_dimension=0, tiled=False).astype(F32)
    dmix_p, dmix_a = dot(dao_p, w_out_p, 1, 1).astype(BF), dot(dao_a, w_out_a, 1, 1).astype(BF)
    dq_slots, dkv_slots = jax.vmap(attend_backward)(
        query_slots,
        keys_slots,
        values_slots,
        probs_a,
        dmix_a.reshape(slot_count, action_rows, -1),
    )
    dkv_pre = dkv_slots[:, :prefix_rows]
    dkv_a = dkv_slots[:, prefix_rows:].reshape(action_rows_all, -1)
    to_prev = jnp.sum(jnp.where(from_prev[:, None, None], dkv_pre, 0.0), axis=0)
    to_here = jnp.sum(jnp.where(from_here[:, None, None], dkv_pre, 0.0), axis=0)

    def own_quarter(rows):
        return quad_reduce(rows.reshape(-1, quad, kv_cols).transpose(1, 0, 2))

    returned = own_quarter(jnp.concatenate([to_prev, dkv_a], axis=0))
    dkv_a = returned[prefix_rows:].astype(BF)
    returned = shift(returned[:prefix_rows].astype(BF), "seq", -1)
    returned, dkv_a, dmix_p, dwg_p, dwu_p = fence(returned, dkv_a, dmix_p, dwg_p, dwu_p)
    dwu_p = a2a(split_rows(dwu_p))
    dq_p, dkv_p = attend_backward(query_p, keys_p, values_p, probs_p, dmix_p)
    dkv_p = dkv_p + to_here
    dq_a = dq_slots.reshape(action_rows_all, -1)

    dkv_p = (own_quarter(dkv_p) + returned.astype(F32)).astype(BF)
    din_p = jnp.concatenate([dq_p, dkv_p], axis=1)
    din_a = jnp.concatenate([dq_a, dkv_a], axis=1)
    gn1_p = dot(pad_rows(din_p, quad * part_p), w_in_p, 1, 1).reshape(quad, part_p, -1)
    gn1_a = dot(pad_rows(din_a, quad * part_a), w_in_a, 1, 1).reshape(quad, part_a, -1)
    gn1 = quad_reduce(pack(gn1_p, gn1_a))
    gn1, dwu_p, dwo = fence(gn1, dwu_p, dwo)
    dx_norm_p, dgain1_p = norm_backward(x_p, gain1_p, gn1[:part_p])
    dx_norm_a, dgain1_a = norm_backward(x_a, gain1_a, action_of(gn1, part_p, x_a.shape[1]))
    dx = quad_gather(pack((dmid_p + dx_norm_p).astype(BF), (dmid_a + dx_norm_a).astype(BF)))
    dx_p, dx_a = whole_rows(dx)
    dx_p, dx_a = dx_p.astype(F32), dx_a.astype(F32)
    y_p, y_a = middle_p + y_sum, middle_a + live_a * y_a
    y_out = quad_gather(pack(y_p.astype(BF), y_a.astype(BF)))
    y_p, y_a = whole_rows(y_out)

    dwd_p = join_rows(dwd_p).astype(F32)
    dwg_p = join_columns(dwg_p).astype(F32)
    dwu_p = join_columns(dwu_p).astype(F32)
    dwg_a = join_columns(d_action[:, :depth_a])
    dwu_a = join_columns(d_action[:, depth_a : 2 * depth_a])
    dwd_a = join_rows(d_action[:, 2 * depth_a :])

    dw_in = jnp.concatenate(
        [
            weight_grad(normed1_p, din_p).reshape(episodes, -1, early_cols),
            weight_grad(normed1_a, din_a).reshape(episodes, -1, early_cols),
        ],
        axis=1,
    )
    dw_in = lax.psum_scatter(dw_in, "seq", scatter_dimension=0, tiled=False)
    dw_kv = quad_gather(dw_in[:, head_cols:]).transpose(1, 0, 2).reshape(-1, 2 * head_size)
    dw_kv = dw_kv.astype(F32)
    dw_in = dw_in.astype(F32)

    dgains = jnp.concatenate(
        [g.reshape(episodes, -1) for g in (dgain1_p, dgain2_p, dgain1_a, dgain2_a)], axis=1
    )
    dgains = seq_halve(dgains)
    return (
        y_p,
        y_a,
        dx_p,
        dx_a,
        dgains[:depth_p],
        dw_in[:depth_p, :head_cols],
        dw_kv[:depth_p, :head_size],
        dw_kv[:depth_p, head_size:],
        dwo[:, :depth_p],
        dgains[depth_p : 2 * depth_p],
        dwg_p,
        dwu_p,
        dwd_p,
        dgains[2 * depth_p : 2 * depth_p + depth_a],
        dw_in[depth_p:, :head_cols],
        dw_kv[depth_p:, :head_size],
        dw_kv[depth_p:, head_size:],
        dwo[:, depth_p:],
        dgains[2 * depth_p + depth_a :],
        dwg_a,
        dwu_a,
        dwd_a,
    )


def solution(mesh):
    rows, flat = P("seq", None), P("seq")
    wide, tall = P("seq", ("mp", "expert")), P(("mp", "expert"), "seq")
    one_expert = (flat, wide, rows, rows, tall, flat, wide, wide, tall)
    return jax.shard_map(
        body,
        mesh=mesh,
        in_specs=(rows, rows) + one_expert + one_expert + (rows, rows, P(), flat),
        out_specs=(rows, rows, rows, rows) + one_expert + one_expert,
        check_vma=False,
    )
```

time: 1190 us -> 1080 us (0.908)
  matrix products: 207 us -> 51.2 us
  Pallas kernels: 0 us -> 119 us
  local copies, waits for them, and re-layouts: 213 us -> 122 us
  blocking collectives: 0 us -> 88.4 us
  starting transfers between devices: 163 us -> 130 us
  waiting for transfers between devices: 436 us -> 405 us
  between operations: 18 us -> 33.7 us
    dot_general x42 -> x22, matrix products: 194 us -> 38.8 us  [dot(): lax.dot_general(left, right, (((left_dim,), (right_dim,)), ((), ())), pre...]
    pallas_call x0 -> x5, Pallas kernels: none -> 119 us  [row_kernel(): pl.pallas_call(body, grid_spec=pltpu.PrefetchScalarGridSpec(num_scalar_pr...]
    all_to_all x0 -> x1, blocking collectives: none -> 88.4 us  [a2a(): return lax.all_to_all(parts, 'seq', 0, 0, tiled=True)]
    all_to_all x8 -> x7, waiting for transfers between devices: 152 us -> 67.6 us  [a2a(): return lax.all_to_all(parts, 'seq', 0, 0, tiled=True)]
    unnamed x466 -> x390, local copies, waits for them, and re-layouts: 109 us -> 32.4 us
    ppermute x28 -> x14, waiting for transfers between devices: 77.7 us -> 135 us  [ring_step(): return lax.ppermute(block, 'seq', pairs)]
    ppermute x28 -> x14, starting transfers between devices: 52.8 us -> 13 us  [ring_step(): return lax.ppermute(block, 'seq', pairs)]
    optimization_barrier x3 -> x0, local copies, waits for them, and re-layouts: 23.4 us -> none  [fence(): return lax.optimization_barrier(values)]
  transfers between devices with their start and end apart: 86 -> 78, of which waited for: 32 -> 35; matrix products, arithmetic and copies ran while one was open for 44% -> 22% of each run, Pallas kernels for 0% -> 11%
where the time goes in v3:
time: 1080 us; the launch traced here: 1070 us
  waiting for transfers between devices  405 us (38%)
  starting transfers between devices  130 us (12%)
  other arithmetic  124 us (11%)
  local copies, waits for them, and re-layouts  122 us (11%)
  Pallas kernels  119 us (11%)
  blocking collectives  88.4 us (8%)
  matrix products  51.2 us (5%)
  between operations  33.7 us (3%)
    ppermute x48, waiting for transfers between devices, shift(): lax.ppermute(block, axis, [(i, (i + distance) % count) for i in range(cou...  173 us
    ppermute x14, waiting for transfers between devices, ring_step(): return lax.ppermute(block, 'seq', pairs)  135 us
    pallas_call x5, Pallas kernels, row_kernel(): pl.pallas_call(body, grid_spec=pltpu.PrefetchScalarGridSpec(num_scalar_pr...  119 us
    all_to_all x1, blocking collectives, a2a(): return lax.all_to_all(parts, 'seq', 0, 0, tiled=True)  88.4 us
    ppermute x48, starting transfers between devices, shift(): lax.ppermute(block, axis, [(i, (i + distance) % count) for i in range(cou...  73.5 us
    all_to_all x7, waiting for transfers between devices, a2a(): return lax.all_to_all(parts, 'seq', 0, 0, tiled=True)  67.6 us
    all_to_all x7, starting transfers between devices, a2a(): return lax.all_to_all(parts, 'seq', 0, 0, tiled=True)  39.7 us
    dot_general x22, matrix products, dot(): lax.dot_general(left, right, (((left_dim,), (right_dim,)), ((), ())), pre...  38.8 us
  transfers between devices with their start and end apart: 78, of which 35 were waited for; matrix products, arithmetic and copies ran while one was open for 22% of the time, Pallas kernels for 11%

profile of v3, /device:TPU:1, one launch (start us, length us, event | category | flops | bytes accessed | tf_op | source)
XLA Modules:
  0.0 1072.9 jit_solution(5106037137960893147)
XLA Ops:
  12.0 88.4 %all_to_all.40 = bf16[8,256,512]{2,1,0:T(8,128)(2,1)} all-to-all(bf16[8,256,512]{2,1,0:T(8,128)(2,1)S(1)} %bitcast.630), channel_id=1, replica_groups=mesh['seq'=8,'mp'=2,'expert'=2] {'seq'}, dimensions={0} | all-to-all | bytes 4194304 | tf_op jit(solution)/shard_map/all_to_all | solution.py:183
  100.4 7.6 collective-permute-start
  126.9 4.3 collective-permute-done.1
  137.3 8.4 collective-permute-done.3
  146.4 4.9 all-to-all-start.1
  174.6 28.4 %collective-permute-done.6.refs_10_.refs_1_ = bf16[2048,512]{1,0:T(8,128)(2,1)} collective-permute-done((bf16[2048,512]{1,0:T(8,128)(2,1)}, bf16[2048,512]{1,0:T(8,128)(2,1)}, u32[]{:S(2)}, u32[]{:S(2)}) %collective-permute-start.6) | collective-permute-done | bytes 2097184 | tf_op jit(solution)/shard_map/ppermute | solution.py:44
  203.0 21.3 %all-to-all-done.1 = bf16[8,256,512]{2,1,0:T(8,128)(2,1)} async-done(((bf16[8,256,512]{2,1,0:T(8,128)(2,1)}), bf16[8,256,512]{2,1,0:T(8,128)(2,1)}, u32[]{:S(2)}, u32[]{:S(2)}) %all-to-all-start.1) | async-done | bytes 2097184 | tf_op jit(solution)/shard_map/all_to_all | solution.py:183
  233.0 4.2 reshape.998
  243.5 4.4 all-to-all-start.2
  251.9 19.3 %collective-permute-done.7.refs_14_.refs_5_ = bf16[2048,512]{1,0:T(8,128)(2,1)} collective-permute-done((bf16[2048,512]{1,0:T(8,128)(2,1)}, bf16[2048,512]{1,0:T(8,128)(2,1)}, u32[]{:S(2)}, u32[]{:S(2)}) %collective-permute-start.7) | collective-permute-done | bytes 2097184 | tf_op jit(solution)/shard_map/ppermute | solution.py:44
  282.9 14.2 %collective-permute-done.10 = bf16[160,2048]{1,0:T(8,128)(2,1)} collective-permute-done((bf16[160,2048]{1,0:T(8,128)(2,1)S(1)}, bf16[160,2048]{1,0:T(8,128)(2,1)}, u32[]{:S(2)}, u32[]{:S(2)}) %collective-permute-start.10) | collective-permute-done | bytes 655392 | tf_op jit(solution)/shard_map/ppermute | solution.py:44
  299.9 16.7 %all-to-all-done.2 = bf16[8,512,256]{2,1,0:T(8,128)(2,1)} async-done(((bf16[8,512,256]{2,1,0:T(8,128)(2,1)}), bf16[8,512,256]{2,1,0:T(8,128)(2,1)}, u32[]{:S(2)}, u32[]{:S(2)}) %all-to-all-start.2) | async-done | bytes 2097184 | tf_op jit(solution)/shard_map/all_to_all | solution.py:183
  324.9 46.2 %collective-permute-done.11.refs_1_ = bf16[160,2048]{1,0:T(8,128)(2,1)S(1)} collective-permute-done((bf16[160,2048]{1,0:T(8,128)(2,1)S(1)}, bf16[160,2048]{1,0:T(8,128)(2,1)S(1)}, u32[]{:S(2)}, u32[]{:S(2)}) %collective-permute-start.11) | collective-permute-done | bytes 655392 | tf_op jit(solution)/shard_map/ppermute | solution.py:49
  372.6 21.0 %collective-permute-done.14.refs_3_ = bf16[160,2048]{1,0:T(8,128)(2,1)S(1)} collective-permute-done((bf16[160,2048]{1,0:T(8,128)(2,1)S(1)}, bf16[160,2048]{1,0:T(8,128)(2,1)S(1)}, u32[]{:S(2)}, u32[]{:S(2)}) %collective-permute-start.14) | collective-permute-done | bytes 655392 | tf_op jit(solution)/shard_map/ppermute | solution.py:49
  396.3 14.3 %collective-permute-done.16.refs_5_ = bf16[160,2048]{1,0:T(8,128)(2,1)} collective-permute-done((bf16[160,2048]{1,0:T(8,128)(2,1)S(1)}, bf16[160,2048]{1,0:T(8,128)(2,1)}, u32[]{:S(2)}, u32[]{:S(2)}) %collective-permute-start.16) | collective-permute-done | bytes 655392 | tf_op jit(solution)/shard_map/ppermute | solution.py:49
  418.8 10.1 collective-permute-done.20.refs_7_
  428.9 4.7 all-to-all-start.3
  433.6 44.4 %feed_inner.1 = (bf16[1152,2048]{1,0:T(8,128)(2,1)}, bf16[1152,2048]{1,0:T(8,128)(2,1)}, bf16[1152,2048]{1,0:T(8,128)(2,1)}, bf16[1152,2048]{1,0:T(8,128)(2,1)},...) custom-call(s32[8]{0:T(128)} %gather_fusion.1, bf16[160,2048]{1,0:T(8,128)(2,1)} %copy-done.78, ...), custom_call_target="tpu_custom_call" | custom-call | flops 28991029248 | bytes 60293120 | tf_op jit(solution)/shard_map/feed_inner/pallas_call | solution.py:282
  479.3 14.4 %convolution_convert_fusion = bf16[2048,2048]{1,0:T(8,128)(2,1)S(1)} fusion(bf16[1152,2048]{1,0:T(8,128)(2,1)} %get-tuple-element.200.mid_ref, bf16[1152,2048]{1,0:T(8,128)(2,1)} %get-tuple-element.194), kind=kOutput, calls=%fused_computation.4 | convolution fusion | flops 9667870720 | bytes 17825792 | tf_op jit(solution)/shard_map/dot_general | solution.py:24
  517.0 15.3 %feed_down.1 = bf16[1152,2048]{1,0:T(8,128)(2,1)} custom-call(bf16[1152,2048]{1,0:T(8,128)(2,1)} %get-tuple-element.200.mid_ref, bf16[512,2048]{1,0:T(8,128)(2,1)} %bitcast.681, bf16[512,2048]{1,0:T(8,128)(2,1)} %collective-permute-done.18.refs_18_.refs_1_, bf16[512,2048]{1,0:T(8,128)(2,1)} %copy-done.174, ...), custom_call_target="tpu_custom_call" | custom-call | flops 9663676416 | bytes 17825792 | tf_op jit(solution)/shard_map/feed_down/pallas_call | solution.py:282
  532.3 3.9 add_convert_fusion.7
  569.4 16.2 %feed_grads.2 = (bf16[2048,512]{1,0:T(8,128)(2,1)}, bf16[2048,512]{1,0:T(8,128)(2,1)}, bf16[2048,512]{1,0:T(8,128)(2,1)}, bf16[2048,512]{1,0:T(8,128)(2,1)}) custom-call(bf16[1152,2048]{1,0:T(8,128)(2,1)} %get-tuple-element.205.left_ref, bf16[1152,2048]{1,0:T(8,128)(2,1)} %get-tuple-element.232.right_ref.dg_ref), custom_call_target="tpu_custom_call" | custom-call | flops 9663676416 | bytes 17825792 | tf_op jit(solution)/shard_map/feed_grads/pallas_call | solution.py:282
  585.7 23.4 %collective-permute-done.28 = bf16[512,2048]{1,0:T(8,128)(2,1)} collective-permute-done((bf16[512,2048]{1,0:T(8,128)(2,1)}, bf16[512,2048]{1,0:T(8,128)(2,1)}, u32[]{:S(2)}, u32[]{:S(2)}) %collective-permute-start.28) | collective-permute-done | bytes 2097184 | tf_op jit(solution)/shard_map/ppermute | solution.py:44
  617.3 6.1 all-to-all-start.4
  623.5 15.9 %feed_grads.3 = (bf16[2048,512]{1,0:T(8,128)(2,1)}, bf16[2048,512]{1,0:T(8,128)(2,1)}, bf16[2048,512]{1,0:T(8,128)(2,1)}, bf16[2048,512]{1,0:T(8,128)(2,1)}) custom-call(bf16[1152,2048]{1,0:T(8,128)(2,1)} %get-tuple-element.205.left_ref, bf16[1152,2048]{1,0:T(8,128)(2,1)} %get-tuple-element.233.right_ref.du_ref), custom_call_target="tpu_custom_call" | custom-call | flops 9663676416 | bytes 17825792 | tf_op jit(solution)/shard_map/feed_grads/pallas_call | solution.py:282
  652.1 27.1 %feed_outer.1 = bf16[1152,2048]{1,0:T(8,128)(2,1)} custom-call(bf16[1152,2048]{1,0:T(8,128)(2,1)} %get-tuple-element.232.right_ref.dg_ref, bf16[1152,2048]{1,0:T(8,128)(2,1)} %get-tuple-element.233.right_ref.du_ref, bf16[2048,512]{1,0:T(8,128)(2,1)} %bitcast.2.refs_9_.refs_0_, bf16[2048,512]{1,0:T(8,128)(2,1)} %collective-permute-done.6.refs_10_.refs_1_, ...), custom_call_target="tpu_custom_call" | custom-call | flops 19327352832 | bytes 30932992 | tf_op jit(solution)/shard_map/feed_outer/pallas_call | solution.py:282
  697.7 16.2 %collective-permute-done.33 = bf16[2048,512]{1,0:T(8,128)(2,1)} collective-permute-done((bf16[2048,512]{1,0:T(8,128)(2,1)}, bf16[2048,512]{1,0:T(8,128)(2,1)}, u32[]{:S(2)}, u32[]{:S(2)}) %collective-permute-start.33) | collective-permute-done | bytes 2097184 | tf_op jit(solution)/shard_map/ppermute | solution.py:44
  721.6 14.8 %collective-permute-done.38 = bf16[176,2048]{1,0:T(8,128)(2,1)S(1)} collective-permute-done((bf16[176,2048]{1,0:T(8,128)(2,1)}, bf16[176,2048]{1,0:T(8,128)(2,1)S(1)}, u32[]{:S(2)}, u32[]{:S(2)}) %collective-permute-start.38) | collective-permute-done | bytes 720928 | tf_op jit(solution)/shard_map/ppermute | solution.py:49
  738.8 13.5 %collective-permute-done.40 = bf16[176,2048]{1,0:T(8,128)(2,1)S(1)} collective-permute-done((bf16[176,2048]{1,0:T(8,128)(2,1)S(1)}, bf16[176,2048]{1,0:T(8,128)(2,1)S(1)}, u32[]{:S(2)}, u32[]{:S(2)}) %collective-permute-start.40) | collective-permute-done | bytes 720928 | tf_op jit(solution)/shard_map/ppermute | solution.py:49
  755.0 11.8 %collective-permute-done.43 = bf16[2048,512]{1,0:T(8,128)(2,1)S(1)} collective-permute-done((bf16[2048,512]{1,0:T(8,128)(2,1)}, bf16[2048,512]{1,0:T(8,128)(2,1)S(1)}, u32[]{:S(2)}, u32[]{:S(2)}) %collective-permute-start.43) | collective-permute-done | bytes 2097184 | tf_op jit(solution)/shard_map/ppermute | solution.py:44
  770.4 13.2 %collective-permute-done.44 = bf16[176,2048]{1,0:T(8,128)(2,1)S(1)} collective-permute-done((bf16[176,2048]{1,0:T(8,128)(2,1)S(1)}, bf16[176,2048]{1,0:T(8,128)(2,1)S(1)}, u32[]{:S(2)}, u32[]{:S(2)}) %collective-permute-start.44) | collective-permute-done | bytes 720928 | tf_op jit(solution)/shard_map/ppermute | solution.py:49
  790.1 5.3 all-to-all-start.5
  795.4 5.7 collective-permute-done.47
  802.4 6.0 collective-permute-start.48
  821.3 5.5 all-to-all-start.6
  850.6 4.4 collective-permute-start.51
  857.3 6.5 collective-permute-done.51
  863.8 24.0 %all-to-all-done.6 = bf16[8,256,512]{2,1,0:T(8,128)(2,1)} async-done(((bf16[8,256,512]{2,1,0:T(8,128)(2,1)}), bf16[8,256,512]{2,1,0:T(8,128)(2,1)}, u32[]{:S(2)}, u32[]{:S(2)}) %all-to-all-start.6) | async-done | bytes 2097184 | tf_op jit(solution)/shard_map/all_to_all | solution.py:183
  894.5 10.0 collective-permute-start.52
  905.4 8.8 all-to-all-start.7
  917.5 4.3 collective-permute-done.53
  928.8 4.2 bitcast_convert_fusion.2
  946.5 9.5 collective-permute-done.55
  958.7 8.8 reduce-scatter.6.cloned.1.call-done
  969.4 5.6 all-to-all-done.7
  1003.3 3.8 collective-permute-done.56
  1010.9 10.4 collective-permute-done.45
  1037.0 16.8 %reduce-scatter.8.cloned.1.call-done = bf16[1,384,640]{2,1,0:T(8,128)(2,1)} async-done(((bf16[8,384,640]{2,1,0:T(8,128)(2,1)}), bf16[1,384,640]{2,1,0:T(8,128)(2,1)}) %reduce-scatter.8.cloned.1.call-update) | async-done | bytes 491536 | tf_op jit(solution)/shard_map/reduce_scatter | solution.py:714
  (805 shorter events, 345.1 us)
Async XLA Ops:
  7.2 109.8 %all-gather.7.cloned.1.call-start = ((), (), s32[]{:S(2)}) async-start(), calls=%async_computation.14 | async-start | bytes 4608000 | tf_op jit(solution)/shard_map/all_gather | solution.py:499
  11.7 214.8 %all-gather.9.cloned.1.call-start = ((), (), s32[]{:S(2)}) async-start(), calls=%async_computation.15 | async-start | bytes 3538944 | tf_op jit(solution)/shard_map/all_gather | solution.py:503
  146.4 77.9 %all-to-all-start.1 = ((bf16[8,256,512]{2,1,0:T(8,128)(2,1)}), bf16[8,256,512]{2,1,0:T(8,128)(2,1)}, u32[]{:S(2)}, u32[]{:S(2)}) async-start(bf16[8,256,512]{2,1,0:T(8,128)(2,1)} %bitcast.628), calls=%async_computation.1 | async-start | bytes 4194304 | tf_op jit(solution)/shard_map/all_to_all | solution.py:183
  155.8 47.3 %collective-permute-start.6 = (bf16[2048,512]{1,0:T(8,128)(2,1)}, bf16[2048,512]{1,0:T(8,128)(2,1)}, u32[]{:S(2)}, u32[]{:S(2)}) collective-permute-start(bf16[2048,512]{1,0:T(8,128)(2,1)} %bitcast.2.refs_9_.refs_0_), channel_id=1, source_target_pairs={{0,2},{2,0},{1,3},{3,1},{4,6},{6,4},{5,7},{7,5},{8,10},{10,8},{9,1... | collective-permute-start | bytes 6291464 | tf_op jit(solution)/shard_map/ppermute | solution.py:44
  224.3 46.8 %collective-permute-start.7 = (bf16[2048,512]{1,0:T(8,128)(2,1)}, bf16[2048,512]{1,0:T(8,128)(2,1)}, u32[]{:S(2)}, u32[]{:S(2)}) collective-permute-start(bf16[2048,512]{1,0:T(8,128)(2,1)} %bitcast.39.refs_13_.refs_4_), channel_id=1, source_target_pairs={{0,2},{2,0},{1,3},{3,1},{4,6},{6,4},{5,7},{7,5},{8,10},{10,8},{9,1... | collective-permute-start | bytes 6291464 | tf_op jit(solution)/shard_map/ppermute | solution.py:44
  225.5 45.6 %collective-permute-start.8 = (bf16[2048,512]{1,0:T(8,128)(2,1)}, bf16[2048,512]{1,0:T(8,128)(2,1)}, u32[]{:S(2)}, u32[]{:S(2)}) collective-permute-start(bf16[2048,512]{1,0:T(8,128)(2,1)} %bitcast.39.refs_13_.refs_4_), channel_id=1, source_target_pairs={{0,1},{1,0},{2,3},{3,2},{4,5},{5,4},{6,7},{7,6},{8,9},{9,8},{10,11... | collective-permute-start | bytes 6291464 | tf_op jit(solution)/shard_map/ppermute | solution.py:44
  243.5 73.1 %all-to-all-start.2 = ((bf16[8,512,256]{2,1,0:T(8,128)(2,1)}), bf16[8,512,256]{2,1,0:T(8,128)(2,1)}, u32[]{:S(2)}, u32[]{:S(2)}) async-start(bf16[8,512,256]{2,1,0:T(8,128)(2,1)} %bitcast.677), calls=%async_computation.2 | async-start | bytes 4194304 | tf_op jit(solution)/shard_map/all_to_all | solution.py:183
  247.9 170.9 %all-gather.11.cloned.1.call-start = ((), (), s32[]{:S(2)}) async-start(), calls=%async_computation.16 | async-start | bytes 5898240 | tf_op jit(solution)/shard_map/all_gather | solution.py:532
  282.3 42.6 %collective-permute-start.13 = (bf16[2048,512]{1,0:T(8,128)(2,1)}, bf16[2048,512]{1,0:T(8,128)(2,1)}, u32[]{:S(2)}, u32[]{:S(2)}) collective-permute-start(bf16[2048,512]{1,0:T(8,128)(2,1)} %collective-permute-done.7.refs_14_.refs_5_), channel_id=1, source_target_pairs={{0,1},{1,0},{2,3},{3,2},{4,5},{5,4},{6,7},{7,6},{8,9},{9,8},{10,11... | collective-permute-start | bytes 6291464 | tf_op jit(solution)/shard_map/ppermute | solution.py:44
  318.5 92.4 %collective-permute-start.18 = (bf16[512,2048]{1,0:T(8,128)(2,1)S(1)}, bf16[512,2048]{1,0:T(8,128)(2,1)}, u32[]{:S(2)}, u32[]{:S(2)}) collective-permute-start(bf16[512,2048]{1,0:T(8,128)(2,1)S(1)} %bitcast.678), channel_id=1, source_target_pairs={{0,2},{2,0},{1,3},{3,1},{4,6},{6,4},{5,7},{7,5},{8,10},{10,8},{9,1... | collective-permute-start | bytes 6291464 | tf_op jit(solution)/shard_map/ppermute | solution.py:44
  318.8 92.1 %collective-permute-start.19 = (bf16[512,2048]{1,0:T(8,128)(2,1)S(1)}, bf16[512,2048]{1,0:T(8,128)(2,1)S(1)}, u32[]{:S(2)}, u32[]{:S(2)}) collective-permute-start(bf16[512,2048]{1,0:T(8,128)(2,1)S(1)} %bitcast.679), channel_id=1, source_target_pairs={{0,1},{1,0},{2,3},{3,2},{4,5},{5,4},{6,7},{7,6},{8,9},{9,8},{10,11... | collective-permute-start | bytes 6291464 | tf_op jit(solution)/shard_map/ppermute | solution.py:44
  323.4 47.7 %collective-permute-start.11 = (bf16[160,2048]{1,0:T(8,128)(2,1)S(1)}, bf16[160,2048]{1,0:T(8,128)(2,1)S(1)}, u32[]{:S(2)}, u32[]{:S(2)}) collective-permute-start(bf16[160,2048]{1,0:T(8,128)(2,1)S(1)} %maximum_maximum_fusion.11.refs_0_), channel_id=1, source_target_pairs={{0,4},{8,0},{16,8},{24,16},{28,24},{20,28},{12,20},{4,12},{1,5},{9... | collective-permute-start | bytes 1966088 | tf_op jit(solution)/shard_map/ppermute | solution.py:49
  324.6 46.5 %collective-permute-start.12 = (bf16[160,2048]{1,0:T(8,128)(2,1)S(1)}, bf16[160,2048]{1,0:T(8,128)(2,1)S(1)}, u32[]{:S(2)}, u32[]{:S(2)}) collective-permute-start(bf16[160,2048]{1,0:T(8,128)(2,1)S(1)} %maximum_maximum_fusion.11.refs_0_), channel_id=1, source_target_pairs={{0,8},{8,16},{16,24},{24,28},{28,20},{20,12},{12,4},{4,0},{1,9},{9... | collective-permute-start | bytes 1966088 | tf_op jit(solution)/shard_map/ppermute | solution.py:49
  371.0 22.5 %collective-permute-start.14 = (bf16[160,2048]{1,0:T(8,128)(2,1)S(1)}, bf16[160,2048]{1,0:T(8,128)(2,1)S(1)}, u32[]{:S(2)}, u32[]{:S(2)}) collective-permute-start(bf16[160,2048]{1,0:T(8,128)(2,1)S(1)} %collective-permute-done.11.refs_1_), channel_id=1, source_target_pairs={{0,4},{8,0},{16,8},{24,16},{28,24},{20,28},{12,20},{4,12},{1,5},{9... | collective-permute-start | bytes 1966088 | tf_op jit(solution)/shard_map/ppermute | solution.py:49
  371.1 23.0 %collective-permute-start.15 = (bf16[160,2048]{1,0:T(8,128)(2,1)S(1)}, bf16[160,2048]{1,0:T(8,128)(2,1)S(1)}, u32[]{:S(2)}, u32[]{:S(2)}) collective-permute-start(bf16[160,2048]{1,0:T(8,128)(2,1)S(1)} %collective-permute-done.12.refs_2_), channel_id=1, source_target_pairs={{0,8},{8,16},{16,24},{24,28},{28,20},{20,12},{12,4},{4,0},{1,9},{9... | collective-permute-start | bytes 1966088 | tf_op jit(solution)/shard_map/ppermute | solution.py:49
  394.1 16.5 %collective-permute-start.16 = (bf16[160,2048]{1,0:T(8,128)(2,1)S(1)}, bf16[160,2048]{1,0:T(8,128)(2,1)}, u32[]{:S(2)}, u32[]{:S(2)}) collective-permute-start(bf16[160,2048]{1,0:T(8,128)(2,1)S(1)} %collective-permute-done.14.refs_3_), channel_id=1, source_target_pairs={{0,4},{8,0},{16,8},{24,16},{28,24},{20,28},{12,20},{4,12},{1,5},{9... | collective-permute-start | bytes 1966088 | tf_op jit(solution)/shard_map/ppermute | solution.py:49
  394.7 16.2 %collective-permute-start.17 = (bf16[160,2048]{1,0:T(8,128)(2,1)S(1)}, bf16[160,2048]{1,0:T(8,128)(2,1)S(1)}, u32[]{:S(2)}, u32[]{:S(2)}) collective-permute-start(bf16[160,2048]{1,0:T(8,128)(2,1)S(1)} %collective-permute-done.15.refs_4_), channel_id=1, source_target_pairs={{0,8},{8,16},{16,24},{24,28},{28,20},{20,12},{12,4},{4,0},{1,9},{9... | collective-permute-start | bytes 1966088 | tf_op jit(solution)/shard_map/ppermute | solution.py:49
  411.0 17.9 %collective-permute-start.21 = (bf16[512,2048]{1,0:T(8,128)(2,1)}, bf16[512,2048]{1,0:T(8,128)(2,1)}, u32[]{:S(2)}, u32[]{:S(2)}) collective-permute-start(bf16[512,2048]{1,0:T(8,128)(2,1)} %collective-permute-done.18.refs_18_.refs_1_), channel_id=1, source_target_pairs={{0,1},{1,0},{2,3},{3,2},{4,5},{5,4},{6,7},{7,6},{8,9},{9,8},{10,11... | collective-permute-start | bytes 6291464 | tf_op jit(solution)/shard_map/ppermute | solution.py:44
  412.5 21.1 %collective-permute-start.22 = (bf16[2048,512]{1,0:T(8,128)(2,1)}, bf16[2048,512]{1,0:T(8,128)(2,1)}, u32[]{:S(2)}, u32[]{:S(2)}) collective-permute-start(bf16[2048,512]{1,0:T(8,128)(2,1)} %collective-permute-done.6.refs_10_.refs_1_), channel_id=1, source_target_pairs={{0,1},{1,0},{2,3},{3,2},{4,5},{5,4},{6,7},{7,6},{8,9},{9,8},{10,11... | collective-permute-start | bytes 6291464 | tf_op jit(solution)/shard_map/ppermute | solution.py:44
  412.6 16.3 %collective-permute-start.20 = (bf16[160,2048]{1,0:T(8,128)(2,1)}, bf16[160,2048]{1,0:T(8,128)(2,1)}, u32[]{:S(2)}, u32[]{:S(2)}) collective-permute-start(bf16[160,2048]{1,0:T(8,128)(2,1)} %collective-permute-done.16.refs_5_), channel_id=1, source_target_pairs={{0,4},{8,0},{16,8},{24,16},{28,24},{20,28},{12,20},{4,12},{1,5},{9... | collective-permute-start | bytes 1966088 | tf_op jit(solution)/shard_map/ppermute | solution.py:49
  428.9 49.2 %all-to-all-start.3 = ((bf16[8,384,128]{1,2,0:T(8,128)(2,1)}), bf16[8,384,128]{1,2,0:T(8,128)(2,1)S(1)}, u32[]{:S(2)}, u32[]{:S(2)}) async-start(bf16[8,384,128]{1,2,0:T(8,128)(2,1)} %pad_maximum_fusion.4), calls=%async_computation.3 | async-start | bytes 1572864 | tf_op jit(solution)/shard_map/all_to_all | solution.py:183
  433.6 283.9 %reduce-scatter.4.cloned.1.call-start = ((), (), s32[]{:S(2)}) async-start(), calls=%async_computation.11 | async-start | bytes 5308416 | tf_op jit(solution)/shard_map/reduce_scatter | solution.py:589
  478.1 18.5 %collective-permute-start.23 = (bf16[8,384,128]{1,2,0:T(8,128)(2,1)S(1)}, bf16[8,384,128]{1,2,0:T(8,128)(2,1)S(1)}, u32[]{:S(2)}, u32[]{:S(2)}) collective-permute-start(bf16[8,384,128]{1,2,0:T(8,128)(2,1)S(1)} %all-to-all-done.3), channel_id=1, source_target_pairs={{0,2},{2,0},{1,3},{3,1},{4,6},{6,4},{5,7},{7,5},{8,10},{10,8},{9,1... | collective-permute-start | bytes 2359304 | tf_op jit(solution)/shard_map/ppermute | solution.py:44
  497.4 34.9 %collective-permute-start.25 = (bf16[512,2048]{1,0:T(8,128)(2,1)}, bf16[512,2048]{1,0:T(8,128)(2,1)}, u32[]{:S(2)}, u32[]{:S(2)}) collective-permute-start(bf16[512,2048]{1,0:T(8,128)(2,1)} %get-tuple-element.199), channel_id=1, source_target_pairs={{0,1},{1,0},{2,3},{3,2},{4,5},{5,4},{6,7},{7,6},{8,9},{9,8},{10,11... | collective-permute-start | bytes 6291464 | tf_op jit(solution)/shard_map/ppermute | solution.py:44
  500.2 36.0 %collective-permute-start.24 = (bf16[512,2048]{1,0:T(8,128)(2,1)}, bf16[512,2048]{1,0:T(8,128)(2,1)}, u32[]{:S(2)}, u32[]{:S(2)}) collective-permute-start(bf16[512,2048]{1,0:T(8,128)(2,1)} %get-tuple-element.197), channel_id=1, source_target_pairs={{0,1},{1,0},{2,3},{3,2},{4,5},{5,4},{6,7},{7,6},{8,9},{9,8},{10,11... | collective-permute-start | bytes 6291464 | tf_op jit(solution)/shard_map/ppermute | solution.py:44
  516.3 22.2 %collective-permute-start.26 = (bf16[8,384,128]{1,2,0:T(8,128)(2,1)S(1)}, bf16[8,384,128]{1,2,0:T(8,128)(2,1)}, u32[]{:S(2)}, u32[]{:S(2)}) collective-permute-start(bf16[8,384,128]{1,2,0:T(8,128)(2,1)S(1)} %all-to-all-done.3), channel_id=1, source_target_pairs={{0,1},{1,0},{2,3},{3,2},{4,5},{5,4},{6,7},{7,6},{8,9},{9,8},{10,11... | collective-permute-start | bytes 2359304 | tf_op jit(solution)/shard_map/ppermute | solution.py:44
  516.9 21.6 %collective-permute-start.27 = (bf16[8,384,128]{1,2,0:T(8,128)(2,1)}, bf16[8,384,128]{1,2,0:T(8,128)(2,1)}, u32[]{:S(2)}, u32[]{:S(2)}) collective-permute-start(bf16[8,384,128]{1,2,0:T(8,128)(2,1)} %copy-done.72), channel_id=1, source_target_pairs={{0,1},{1,0},{2,3},{3,2},{4,5},{5,4},{6,7},{7,6},{8,9},{9,8},{10,11... | collective-permute-start | bytes 2359304 | tf_op jit(solution)/shard_map/ppermute | solution.py:44
  561.9 47.2 %collective-permute-start.28 = (bf16[512,2048]{1,0:T(8,128)(2,1)}, bf16[512,2048]{1,0:T(8,128)(2,1)}, u32[]{:S(2)}, u32[]{:S(2)}) collective-permute-start(bf16[512,2048]{1,0:T(8,128)(2,1)} %add_convert_fusion.7), channel_id=1, source_target_pairs={{0,2},{2,0},{1,3},{3,1},{4,6},{6,4},{5,7},{7,5},{8,10},{10,8},{9,1... | collective-permute-start | bytes 6291464 | tf_op jit(solution)/shard_map/ppermute | solution.py:44
  611.5 32.6 %collective-permute-start.30 = (bf16[2048,512]{1,0:T(8,128)(2,1)}, bf16[2048,512]{1,0:T(8,128)(2,1)}, u32[]{:S(2)}, u32[]{:S(2)}) collective-permute-start(bf16[2048,512]{1,0:T(8,128)(2,1)} %get-tuple-element.221), channel_id=1, source_target_pairs={{0,1},{1,0},{2,3},{3,2},{4,5},{5,4},{6,7},{7,6},{8,9},{9,8},{10,11... | collective-permute-start | bytes 6291464 | tf_op jit(solution)/shard_map/ppermute | solution.py:44
  614.0 33.7 %collective-permute-start.29 = (bf16[2048,512]{1,0:T(8,128)(2,1)}, bf16[2048,512]{1,0:T(8,128)(2,1)}, u32[]{:S(2)}, u32[]{:S(2)}) collective-permute-start(bf16[2048,512]{1,0:T(8,128)(2,1)} %get-tuple-element.219), channel_id=1, source_target_pairs={{0,1},{1,0},{2,3},{3,2},{4,5},{5,4},{6,7},{7,6},{8,9},{9,8},{10,11... | collective-permute-start | bytes 6291464 | tf_op jit(solution)/shard_map/ppermute | solution.py:44
  615.3 24.1 %collective-permute-start.32 = (bf16[8,384,128]{2,1,0:T(8,128)(2,1)S(1)}, bf16[8,384,128]{2,1,0:T(8,128)(2,1)}, u32[]{:S(2)}, u32[]{:S(2)}) collective-permute-start(bf16[8,384,128]{2,1,0:T(8,128)(2,1)S(1)} %copy-done.74), channel_id=1, source_target_pairs={{0,1},{1,0},{2,3},{3,2},{4,5},{5,4},{6,7},{7,6},{8,9},{9,8},{10,11... | collective-permute-start | bytes 2359304 | tf_op jit(solution)/shard_map/ppermute | solution.py:44
  615.4 26.3 %collective-permute-start.31 = (bf16[8,384,128]{2,1,0:T(8,128)(2,1)S(1)}, bf16[8,384,128]{2,1,0:T(8,128)(2,1)}, u32[]{:S(2)}, u32[]{:S(2)}) collective-permute-start(bf16[8,384,128]{2,1,0:T(8,128)(2,1)S(1)} %copy-done.73), channel_id=1, source_target_pairs={{0,1},{1,0},{2,3},{3,2},{4,5},{5,4},{6,7},{7,6},{8,9},{9,8},{10,11... | collective-permute-start | bytes 2359304 | tf_op jit(solution)/shard_map/ppermute | solution.py:44
  617.3 102.5 %all-to-all-start.4 = ((bf16[8,512,256]{2,1,0:T(8,128)(2,1)}), bf16[8,512,256]{2,1,0:T(8,128)(2,1)}, u32[]{:S(2)}, u32[]{:S(2)}) async-start(bf16[8,512,256]{2,1,0:T(8,128)(2,1)} %bitcast.590), calls=%async_computation.4 | async-start | bytes 4194304 | tf_op jit(solution)/shard_map/all_to_all | solution.py:183
  649.9 37.9 %collective-permute-start.36 = (bf16[8,384,128]{2,1,0:T(8,128)(2,1)}, bf16[8,384,128]{2,1,0:T(8,128)(2,1)}, u32[]{:S(2)}, u32[]{:S(2)}) collective-permute-start(bf16[8,384,128]{2,1,0:T(8,128)(2,1)} %add_convert_fusion.10), channel_id=1, source_target_pairs={{0,2},{2,0},{1,3},{3,1},{4,6},{6,4},{5,7},{7,5},{8,10},{10,8},{9,1... | collective-permute-start | bytes 2359304 | tf_op jit(solution)/shard_map/ppermute | solution.py:44
  650.3 40.2 %collective-permute-start.35 = (bf16[2048,512]{1,0:T(8,128)(2,1)}, bf16[2048,512]{1,0:T(8,128)(2,1)}, u32[]{:S(2)}, u32[]{:S(2)}) collective-permute-start(bf16[2048,512]{1,0:T(8,128)(2,1)} %get-tuple-element.240), channel_id=1, source_target_pairs={{0,1},{1,0},{2,3},{3,2},{4,5},{5,4},{6,7},{7,6},{8,9},{9,8},{10,11... | collective-permute-start | bytes 6291464 | tf_op jit(solution)/shard_map/ppermute | solution.py:44
  650.9 43.3 %collective-permute-start.34 = (bf16[2048,512]{1,0:T(8,128)(2,1)}, bf16[2048,512]{1,0:T(8,128)(2,1)}, u32[]{:S(2)}, u32[]{:S(2)}) collective-permute-start(bf16[2048,512]{1,0:T(8,128)(2,1)} %get-tuple-element.238), channel_id=1, source_target_pairs={{0,1},{1,0},{2,3},{3,2},{4,5},{5,4},{6,7},{7,6},{8,9},{9,8},{10,11... | collective-permute-start | bytes 6291464 | tf_op jit(solution)/shard_map/ppermute | solution.py:44
  650.9 63.1 %collective-permute-start.33 = (bf16[2048,512]{1,0:T(8,128)(2,1)}, bf16[2048,512]{1,0:T(8,128)(2,1)}, u32[]{:S(2)}, u32[]{:S(2)}) collective-permute-start(bf16[2048,512]{1,0:T(8,128)(2,1)} %add_convert_fusion.4), channel_id=1, source_target_pairs={{0,2},{2,0},{1,3},{3,1},{4,6},{6,4},{5,7},{7,5},{8,10},{10,8},{9,1... | collective-permute-start | bytes 6291464 | tf_op jit(solution)/shard_map/ppermute | solution.py:44
  719.8 16.6 %collective-permute-start.38 = (bf16[176,2048]{1,0:T(8,128)(2,1)}, bf16[176,2048]{1,0:T(8,128)(2,1)S(1)}, u32[]{:S(2)}, u32[]{:S(2)}) collective-permute-start(bf16[176,2048]{1,0:T(8,128)(2,1)} %maximum_maximum_fusion.8), channel_id=1, source_target_pairs={{0,4},{8,0},{16,8},{24,16},{28,24},{20,28},{12,20},{4,12},{1,5},{9... | collective-permute-start | bytes 2162696 | tf_op jit(solution)/shard_map/ppermute | solution.py:49
  721.3 45.6 %collective-permute-start.43 = (bf16[2048,512]{1,0:T(8,128)(2,1)}, bf16[2048,512]{1,0:T(8,128)(2,1)S(1)}, u32[]{:S(2)}, u32[]{:S(2)}) collective-permute-start(bf16[2048,512]{1,0:T(8,128)(2,1)} %add_convert_fusion.1), channel_id=1, source_target_pairs={{0,2},{2,0},{1,3},{3,1},{4,6},{6,4},{5,7},{7,5},{8,10},{10,8},{9,1... | collective-permute-start | bytes 6291464 | tf_op jit(solution)/shard_map/ppermute | solution.py:44
  790.1 24.3 %all-to-all-start.5 = ((bf16[8,384,128]{2,1,0:T(8,128)(2,1)}), bf16[8,384,128]{2,1,0:T(8,128)(2,1)S(1)}, u32[]{:S(2)}, u32[]{:S(2)}) async-start(bf16[8,384,128]{2,1,0:T(8,128)(2,1)} %add_convert_fusion.9), calls=%async_computation.6 | async-start | bytes 1572864 | tf_op jit(solution)/shard_map/all_to_all | solution.py:183
  821.3 66.6 %all-to-all-start.6 = ((bf16[8,256,512]{2,1,0:T(8,128)(2,1)}), bf16[8,256,512]{2,1,0:T(8,128)(2,1)}, u32[]{:S(2)}, u32[]{:S(2)}) async-start(bf16[8,256,512]{2,1,0:T(8,128)(2,1)} %bitcast.166), calls=%async_computation.7 | async-start | bytes 4194304 | tf_op jit(solution)/shard_map/all_to_all | solution.py:183
  826.8 140.7 %reduce-scatter.6.cloned.1.call-start = ((), (), s32[]{:S(2)}) async-start(), calls=%async_computation.12 | async-start | bytes 3538944 | tf_op jit(solution)/shard_map/reduce_scatter | solution.py:658
  894.5 20.3 %collective-permute-start.52 = (bf16[2,560,128]{2,1,0:T(8,128)(2,1)}, bf16[2,560,128]{2,1,0:T(8,128)(2,1)}, u32[]{:S(2)}, u32[]{:S(2)}) collective-permute-start(bf16[2,560,128]{2,1,0:T(8,128)(2,1)} %fusion.73), channel_id=1, source_target_pairs={{0,1},{1,0},{2,3},{3,2},{4,5},{5,4},{6,7},{7,6},{8,9},{9,8},{10,11... | collective-permute-start | bytes 860168 | tf_op jit(solution)/shard_map/ppermute | solution.py:44
  905.4 69.6 %all-to-all-start.7 = ((bf16[8,256,512]{2,1,0:T(8,128)(2,1)}), bf16[8,256,512]{2,1,0:T(8,128)(2,1)}, u32[]{:S(2)}, u32[]{:S(2)}) async-start(bf16[8,256,512]{2,1,0:T(8,128)(2,1)} %bitcast.625), calls=%async_computation.8 | async-start | bytes 4194304 | tf_op jit(solution)/shard_map/all_to_all | solution.py:183
  914.2 139.7 %reduce-scatter.8.cloned.1.call-start = ((), (), s32[]{:S(2)}) async-start(), calls=%async_computation.13 | async-start | bytes 4423680 | tf_op jit(solution)/shard_map/reduce_scatter | solution.py:714
  993.3 27.9 %collective-permute-start.45 = (bf16[160,2048]{1,0:T(8,128)(2,1)S(1)}, bf16[160,2048]{1,0:T(8,128)(2,1)S(1)}, u32[]{:S(2)}, u32[]{:S(2)}) collective-permute-start(bf16[160,2048]{1,0:T(8,128)(2,1)S(1)} %get-tuple-element.435), channel_id=1, source_target_pairs={{0,2},{2,0},{1,3},{3,1},{4,6},{6,4},{5,7},{7,5},{8,10},{10,8},{9,1... | collective-permute-start | bytes 1966088 | tf_op jit(solution)/shard_map/ppermute | solution.py:44
  1002.6 27.2 %collective-permute-start.62 = (f32[1,768]{1,0:T(1,128)S(1)}, f32[1,768]{1,0:T(1,128)S(1)}, u32[]{:S(2)}, u32[]{:S(2)}) collective-permute-start(f32[1,768]{1,0:T(1,128)S(1)} %add.517), channel_id=1, source_target_pairs={{0,2},{2,0},{1,3},{3,1},{4,6},{6,4},{5,7},{7,5},{8,10},{10,8},{9,1... | collective-permute-start | bytes 9224 | tf_op jit(solution)/shard_map/ppermute | solution.py:44
  1007.4 23.9 %collective-permute-start.57 = (bf16[2,160,2048]{2,1,0:T(8,128)(2,1)S(1)}, bf16[2,160,2048]{2,1,0:T(8,128)(2,1)S(1)}, u32[]{:S(2)}, u32[]{:S(2)}) collective-permute-start(bf16[2,160,2048]{2,1,0:T(8,128)(2,1)S(1)} %maximum_select_fusion.7), channel_id=1, source_target_pairs={{0,1},{1,0},{2,3},{3,2},{4,5},{5,4},{6,7},{7,6},{8,9},{9,8},{10,11... | collective-permute-start | bytes 3932168 | tf_op jit(solution)/shard_map/ppermute | solution.py:44
  (215 other events, 2869.4 us)
Sparse Core Ops, SparseCore 0:
  11.8 105.1 all-gather.6
  119.7 95.6 all-gather.8
  274.1 112.2 all-gather.10
  562.4 129.1 reduce-scatter.3
  857.4 110.0 reduce-scatter.5
  971.0 82.8 reduce-scatter.7

commit v4 on v3

--- a/solution.py
+++ b/solution.py
@@ -14,6 +14,7 @@
 GELU_B = 0.044715
 TILE = 256
 VMEM_BYTES = 60 * 2**20
+SHARE = 1000
 BF = jnp.bfloat16
 F32 = jnp.float32
 
@@ -290,7 +291,7 @@
         ),
         out_shape=[shape for shape, _ in outs],
         compiler_params=pltpu.CompilerParams(vmem_limit_bytes=VMEM_BYTES),
-        cost_estimate=pl.CostEstimate(flops=flops, transcendentals=0, bytes_accessed=moved),
+        cost_estimate=pl.CostEstimate(flops=flops // SHARE, transcendentals=0, bytes_accessed=moved // SHARE),
         name=name,
     )(*order, *[a for a, _ in ins])
 
@@ -392,6 +393,55 @@
     ins += [(part, column_block(width // 4, TILE)) for part in w_down]
     outs = [(like(rows, depth), column_block(rows, TILE))]
     return row_kernel(body, depth // TILE, ins, outs, 2 * rows * depth * width, "feed_down")[0]
+
+
+def action_weights(part, depth):
+    gate, up = part[:, :depth], part[:, depth : 2 * depth]
+    down = cat([part[k, 2 * depth :] for k in range(part.shape[0])], 1)
+    return gate.reshape(-1, gate.shape[-1]), up.reshape(-1, up.shape[-1]), down
+
+
+def action_grads(normed, cot, mid, d_gate, d_up, depth):
+    gate, up = dot(normed, d_gate, 0, 0).astype(BF), dot(normed, d_up, 0, 0).astype(BF)
+    down = dot(mid, cot, 0, 0).astype(BF)
+    return (
+        gate.reshape(-1, depth, gate.shape[-1]),
+        up.reshape(-1, depth, up.shape[-1]),
+        [down[:, k : k + depth] for k in range(0, down.shape[1], depth)],
+    )
+
+
+def feed_action(normed, cot, parts, depth):
+    def run(normed, cot, parts):
+        grad_rows, y, grads = 0.0, 0.0, []
+        for part in parts:
+            gate, up, down = action_weights(part, depth)
+            mid, d_gate, d_up = feed_back(normed, cot, gate, up, down)
+            grad_rows = grad_rows + dot(d_gate, gate, 1, 1) + dot(d_up, up, 1, 1)
+            y = y + dot(mid, down, 1, 0)
+            grads.append(action_grads(normed, cot, mid, d_gate, d_up, depth))
+        return grad_rows.astype(BF), y.astype(BF), grads
+
+    if not on_ring():
+        grad_rows, y, grads = run(normed, cot, parts)
+        grads = [jnp.concatenate([g, u, jnp.stack(d)], axis=1) for g, u, d in grads]
+        return grad_rows, y, grads
+
+    def body(n_ref, c_ref, *refs):
+        grad_rows, y, grads = run(n_ref[...], c_ref[...], [ref[...] for ref in refs[:4]])
+        refs[4][...], refs[5][...] = grad_rows, y
+        for out_ref, (gate, up, down) in zip(refs[6:], grads):
+            out_ref[:, :depth, :], out_ref[:, depth : 2 * depth, :] = gate, up
+            for k, block in enumerate(down):
+                out_ref[k, 2 * depth :, :] = block
+
+    rows = [normed, cot] + list(parts)
+    ins = [(a, whole_block(a.shape)) for a in rows]
+    outs = [jax.ShapeDtypeStruct(a.shape, BF) for a in rows]
+    outs = [(shape, whole_block(shape.shape)) for shape in outs]
+    flops = 80 * normed.shape[0] * normed.shape[1] * parts[0].shape[-1]
+    out = row_kernel(body, 1, ins, outs, flops, "feed_action")
+    return out[0], out[1], out[2:]
 
 
 def weight_grad(left, right):
@@ -588,27 +638,14 @@
     y_sum = y_sum.reshape(episodes, part_p, -1)
     y_sum = lax.psum_scatter(y_sum, "seq", scatter_dimension=0).astype(F32)
     dwd_p, dwg_p = across_reduce(*dwd_p), quarter_grads(normed2_p, d_gate_p)
-    w_gate_a = cat([join_rows(part[:, :depth_a]) for part in in_action], 1)
-    w_up_a = cat([join_rows(part[:, depth_a : 2 * depth_a]) for part in in_action], 1)
-    w_down_a = cat([join_columns(part[:, 2 * depth_a :]) for part in in_action], 0)
-    mid_a, d_gate_a, d_up_a = feed_back(normed2_a, cots_a, w_gate_a, w_up_a, w_down_a)
-    gn2_a = (dot(d_gate_a, w_gate_a, 1, 1) + dot(d_up_a, w_up_a, 1, 1)).astype(BF)
-    y_a = dot(mid_a, w_down_a, 1, 0).astype(BF)
-    d_action = zip(
-        quarters(weight_grad(normed2_a, d_gate_a), 1),
-        quarters(weight_grad(normed2_a, d_up_a), 1),
-        quarters(weight_grad(mid_a, cots_a), 0),
-    )
-    d_action = [
-        jnp.concatenate([split_rows(g), split_rows(u), split_columns(d)], axis=1)
-        for g, u, d in d_action
-    ]
-    dwd_p, dwg_p, d_gate_p, d_up_p, d_action = fence(dwd_p, dwg_p, d_gate_p, d_up_p, d_action)
-    dwd_p, dwg_p = a2a(split_columns(dwd_p)), pair_reduce_rel(dwg_p)
-    dwu_p, d_action = quarter_grads(normed2_p, d_up_p), pair_reduce_rel(d_action)
-    dwg_p, dwu_p, d_gate_p, d_up_p, d_action = fence(dwg_p, dwu_p, d_gate_p, d_up_p, d_action)
-    dwg_p, dwu_p = across_reduce(*dwg_p), pair_reduce_rel(dwu_p)
-    d_action = across_reduce(*d_action)
+    dwg_p, d_up_p, in_action = fence(dwg_p, d_up_p, in_action)
+    dwg_p, dwu_p = pair_reduce_rel(dwg_p), quarter_grads(normed2_p, d_up_p)
+    gn2_a, y_a, d_action = feed_action(normed2_a, cots_a, in_action, depth_a)
+    dwd_p, dwg_p, dwu_p, d_gate_p, d_up_p, gn2_a, y_a, d_action = fence(
+        dwd_p, dwg_p, dwu_p, d_gate_p, d_up_p, gn2_a, y_a, d_action
+    )
+    dwd_p, dwg_p = a2a(split_columns(dwd_p)), across_reduce(*dwg_p)
+    dwu_p, d_action = pair_reduce_rel(dwu_p), pair_reduce_rel(d_action)
     gn2_p = feed_outer(d_gate_p, d_up_p, w_gate_p, w_up_p).reshape(episodes, part_p, -1)
     gn2_a, y_a = gn2_a.reshape(episodes, part_a, -1), y_a.reshape(episodes, part_a, -1)
     owners = ring_owners() if on_ring() else range(episodes)
@@ -618,7 +655,7 @@
     )
     gn2 = Summed(chunks)
     gn2.hop()
-    dwu_p = across_reduce(*dwu_p)
+    dwu_p, d_action = across_reduce(*dwu_p), across_reduce(*d_action)
     gn2.meet()
     gn2.hop()
     gn2.meet()
@@ -655,6 +692,7 @@
         ],
         axis=2,
     ).transpose(1, 0, 2)
+    dwo, dao_p, dao_a = fence(dwo, dao_p, dao_a)
     dwo = lax.psum_scatter(dwo, "seq", scatter_dimension=0, tiled=False).astype(F32)
     dmix_p, dmix_a = dot(dao_p, w_out_p, 1, 1).astype(BF), dot(dao_a, w_out_a, 1, 1).astype(BF)
     dq_slots, dkv_slots = jax.vmap(attend_backward)(

time: 1080 us -> 1030 us (0.954)
  waiting for transfers between devices: 405 us -> 378 us
  local copies, waits for them, and re-layouts: 122 us -> 103 us
    ppermute x48, waiting for transfers between devices: 173 us -> 153 us  [shift(): lax.ppermute(block, axis, [(i, (i + distance) % count) for i in range(cou...]
    slice x12 -> x0, local copies, waits for them, and re-layouts: 14.7 us -> none  [the longest x4 6.66 us: body(): part[:, 2 * depth_a:]]
    pallas_call x5 -> x6, Pallas kernels: 119 us -> 128 us  [row_kernel(): pl.pallas_call(body, grid_spec=pltpu.PrefetchScalarGridSpec(num_scalar_pr...]
    dot_general x22 -> x13, matrix products: 38.8 us -> 33.8 us  [dot(): lax.dot_general(left, right, (((left_dim,), (right_dim,)), ((), ())), pre...]
    unnamed x390 -> x291, local copies, waits for them, and re-layouts: 32.4 us -> 33.7 us
  transfers between devices with their start and end apart: 78 -> 78, of which waited for: 35 -> 38; matrix products, arithmetic and copies ran while one was open for 22% -> 23% of each run, Pallas kernels for 11% -> 12%
where the time goes in v4:
time: 1030 us
  waiting for transfers between devices  378 us (37%)
  Pallas kernels  128 us (12%)
  other arithmetic  127 us (12%)
  starting transfers between devices  125 us (12%)
  local copies, waits for them, and re-layouts  103 us (10%)
  blocking collectives  88.4 us (9%)
  matrix products  45.3 us (4%)
  between operations  32.9 us (3%)
    ppermute x48, waiting for transfers between devices, shift(): lax.ppermute(block, axis, [(i, (i + distance) % count) for i in range(cou...  153 us
    pallas_call x6, Pallas kernels, row_kernel(): pl.pallas_call(body, grid_spec=pltpu.PrefetchScalarGridSpec(num_scalar_pr...  128 us
    ppermute x14, waiting for transfers between devices, ring_step(): return lax.ppermute(block, 'seq', pairs)  125 us
    all_to_all x1, blocking collectives, a2a(): return lax.all_to_all(parts, 'seq', 0, 0, tiled=True)  88.4 us
    ppermute x48, starting transfers between devices, shift(): lax.ppermute(block, axis, [(i, (i + distance) % count) for i in range(cou...  76.5 us
    all_to_all x7, waiting for transfers between devices, a2a(): return lax.all_to_all(parts, 'seq', 0, 0, tiled=True)  72.9 us
    dot_general x13, matrix products, dot(): lax.dot_general(left, right, (((left_dim,), (right_dim,)), ((), ())), pre...  33.8 us
    unnamed x291, local copies, waits for them, and re-layouts  33.7 us
  transfers between devices with their start and end apart: 78, of which 38 were waited for; matrix products, arithmetic and copies ran while one was open for 23% of the time, Pallas kernels for 12%

profile of v4, /device:TPU:1, one launch (start us, length us, event | category | flops | bytes accessed | tf_op | source)
XLA Modules:
  0.0 1026.3 jit_solution(870488943247062097)
XLA Ops:
  12.0 88.4 %all_to_all.40 = bf16[8,256,512]{2,1,0:T(8,128)(2,1)} all-to-all(bf16[8,256,512]{2,1,0:T(8,128)(2,1)S(1)} %bitcast.559), channel_id=1, replica_groups=mesh['seq'=8,'mp'=2,'expert'=2] {'seq'}, dimensions={0} | all-to-all | bytes 4194304 | tf_op jit(solution)/shard_map/all_to_all | solution.py:184
  100.4 7.6 collective-permute-start
  127.4 4.3 collective-permute-done.1
  137.8 8.4 collective-permute-done.3
  146.8 4.9 all-to-all-start.1
  173.8 29.7 %collective-permute-done.6.refs_10_.refs_1_ = bf16[2048,512]{1,0:T(8,128)(2,1)} collective-permute-done((bf16[2048,512]{1,0:T(8,128)(2,1)}, bf16[2048,512]{1,0:T(8,128)(2,1)}, u32[]{:S(2)}, u32[]{:S(2)}) %collective-permute-start.6) | collective-permute-done | bytes 2097184 | tf_op jit(solution)/shard_map/ppermute | solution.py:45
  203.5 21.0 %all-to-all-done.1 = bf16[8,256,512]{2,1,0:T(8,128)(2,1)} async-done(((bf16[8,256,512]{2,1,0:T(8,128)(2,1)}), bf16[8,256,512]{2,1,0:T(8,128)(2,1)}, u32[]{:S(2)}, u32[]{:S(2)}) %all-to-all-start.1) | async-done | bytes 2097184 | tf_op jit(solution)/shard_map/all_to_all | solution.py:184
  233.0 4.2 reshape.902
  243.5 4.4 all-to-all-start.2
  252.0 19.4 %collective-permute-done.7.refs_14_.refs_5_ = bf16[2048,512]{1,0:T(8,128)(2,1)} collective-permute-done((bf16[2048,512]{1,0:T(8,128)(2,1)}, bf16[2048,512]{1,0:T(8,128)(2,1)}, u32[]{:S(2)}, u32[]{:S(2)}) %collective-permute-start.7) | collective-permute-done | bytes 2097184 | tf_op jit(solution)/shard_map/ppermute | solution.py:45
  283.1 14.2 %collective-permute-done.10 = bf16[160,2048]{1,0:T(8,128)(2,1)} collective-permute-done((bf16[160,2048]{1,0:T(8,128)(2,1)S(1)}, bf16[160,2048]{1,0:T(8,128)(2,1)}, u32[]{:S(2)}, u32[]{:S(2)}) %collective-permute-start.10) | collective-permute-done | bytes 655392 | tf_op jit(solution)/shard_map/ppermute | solution.py:45
  300.0 16.6 %all-to-all-done.2 = bf16[8,512,256]{2,1,0:T(8,128)(2,1)} async-done(((bf16[8,512,256]{2,1,0:T(8,128)(2,1)}), bf16[8,512,256]{2,1,0:T(8,128)(2,1)}, u32[]{:S(2)}, u32[]{:S(2)}) %all-to-all-start.2) | async-done | bytes 2097184 | tf_op jit(solution)/shard_map/all_to_all | solution.py:184
  324.6 46.4 %collective-permute-done.11.refs_1_ = bf16[160,2048]{1,0:T(8,128)(2,1)S(1)} collective-permute-done((bf16[160,2048]{1,0:T(8,128)(2,1)S(1)}, bf16[160,2048]{1,0:T(8,128)(2,1)S(1)}, u32[]{:S(2)}, u32[]{:S(2)}) %collective-permute-start.11) | collective-permute-done | bytes 655392 | tf_op jit(solution)/shard_map/ppermute | solution.py:50
  372.5 21.1 %collective-permute-done.14.refs_3_ = bf16[160,2048]{1,0:T(8,128)(2,1)S(1)} collective-permute-done((bf16[160,2048]{1,0:T(8,128)(2,1)S(1)}, bf16[160,2048]{1,0:T(8,128)(2,1)S(1)}, u32[]{:S(2)}, u32[]{:S(2)}) %collective-permute-start.14) | collective-permute-done | bytes 655392 | tf_op jit(solution)/shard_map/ppermute | solution.py:50
  396.3 14.3 %collective-permute-done.16.refs_5_ = bf16[160,2048]{1,0:T(8,128)(2,1)} collective-permute-done((bf16[160,2048]{1,0:T(8,128)(2,1)S(1)}, bf16[160,2048]{1,0:T(8,128)(2,1)}, u32[]{:S(2)}, u32[]{:S(2)}) %collective-permute-start.16) | collective-permute-done | bytes 655392 | tf_op jit(solution)/shard_map/ppermute | solution.py:50
  422.1 8.9 collective-permute-done.20.refs_7_
  431.1 4.7 all-to-all-start.3
  438.2 44.5 %feed_inner.1 = (bf16[1152,2048]{1,0:T(8,128)(2,1)}, bf16[1152,2048]{1,0:T(8,128)(2,1)}, bf16[1152,2048]{1,0:T(8,128)(2,1)}, bf16[1152,2048]{1,0:T(8,128)(2,1)},...) custom-call(s32[8]{0:T(128)} %gather_fusion.1, bf16[160,2048]{1,0:T(8,128)(2,1)} %copy-done.47, ...), custom_call_target="tpu_custom_call" | custom-call | flops 28991028 | bytes 60293 | tf_op jit(solution)/shard_map/feed_inner/pallas_call | solution.py:283
  483.9 14.4 %convolution_convert_fusion = bf16[2048,2048]{1,0:T(8,128)(2,1)S(1)} fusion(bf16[1152,2048]{1,0:T(8,128)(2,1)} %get-tuple-element.213.mid_ref, bf16[1152,2048]{1,0:T(8,128)(2,1)} %get-tuple-element.207), kind=kOutput, calls=%fused_computation.4 | convolution fusion | flops 9667870720 | bytes 17825792 | tf_op jit(solution)/shard_map/dot_general | solution.py:25
  503.6 15.3 %feed_down.1 = bf16[1152,2048]{1,0:T(8,128)(2,1)} custom-call(bf16[1152,2048]{1,0:T(8,128)(2,1)} %get-tuple-element.213.mid_ref, bf16[512,2048]{1,0:T(8,128)(2,1)} %bitcast.532, bf16[512,2048]{1,0:T(8,128)(2,1)} %collective-permute-done.18.refs_18_.refs_1_, bf16[512,2048]{1,0:T(8,128)(2,1)} %copy-done.12, bf16[512,2048]{1,0:T(8,128)(2,1)} %copy-done.14), custom_call_target="tpu_custom_call" | custom-call | flops 9663676 | bytes 17825 | tf_op jit(solution)/shard_map/feed_down/pallas_call | solution.py:283
  518.9 4.5 add_convert_fusion.7
  527.2 15.8 %feed_grads.2 = (bf16[2048,512]{1,0:T(8,128)(2,1)}, bf16[2048,512]{1,0:T(8,128)(2,1)}, bf16[2048,512]{1,0:T(8,128)(2,1)}, bf16[2048,512]{1,0:T(8,128)(2,1)}) custom-call(bf16[1152,2048]{1,0:T(8,128)(2,1)} %get-tuple-element.218.left_ref, bf16[1152,2048]{1,0:T(8,128)(2,1)} %get-tuple-element.250.right_ref.dg_ref), custom_call_target="tpu_custom_call" | custom-call | flops 9663676 | bytes 17825 | tf_op jit(solution)/shard_map/feed_grads/pallas_call | solution.py:283
  560.7 8.5 feed_action.1
  569.1 16.4 %feed_grads.3 = (bf16[2048,512]{1,0:T(8,128)(2,1)}, bf16[2048,512]{1,0:T(8,128)(2,1)}, bf16[2048,512]{1,0:T(8,128)(2,1)}, bf16[2048,512]{1,0:T(8,128)(2,1)}) custom-call(bf16[1152,2048]{1,0:T(8,128)(2,1)} %get-tuple-element.218.left_ref, bf16[1152,2048]{1,0:T(8,128)(2,1)} %get-tuple-element.251.right_ref.du_ref), custom_call_target="tpu_custom_call" | custom-call | flops 9663676 | bytes 17825 | tf_op jit(solution)/shard_map/feed_grads/pallas_call | solution.py:283
  597.5 5.4 all-to-all-start.4
  602.9 27.1 %feed_outer.1 = bf16[1152,2048]{1,0:T(8,128)(2,1)} custom-call(bf16[1152,2048]{1,0:T(8,128)(2,1)} %get-tuple-element.250.right_ref.dg_ref, bf16[1152,2048]{1,0:T(8,128)(2,1)} %get-tuple-element.251.right_ref.du_ref, bf16[2048,512]{1,0:T(8,128)(2,1)} %bitcast.2.refs_9_.refs_0_, bf16[2048,512]{1,0:T(8,128)(2,1)} %collective-permute-done.6.refs_10_.refs_1_, ...), custom_call_target="tpu_custom_call" | custom-call | flops 19327352 | bytes 30932 | tf_op jit(solution)/shard_map/feed_outer/pallas_call | solution.py:283
  659.1 9.2 all-to-all-done.4
  670.9 14.7 %collective-permute-done.37 = bf16[176,2048]{1,0:T(8,128)(2,1)S(1)} collective-permute-done((bf16[176,2048]{1,0:T(8,128)(2,1)}, bf16[176,2048]{1,0:T(8,128)(2,1)S(1)}, u32[]{:S(2)}, u32[]{:S(2)}) %collective-permute-start.37) | collective-permute-done | bytes 720928 | tf_op jit(solution)/shard_map/ppermute | solution.py:50
  688.3 14.4 %collective-permute-done.39 = bf16[176,2048]{1,0:T(8,128)(2,1)S(1)} collective-permute-done((bf16[176,2048]{1,0:T(8,128)(2,1)S(1)}, bf16[176,2048]{1,0:T(8,128)(2,1)S(1)}, u32[]{:S(2)}, u32[]{:S(2)}) %collective-permute-start.39) | collective-permute-done | bytes 720928 | tf_op jit(solution)/shard_map/ppermute | solution.py:50
  706.2 9.7 collective-permute-done.42
  721.0 11.7 %collective-permute-done.44 = bf16[8,384,128]{2,1,0:T(8,128)(2,1)S(1)} collective-permute-done((bf16[8,384,128]{2,1,0:T(8,128)(2,1)S(1)}, bf16[8,384,128]{2,1,0:T(8,128)(2,1)S(1)}, u32[]{:S(2)}, u32[]{:S(2)}) %collective-permute-start.44) | collective-permute-done | bytes 786464 | tf_op jit(solution)/shard_map/ppermute | solution.py:45
  745.0 7.5 collective-permute-done.47
  753.8 5.6 collective-permute-start.48
  774.9 4.5 all-to-all-start.6
  794.8 4.6 convolution_convert_fusion.6
  799.9 4.6 collective-permute-start.51
  804.9 16.7 %collective-permute-done.51 = bf16[560,128]{1,0:T(8,128)(2,1)S(1)} collective-permute-done((bf16[560,128]{1,0:T(8,128)(2,1)S(1)}, bf16[560,128]{1,0:T(8,128)(2,1)S(1)}, u32[]{:S(2)}, u32[]{:S(2)}) %collective-permute-start.51) | collective-permute-done | bytes 143392 | tf_op jit(solution)/shard_map/ppermute | solution.py:45
  821.7 20.3 %all-to-all-done.6 = bf16[8,256,512]{2,1,0:T(8,128)(2,1)} async-done(((bf16[8,256,512]{2,1,0:T(8,128)(2,1)}), bf16[8,256,512]{2,1,0:T(8,128)(2,1)}, u32[]{:S(2)}, u32[]{:S(2)}) %all-to-all-start.6) | async-done | bytes 2097184 | tf_op jit(solution)/shard_map/all_to_all | solution.py:184
  848.9 13.3 %collective-permute-start.52 = (bf16[2,560,128]{2,1,0:T(8,128)(2,1)}, bf16[2,560,128]{2,1,0:T(8,128)(2,1)}, u32[]{:S(2)}, u32[]{:S(2)}) collective-permute-start(bf16[2,560,128]{2,1,0:T(8,128)(2,1)} %fusion.71), channel_id=1, source_target_pairs={{0,1},{1,0},{2,3},{3,2},{4,5},{5,4},{6,7},{7,6},{8,9},{9,8},{10,11... | collective-permute-start | bytes 860168 | tf_op jit(solution)/shard_map/ppermute | solution.py:45
  863.2 4.5 all-to-all-start.7
  870.9 4.5 collective-permute-done.53
  882.5 4.0 bitcast_convert_fusion.2
  902.3 9.6 collective-permute-done.55
  914.7 6.0 reduce-scatter.6.cloned.1.call-done
  922.6 5.8 all-to-all-done.7
  956.7 3.8 collective-permute-done.56
  964.2 10.4 %collective-permute-done.45 = bf16[160,2048]{1,0:T(8,128)(2,1)S(1)} collective-permute-done((bf16[160,2048]{1,0:T(8,128)(2,1)S(1)}, bf16[160,2048]{1,0:T(8,128)(2,1)S(1)}, u32[]{:S(2)}, u32[]{:S(2)}) %collective-permute-start.45) | collective-permute-done | bytes 655392 | tf_op jit(solution)/shard_map/ppermute | solution.py:45
  990.3 16.8 %reduce-scatter.8.cloned.1.call-done = bf16[1,384,640]{2,1,0:T(8,128)(2,1)} async-done(((bf16[8,384,640]{2,1,0:T(8,128)(2,1)}), bf16[1,384,640]{2,1,0:T(8,128)(2,1)}) %reduce-scatter.8.cloned.1.call-update) | async-done | bytes 491536 | tf_op jit(solution)/shard_map/reduce_scatter | solution.py:752
  (679 shorter events, 320.9 us)
Async XLA Ops:
  7.2 109.8 %all-gather.7.cloned.1.call-start = ((), (), s32[]{:S(2)}) async-start(), calls=%async_computation.14 | async-start | bytes 4608000 | tf_op jit(solution)/shard_map/all_gather | solution.py:549
  11.7 214.8 %all-gather.9.cloned.1.call-start = ((), (), s32[]{:S(2)}) async-start(), calls=%async_computation.15 | async-start | bytes 3538944 | tf_op jit(solution)/shard_map/all_gather | solution.py:553
  146.8 77.6 %all-to-all-start.1 = ((bf16[8,256,512]{2,1,0:T(8,128)(2,1)}), bf16[8,256,512]{2,1,0:T(8,128)(2,1)}, u32[]{:S(2)}, u32[]{:S(2)}) async-start(bf16[8,256,512]{2,1,0:T(8,128)(2,1)} %bitcast.556), calls=%async_computation.1 | async-start | bytes 4194304 | tf_op jit(solution)/shard_map/all_to_all | solution.py:184
  156.3 47.2 %collective-permute-start.6 = (bf16[2048,512]{1,0:T(8,128)(2,1)}, bf16[2048,512]{1,0:T(8,128)(2,1)}, u32[]{:S(2)}, u32[]{:S(2)}) collective-permute-start(bf16[2048,512]{1,0:T(8,128)(2,1)} %bitcast.2.refs_9_.refs_0_), channel_id=1, source_target_pairs={{0,2},{2,0},{1,3},{3,1},{4,6},{6,4},{5,7},{7,5},{8,10},{10,8},{9,1... | collective-permute-start | bytes 6291464 | tf_op jit(solution)/shard_map/ppermute | solution.py:45
  224.4 46.9 %collective-permute-start.7 = (bf16[2048,512]{1,0:T(8,128)(2,1)}, bf16[2048,512]{1,0:T(8,128)(2,1)}, u32[]{:S(2)}, u32[]{:S(2)}) collective-permute-start(bf16[2048,512]{1,0:T(8,128)(2,1)} %bitcast.39.refs_13_.refs_4_), channel_id=1, source_target_pairs={{0,2},{2,0},{1,3},{3,1},{4,6},{6,4},{5,7},{7,5},{8,10},{10,8},{9,1... | collective-permute-start | bytes 6291464 | tf_op jit(solution)/shard_map/ppermute | solution.py:45
  225.6 45.7 %collective-permute-start.8 = (bf16[2048,512]{1,0:T(8,128)(2,1)}, bf16[2048,512]{1,0:T(8,128)(2,1)}, u32[]{:S(2)}, u32[]{:S(2)}) collective-permute-start(bf16[2048,512]{1,0:T(8,128)(2,1)} %bitcast.39.refs_13_.refs_4_), channel_id=1, source_target_pairs={{0,1},{1,0},{2,3},{3,2},{4,5},{5,4},{6,7},{7,6},{8,9},{9,8},{10,11... | collective-permute-start | bytes 6291464 | tf_op jit(solution)/shard_map/ppermute | solution.py:45
  243.5 73.1 %all-to-all-start.2 = ((bf16[8,512,256]{2,1,0:T(8,128)(2,1)}), bf16[8,512,256]{2,1,0:T(8,128)(2,1)}, u32[]{:S(2)}, u32[]{:S(2)}) async-start(bf16[8,512,256]{2,1,0:T(8,128)(2,1)} %bitcast.605), calls=%async_computation.2 | async-start | bytes 4194304 | tf_op jit(solution)/shard_map/all_to_all | solution.py:184
  247.9 174.2 %all-gather.11.cloned.1.call-start = ((), (), s32[]{:S(2)}) async-start(), calls=%async_computation.16 | async-start | bytes 5898240 | tf_op jit(solution)/shard_map/all_gather | solution.py:582
  282.3 42.2 %collective-permute-start.13 = (bf16[2048,512]{1,0:T(8,128)(2,1)}, bf16[2048,512]{1,0:T(8,128)(2,1)}, u32[]{:S(2)}, u32[]{:S(2)}) collective-permute-start(bf16[2048,512]{1,0:T(8,128)(2,1)} %collective-permute-done.7.refs_14_.refs_5_), channel_id=1, source_target_pairs={{0,1},{1,0},{2,3},{3,2},{4,5},{5,4},{6,7},{7,6},{8,9},{9,8},{10,11... | collective-permute-start | bytes 6291464 | tf_op jit(solution)/shard_map/ppermute | solution.py:45
  318.6 92.4 %collective-permute-start.18 = (bf16[512,2048]{1,0:T(8,128)(2,1)S(1)}, bf16[512,2048]{1,0:T(8,128)(2,1)}, u32[]{:S(2)}, u32[]{:S(2)}) collective-permute-start(bf16[512,2048]{1,0:T(8,128)(2,1)S(1)} %bitcast.529), channel_id=1, source_target_pairs={{0,2},{2,0},{1,3},{3,1},{4,6},{6,4},{5,7},{7,5},{8,10},{10,8},{9,1... | collective-permute-start | bytes 6291464 | tf_op jit(solution)/shard_map/ppermute | solution.py:45
  318.9 92.1 %collective-permute-start.19 = (bf16[512,2048]{1,0:T(8,128)(2,1)S(1)}, bf16[512,2048]{1,0:T(8,128)(2,1)S(1)}, u32[]{:S(2)}, u32[]{:S(2)}) collective-permute-start(bf16[512,2048]{1,0:T(8,128)(2,1)S(1)} %bitcast.530), channel_id=1, source_target_pairs={{0,1},{1,0},{2,3},{3,2},{4,5},{5,4},{6,7},{7,6},{8,9},{9,8},{10,11... | collective-permute-start | bytes 6291464 | tf_op jit(solution)/shard_map/ppermute | solution.py:45
  323.1 47.9 %collective-permute-start.11 = (bf16[160,2048]{1,0:T(8,128)(2,1)S(1)}, bf16[160,2048]{1,0:T(8,128)(2,1)S(1)}, u32[]{:S(2)}, u32[]{:S(2)}) collective-permute-start(bf16[160,2048]{1,0:T(8,128)(2,1)S(1)} %maximum_maximum_fusion.11.refs_0_), channel_id=1, source_target_pairs={{0,4},{8,0},{16,8},{24,16},{28,24},{20,28},{12,20},{4,12},{1,5},{9... | collective-permute-start | bytes 1966088 | tf_op jit(solution)/shard_map/ppermute | solution.py:50
  324.2 46.7 %collective-permute-start.12 = (bf16[160,2048]{1,0:T(8,128)(2,1)S(1)}, bf16[160,2048]{1,0:T(8,128)(2,1)S(1)}, u32[]{:S(2)}, u32[]{:S(2)}) collective-permute-start(bf16[160,2048]{1,0:T(8,128)(2,1)S(1)} %maximum_maximum_fusion.11.refs_0_), channel_id=1, source_target_pairs={{0,8},{8,16},{16,24},{24,28},{28,20},{20,12},{12,4},{4,0},{1,9},{9... | collective-permute-start | bytes 1966088 | tf_op jit(solution)/shard_map/ppermute | solution.py:50
  371.0 22.6 %collective-permute-start.14 = (bf16[160,2048]{1,0:T(8,128)(2,1)S(1)}, bf16[160,2048]{1,0:T(8,128)(2,1)S(1)}, u32[]{:S(2)}, u32[]{:S(2)}) collective-permute-start(bf16[160,2048]{1,0:T(8,128)(2,1)S(1)} %collective-permute-done.11.refs_1_), channel_id=1, source_target_pairs={{0,4},{8,0},{16,8},{24,16},{28,24},{20,28},{12,20},{4,12},{1,5},{9... | collective-permute-start | bytes 1966088 | tf_op jit(solution)/shard_map/ppermute | solution.py:50
  371.0 23.1 %collective-permute-start.15 = (bf16[160,2048]{1,0:T(8,128)(2,1)S(1)}, bf16[160,2048]{1,0:T(8,128)(2,1)S(1)}, u32[]{:S(2)}, u32[]{:S(2)}) collective-permute-start(bf16[160,2048]{1,0:T(8,128)(2,1)S(1)} %collective-permute-done.12.refs_2_), channel_id=1, source_target_pairs={{0,8},{8,16},{16,24},{24,28},{28,20},{20,12},{12,4},{4,0},{1,9},{9... | collective-permute-start | bytes 1966088 | tf_op jit(solution)/shard_map/ppermute | solution.py:50
  412.4 18.7 %collective-permute-start.21 = (bf16[512,2048]{1,0:T(8,128)(2,1)}, bf16[512,2048]{1,0:T(8,128)(2,1)S(1)}, u32[]{:S(2)}, u32[]{:S(2)}) collective-permute-start(bf16[512,2048]{1,0:T(8,128)(2,1)} %collective-permute-done.18.refs_18_.refs_1_), channel_id=1, source_target_pairs={{0,1},{1,0},{2,3},{3,2},{4,5},{5,4},{6,7},{7,6},{8,9},{9,8},{10,11... | collective-permute-start | bytes 6291464 | tf_op jit(solution)/shard_map/ppermute | solution.py:45
  413.8 24.4 %collective-permute-start.22 = (bf16[2048,512]{1,0:T(8,128)(2,1)}, bf16[2048,512]{1,0:T(8,128)(2,1)}, u32[]{:S(2)}, u32[]{:S(2)}) collective-permute-start(bf16[2048,512]{1,0:T(8,128)(2,1)} %collective-permute-done.6.refs_10_.refs_1_), channel_id=1, source_target_pairs={{0,1},{1,0},{2,3},{3,2},{4,5},{5,4},{6,7},{7,6},{8,9},{9,8},{10,11... | collective-permute-start | bytes 6291464 | tf_op jit(solution)/shard_map/ppermute | solution.py:45
  413.9 17.2 %collective-permute-start.20 = (bf16[160,2048]{1,0:T(8,128)(2,1)}, bf16[160,2048]{1,0:T(8,128)(2,1)}, u32[]{:S(2)}, u32[]{:S(2)}) collective-permute-start(bf16[160,2048]{1,0:T(8,128)(2,1)} %collective-permute-done.16.refs_5_), channel_id=1, source_target_pairs={{0,4},{8,0},{16,8},{24,16},{28,24},{20,28},{12,20},{4,12},{1,5},{9... | collective-permute-start | bytes 1966088 | tf_op jit(solution)/shard_map/ppermute | solution.py:50
  431.1 51.6 %all-to-all-start.3 = ((bf16[8,384,128]{2,1,0:T(8,128)(2,1)}), bf16[8,384,128]{2,1,0:T(8,128)(2,1)}, u32[]{:S(2)}, u32[]{:S(2)}) async-start(bf16[8,384,128]{2,1,0:T(8,128)(2,1)} %pad_maximum_fusion.1), calls=%async_computation.3 | async-start | bytes 1572864 | tf_op jit(solution)/shard_map/all_to_all | solution.py:184
  435.7 221.0 %reduce-scatter.4.cloned.1.call-start = ((), (), s32[]{:S(2)}) async-start(), calls=%async_computation.11 | async-start | bytes 5308416 | tf_op jit(solution)/shard_map/reduce_scatter | solution.py:639
  482.7 18.5 %collective-permute-start.23 = (bf16[8,384,128]{2,1,0:T(8,128)(2,1)}, bf16[8,384,128]{2,1,0:T(8,128)(2,1)}, u32[]{:S(2)}, u32[]{:S(2)}) collective-permute-start(bf16[8,384,128]{2,1,0:T(8,128)(2,1)} %all-to-all-done.3.refs_0_), channel_id=1, source_target_pairs={{0,2},{2,0},{1,3},{3,1},{4,6},{6,4},{5,7},{7,5},{8,10},{10,8},{9,1... | collective-permute-start | bytes 2359304 | tf_op jit(solution)/shard_map/ppermute | solution.py:45
  501.1 17.8 %collective-permute-start.25 = (bf16[512,2048]{1,0:T(8,128)(2,1)}, bf16[512,2048]{1,0:T(8,128)(2,1)}, u32[]{:S(2)}, u32[]{:S(2)}) collective-permute-start(bf16[512,2048]{1,0:T(8,128)(2,1)} %get-tuple-element.212), channel_id=1, source_target_pairs={{0,1},{1,0},{2,3},{3,2},{4,5},{5,4},{6,7},{7,6},{8,9},{9,8},{10,11... | collective-permute-start | bytes 6291464 | tf_op jit(solution)/shard_map/ppermute | solution.py:45
  503.0 20.4 %collective-permute-start.24 = (bf16[512,2048]{1,0:T(8,128)(2,1)}, bf16[512,2048]{1,0:T(8,128)(2,1)}, u32[]{:S(2)}, u32[]{:S(2)}) collective-permute-start(bf16[512,2048]{1,0:T(8,128)(2,1)} %get-tuple-element.210), channel_id=1, source_target_pairs={{0,1},{1,0},{2,3},{3,2},{4,5},{5,4},{6,7},{7,6},{8,9},{9,8},{10,11... | collective-permute-start | bytes 6291464 | tf_op jit(solution)/shard_map/ppermute | solution.py:45
  503.1 24.0 %collective-permute-start.26 = (bf16[8,384,128]{2,1,0:T(8,128)(2,1)}, bf16[8,384,128]{2,1,0:T(8,128)(2,1)}, u32[]{:S(2)}, u32[]{:S(2)}) collective-permute-start(bf16[8,384,128]{2,1,0:T(8,128)(2,1)} %all-to-all-done.3.refs_0_), channel_id=1, source_target_pairs={{0,1},{1,0},{2,3},{3,2},{4,5},{5,4},{6,7},{7,6},{8,9},{9,8},{10,11... | collective-permute-start | bytes 2359304 | tf_op jit(solution)/shard_map/ppermute | solution.py:45
  503.5 23.6 %collective-permute-start.27 = (bf16[8,384,128]{2,1,0:T(8,128)(2,1)}, bf16[8,384,128]{2,1,0:T(8,128)(2,1)}, u32[]{:S(2)}, u32[]{:S(2)}) collective-permute-start(bf16[8,384,128]{2,1,0:T(8,128)(2,1)} %collective-permute-done.23.refs_1_), channel_id=1, source_target_pairs={{0,1},{1,0},{2,3},{3,2},{4,5},{5,4},{6,7},{7,6},{8,9},{9,8},{10,11... | collective-permute-start | bytes 2359304 | tf_op jit(solution)/shard_map/ppermute | solution.py:45
  543.0 42.6 %collective-permute-start.30 = (bf16[2048,512]{1,0:T(8,128)(2,1)}, bf16[2048,512]{1,0:T(8,128)(2,1)}, u32[]{:S(2)}, u32[]{:S(2)}) collective-permute-start(bf16[2048,512]{1,0:T(8,128)(2,1)} %get-tuple-element.232), channel_id=1, source_target_pairs={{0,1},{1,0},{2,3},{3,2},{4,5},{5,4},{6,7},{7,6},{8,9},{9,8},{10,11... | collective-permute-start | bytes 6291464 | tf_op jit(solution)/shard_map/ppermute | solution.py:45
  543.4 45.8 %collective-permute-start.29 = (bf16[2048,512]{1,0:T(8,128)(2,1)}, bf16[2048,512]{1,0:T(8,128)(2,1)}, u32[]{:S(2)}, u32[]{:S(2)}) collective-permute-start(bf16[2048,512]{1,0:T(8,128)(2,1)} %get-tuple-element.230), channel_id=1, source_target_pairs={{0,1},{1,0},{2,3},{3,2},{4,5},{5,4},{6,7},{7,6},{8,9},{9,8},{10,11... | collective-permute-start | bytes 6291464 | tf_op jit(solution)/shard_map/ppermute | solution.py:45
  543.5 48.1 %collective-permute-start.28 = (bf16[512,2048]{1,0:T(8,128)(2,1)}, bf16[512,2048]{1,0:T(8,128)(2,1)}, u32[]{:S(2)}, u32[]{:S(2)}) collective-permute-start(bf16[512,2048]{1,0:T(8,128)(2,1)} %add_convert_fusion.7), channel_id=1, source_target_pairs={{0,2},{2,0},{1,3},{3,1},{4,6},{6,4},{5,7},{7,5},{8,10},{10,8},{9,1... | collective-permute-start | bytes 6291464 | tf_op jit(solution)/shard_map/ppermute | solution.py:45
  594.0 47.4 %collective-permute-start.35 = (bf16[8,384,128]{2,1,0:T(8,128)(2,1)}, bf16[8,384,128]{2,1,0:T(8,128)(2,1)}, u32[]{:S(2)}, u32[]{:S(2)}) collective-permute-start(bf16[8,384,128]{2,1,0:T(8,128)(2,1)} %get-tuple-element.265), channel_id=1, source_target_pairs={{0,1},{1,0},{2,3},{3,2},{4,5},{5,4},{6,7},{7,6},{8,9},{9,8},{10,11... | collective-permute-start | bytes 2359304 | tf_op jit(solution)/shard_map/ppermute | solution.py:45
  594.9 48.7 %collective-permute-start.34 = (bf16[8,384,128]{2,1,0:T(8,128)(2,1)}, bf16[8,384,128]{2,1,0:T(8,128)(2,1)}, u32[]{:S(2)}, u32[]{:S(2)}) collective-permute-start(bf16[8,384,128]{2,1,0:T(8,128)(2,1)} %get-tuple-element.263), channel_id=1, source_target_pairs={{0,1},{1,0},{2,3},{3,2},{4,5},{5,4},{6,7},{7,6},{8,9},{9,8},{10,11... | collective-permute-start | bytes 2359304 | tf_op jit(solution)/shard_map/ppermute | solution.py:45
  595.0 51.0 %collective-permute-start.33 = (bf16[2048,512]{1,0:T(8,128)(2,1)}, bf16[2048,512]{1,0:T(8,128)(2,1)}, u32[]{:S(2)}, u32[]{:S(2)}) collective-permute-start(bf16[2048,512]{1,0:T(8,128)(2,1)} %get-tuple-element.260), channel_id=1, source_target_pairs={{0,1},{1,0},{2,3},{3,2},{4,5},{5,4},{6,7},{7,6},{8,9},{9,8},{10,11... | collective-permute-start | bytes 6291464 | tf_op jit(solution)/shard_map/ppermute | solution.py:45
  595.4 54.3 %collective-permute-start.32 = (bf16[2048,512]{1,0:T(8,128)(2,1)}, bf16[2048,512]{1,0:T(8,128)(2,1)}, u32[]{:S(2)}, u32[]{:S(2)}) collective-permute-start(bf16[2048,512]{1,0:T(8,128)(2,1)} %get-tuple-element.258), channel_id=1, source_target_pairs={{0,1},{1,0},{2,3},{3,2},{4,5},{5,4},{6,7},{7,6},{8,9},{9,8},{10,11... | collective-permute-start | bytes 6291464 | tf_op jit(solution)/shard_map/ppermute | solution.py:45
  595.5 57.7 %collective-permute-start.31 = (bf16[2048,512]{1,0:T(8,128)(2,1)}, bf16[2048,512]{1,0:T(8,128)(2,1)}, u32[]{:S(2)}, u32[]{:S(2)}) collective-permute-start(bf16[2048,512]{1,0:T(8,128)(2,1)} %add_convert_fusion.4), channel_id=1, source_target_pairs={{0,2},{2,0},{1,3},{3,1},{4,6},{6,4},{5,7},{7,5},{8,10},{10,8},{9,1... | collective-permute-start | bytes 6291464 | tf_op jit(solution)/shard_map/ppermute | solution.py:45
  597.5 70.8 %all-to-all-start.4 = ((bf16[8,512,256]{2,1,0:T(8,128)(2,1)}), bf16[8,512,256]{2,1,0:T(8,128)(2,1)}, u32[]{:S(2)}, u32[]{:S(2)}) async-start(bf16[8,512,256]{2,1,0:T(8,128)(2,1)} %bitcast.557), calls=%async_computation.4 | async-start | bytes 4194304 | tf_op jit(solution)/shard_map/all_to_all | solution.py:184
  668.3 17.3 %collective-permute-start.37 = (bf16[176,2048]{1,0:T(8,128)(2,1)}, bf16[176,2048]{1,0:T(8,128)(2,1)S(1)}, u32[]{:S(2)}, u32[]{:S(2)}) collective-permute-start(bf16[176,2048]{1,0:T(8,128)(2,1)} %maximum_maximum_fusion.8), channel_id=1, source_target_pairs={{0,4},{8,0},{16,8},{24,16},{28,24},{20,28},{12,20},{4,12},{1,5},{9... | collective-permute-start | bytes 2162696 | tf_op jit(solution)/shard_map/ppermute | solution.py:50
  669.5 17.0 %collective-permute-start.36 = (bf16[176,2048]{1,0:T(8,128)(2,1)}, bf16[176,2048]{1,0:T(8,128)(2,1)S(1)}, u32[]{:S(2)}, u32[]{:S(2)}) collective-permute-start(bf16[176,2048]{1,0:T(8,128)(2,1)} %maximum_maximum_fusion.9), channel_id=1, source_target_pairs={{0,8},{8,16},{16,24},{24,28},{28,20},{20,12},{12,4},{4,0},{1,9},{9... | collective-permute-start | bytes 2162696 | tf_op jit(solution)/shard_map/ppermute | solution.py:50
  669.7 46.2 %collective-permute-start.42 = (bf16[2048,512]{1,0:T(8,128)(2,1)}, bf16[2048,512]{1,0:T(8,128)(2,1)S(1)}, u32[]{:S(2)}, u32[]{:S(2)}) collective-permute-start(bf16[2048,512]{1,0:T(8,128)(2,1)} %add_convert_fusion.1), channel_id=1, source_target_pairs={{0,2},{2,0},{1,3},{3,1},{4,6},{6,4},{5,7},{7,5},{8,10},{10,8},{9,1... | collective-permute-start | bytes 6291464 | tf_op jit(solution)/shard_map/ppermute | solution.py:45
  704.3 28.4 %collective-permute-start.44 = (bf16[8,384,128]{2,1,0:T(8,128)(2,1)S(1)}, bf16[8,384,128]{2,1,0:T(8,128)(2,1)S(1)}, u32[]{:S(2)}, u32[]{:S(2)}) collective-permute-start(bf16[8,384,128]{2,1,0:T(8,128)(2,1)S(1)} %copy-done.69), channel_id=1, source_target_pairs={{0,2},{2,0},{1,3},{3,1},{4,6},{6,4},{5,7},{7,5},{8,10},{10,8},{9,1... | collective-permute-start | bytes 2359304 | tf_op jit(solution)/shard_map/ppermute | solution.py:45
  741.5 22.8 %all-to-all-start.5 = ((bf16[8,384,128]{2,1,0:T(8,128)(2,1)}), bf16[8,384,128]{2,1,0:T(8,128)(2,1)S(1)}, u32[]{:S(2)}, u32[]{:S(2)}) async-start(bf16[8,384,128]{2,1,0:T(8,128)(2,1)} %add_convert_fusion.9), calls=%async_computation.6 | async-start | bytes 1572864 | tf_op jit(solution)/shard_map/all_to_all | solution.py:184
  774.9 67.1 %all-to-all-start.6 = ((bf16[8,256,512]{2,1,0:T(8,128)(2,1)}), bf16[8,256,512]{2,1,0:T(8,128)(2,1)}, u32[]{:S(2)}, u32[]{:S(2)}) async-start(bf16[8,256,512]{2,1,0:T(8,128)(2,1)} %bitcast.139), calls=%async_computation.7 | async-start | bytes 4194304 | tf_op jit(solution)/shard_map/all_to_all | solution.py:184
  779.4 141.3 %reduce-scatter.6.cloned.1.call-start = ((), (), s32[]{:S(2)}) async-start(), calls=%async_computation.12 | async-start | bytes 3538944 | tf_op jit(solution)/shard_map/reduce_scatter | solution.py:696
  799.9 21.8 %collective-permute-start.51 = (bf16[560,128]{1,0:T(8,128)(2,1)S(1)}, bf16[560,128]{1,0:T(8,128)(2,1)S(1)}, u32[]{:S(2)}, u32[]{:S(2)}) collective-permute-start(bf16[560,128]{1,0:T(8,128)(2,1)S(1)} %slice.685), channel_id=1, source_target_pairs={{0,28},{4,0},{8,4},{12,8},{16,12},{20,16},{24,20},{28,24},{1,29},{... | collective-permute-start | bytes 430088 | tf_op jit(solution)/shard_map/ppermute | solution.py:45
  848.9 19.4 %collective-permute-start.52 = (bf16[2,560,128]{2,1,0:T(8,128)(2,1)}, bf16[2,560,128]{2,1,0:T(8,128)(2,1)}, u32[]{:S(2)}, u32[]{:S(2)}) collective-permute-start(bf16[2,560,128]{2,1,0:T(8,128)(2,1)} %fusion.71), channel_id=1, source_target_pairs={{0,1},{1,0},{2,3},{3,2},{4,5},{5,4},{6,7},{7,6},{8,9},{9,8},{10,11... | collective-permute-start | bytes 860168 | tf_op jit(solution)/shard_map/ppermute | solution.py:45
  863.2 65.3 %all-to-all-start.7 = ((bf16[8,256,512]{2,1,0:T(8,128)(2,1)}), bf16[8,256,512]{2,1,0:T(8,128)(2,1)}, u32[]{:S(2)}, u32[]{:S(2)}) async-start(bf16[8,256,512]{2,1,0:T(8,128)(2,1)} %bitcast.553), calls=%async_computation.8 | async-start | bytes 4194304 | tf_op jit(solution)/shard_map/all_to_all | solution.py:184
  867.7 139.5 %reduce-scatter.8.cloned.1.call-start = ((), (), s32[]{:S(2)}) async-start(), calls=%async_computation.13 | async-start | bytes 4423680 | tf_op jit(solution)/shard_map/reduce_scatter | solution.py:752
  946.6 27.9 %collective-permute-start.45 = (bf16[160,2048]{1,0:T(8,128)(2,1)S(1)}, bf16[160,2048]{1,0:T(8,128)(2,1)S(1)}, u32[]{:S(2)}, u32[]{:S(2)}) collective-permute-start(bf16[160,2048]{1,0:T(8,128)(2,1)S(1)} %get-tuple-element.434), channel_id=1, source_target_pairs={{0,2},{2,0},{1,3},{3,1},{4,6},{6,4},{5,7},{7,5},{8,10},{10,8},{9,1... | collective-permute-start | bytes 1966088 | tf_op jit(solution)/shard_map/ppermute | solution.py:45
  956.0 27.1 %collective-permute-start.62 = (f32[1,768]{1,0:T(1,128)S(1)}, f32[1,768]{1,0:T(1,128)S(1)}, u32[]{:S(2)}, u32[]{:S(2)}) collective-permute-start(f32[1,768]{1,0:T(1,128)S(1)} %add.497), channel_id=1, source_target_pairs={{0,2},{2,0},{1,3},{3,1},{4,6},{6,4},{5,7},{7,5},{8,10},{10,8},{9,1... | collective-permute-start | bytes 9224 | tf_op jit(solution)/shard_map/ppermute | solution.py:45
  960.7 23.9 %collective-permute-start.57 = (bf16[2,160,2048]{2,1,0:T(8,128)(2,1)S(1)}, bf16[2,160,2048]{2,1,0:T(8,128)(2,1)S(1)}, u32[]{:S(2)}, u32[]{:S(2)}) collective-permute-start(bf16[2,160,2048]{2,1,0:T(8,128)(2,1)S(1)} %maximum_select_fusion.7), channel_id=1, source_target_pairs={{0,1},{1,0},{2,3},{3,2},{4,5},{5,4},{6,7},{7,6},{8,9},{9,8},{10,11... | collective-permute-start | bytes 3932168 | tf_op jit(solution)/shard_map/ppermute | solution.py:45
  (166 other events, 1742.1 us)
Sparse Core Ops, SparseCore 0:
  11.8 105.1 all-gather.6
  119.7 95.4 all-gather.8
  274.2 112.3 all-gather.10
  527.3 112.5 reduce-scatter.3
  793.7 126.9 reduce-scatter.5
  924.2 82.9 reduce-scatter.7

commit v5 on v4

--- a/solution.py
+++ b/solution.py
@@ -604,7 +604,7 @@
     attn_p = dot(pad_rows(mixed_p, quad * part_p), w_out_p, 1, 0).reshape(quad, part_p, -1)
     attn_a = dot(pad_rows(mixed_a, quad * part_a), w_out_a, 1, 0).reshape(quad, part_a, -1)
     attn, up_far, up_other = fence(pack(attn_p, attn_a), up_far, up_other)
-    attn, down_p = fence(quad_reduce(attn), down_p)
+    attn, down_p, cots = fence(quad_reduce(attn), down_p, cots)
     down_p = join_columns(down_p)
     down_far, down_other = swap(down_p, "mp"), swap(down_p, "expert")
     middle_p = x_p + attn[:part_p]
@@ -621,7 +621,7 @@
     down_far, down_other = normed2.meet(down_far, down_other)
     normed2.hop()
     w_down_p = [down_p, down_far, down_other, swap(down_far, "expert")]
-    w_down_p, cots, in_action = normed2.meet(w_down_p, cots, in_action)
+    w_down_p, in_action = normed2.meet(w_down_p, in_action)
     in_action = a2a(in_action)
 
     inner, (normed2_p, cots_p), (normed2_a, cots_a) = feed_inner(

time: 1030 us -> 1020 us (level)
  blocking collectives: 88.4 us -> 0 us
  waiting for transfers between devices: 378 us -> 444 us
    all_to_all x7 -> x8, waiting for transfers between devices: 72.9 us -> 172 us  [a2a(): return lax.all_to_all(parts, 'seq', 0, 0, tiled=True)]
    all_to_all x1 -> x0, blocking collectives: 88.4 us -> none  [a2a(): return lax.all_to_all(parts, 'seq', 0, 0, tiled=True)]
    ppermute x14, waiting for transfers between devices: 125 us -> 82.6 us  [ring_step(): return lax.ppermute(block, 'seq', pairs)]
    all_to_all x7 -> x8, starting transfers between devices: 32 us -> 39.4 us  [a2a(): return lax.all_to_all(parts, 'seq', 0, 0, tiled=True)]
    unnamed x291 -> x269, local copies, waits for them, and re-layouts: 33.7 us -> 34.9 us
  transfers between devices with their start and end apart: 78 -> 79, of which waited for: 38 -> 42; matrix products, arithmetic and copies ran while one was open for 23% -> 24% of each run, Pallas kernels for 12% -> 13%
where the time goes in v5:
time: 1020 us; the launch traced here: 1010 us
  waiting for transfers between devices  444 us (44%)
  Pallas kernels  128 us (13%)
  other arithmetic  125 us (12%)
  starting transfers between devices  124 us (12%)
  local copies, waits for them, and re-layouts  111 us (11%)
  matrix products  44.6 us (4%)
  between operations  32.9 us (3%)
    all_to_all x8, waiting for transfers between devices, a2a(): return lax.all_to_all(parts, 'seq', 0, 0, tiled=True)  172 us
    ppermute x48, waiting for transfers between devices, shift(): lax.ppermute(block, axis, [(i, (i + distance) % count) for i in range(cou...  158 us
    pallas_call x6, Pallas kernels, row_kernel(): pl.pallas_call(body, grid_spec=pltpu.PrefetchScalarGridSpec(num_scalar_pr...  128 us
    ppermute x14, waiting for transfers between devices, ring_step(): return lax.ppermute(block, 'seq', pairs)  82.6 us
    ppermute x48, starting transfers between devices, shift(): lax.ppermute(block, axis, [(i, (i + distance) % count) for i in range(cou...  70.8 us
    all_to_all x8, starting transfers between devices, a2a(): return lax.all_to_all(parts, 'seq', 0, 0, tiled=True)  39.4 us
    unnamed x269, local copies, waits for them, and re-layouts  34.9 us
    dot_general x13, matrix products, dot(): lax.dot_general(left, right, (((left_dim,), (right_dim,)), ((), ())), pre...  32.4 us
  transfers between devices with their start and end apart: 79, of which 42 were waited for; matrix products, arithmetic and copies ran while one was open for 24% of the time, Pallas kernels for 13%

profile of v5, /device:TPU:1, one launch (start us, length us, event | category | flops | bytes accessed | tf_op | source)
XLA Modules:
  0.0 1010.0 jit_solution(14465295985257533169)
XLA Ops:
  13.2 6.5 all-to-all-start
  20.6 83.9 %all-to-all-done = bf16[8,256,512]{2,1,0:T(8,128)(2,1)} async-done(((bf16[8,256,512]{2,1,0:T(8,128)(2,1)}), bf16[8,256,512]{2,1,0:T(8,128)(2,1)}, u32[]{:S(2)}, u32[]{:S(2)}) %all-to-all-start) | async-done | bytes 2097184 | tf_op jit(solution)/shard_map/all_to_all | solution.py:184
  104.6 7.3 collective-permute-start
  130.2 4.3 collective-permute-done.1
  140.1 8.9 collective-permute-done.3
  149.1 4.5 all-to-all-start.1
  176.8 29.3 %collective-permute-done.6.refs_10_.refs_1_ = bf16[2048,512]{1,0:T(8,128)(2,1)} collective-permute-done((bf16[2048,512]{1,0:T(8,128)(2,1)}, bf16[2048,512]{1,0:T(8,128)(2,1)}, u32[]{:S(2)}, u32[]{:S(2)}) %collective-permute-start.6) | collective-permute-done | bytes 2097184 | tf_op jit(solution)/shard_map/ppermute | solution.py:45
  206.1 20.0 %all-to-all-done.1 = bf16[8,256,512]{2,1,0:T(8,128)(2,1)} async-done(((bf16[8,256,512]{2,1,0:T(8,128)(2,1)}), bf16[8,256,512]{2,1,0:T(8,128)(2,1)}, u32[]{:S(2)}, u32[]{:S(2)}) %all-to-all-start.1) | async-done | bytes 2097184 | tf_op jit(solution)/shard_map/all_to_all | solution.py:184
  244.7 4.5 all-to-all-start.2
  253.0 20.0 %collective-permute-done.7.refs_14_.refs_5_ = bf16[2048,512]{1,0:T(8,128)(2,1)} collective-permute-done((bf16[2048,512]{1,0:T(8,128)(2,1)}, bf16[2048,512]{1,0:T(8,128)(2,1)}, u32[]{:S(2)}, u32[]{:S(2)}) %collective-permute-start.7) | collective-permute-done | bytes 2097184 | tf_op jit(solution)/shard_map/ppermute | solution.py:45
  284.6 14.2 %collective-permute-done.10 = bf16[160,2048]{1,0:T(8,128)(2,1)} collective-permute-done((bf16[160,2048]{1,0:T(8,128)(2,1)S(1)}, bf16[160,2048]{1,0:T(8,128)(2,1)}, u32[]{:S(2)}, u32[]{:S(2)}) %collective-permute-start.10) | collective-permute-done | bytes 655392 | tf_op jit(solution)/shard_map/ppermute | solution.py:45
  301.6 33.3 %all-to-all-done.2 = bf16[8,512,256]{2,1,0:T(8,128)(2,1)} async-done(((bf16[8,512,256]{2,1,0:T(8,128)(2,1)}), bf16[8,512,256]{2,1,0:T(8,128)(2,1)}, u32[]{:S(2)}, u32[]{:S(2)}) %all-to-all-start.2) | async-done | bytes 2097184 | tf_op jit(solution)/shard_map/all_to_all | solution.py:184
  334.8 5.6 all-gather.11.cloned.1.call-done
  348.7 14.9 %collective-permute-done.11.refs_1_ = bf16[160,2048]{1,0:T(8,128)(2,1)S(1)} collective-permute-done((bf16[160,2048]{1,0:T(8,128)(2,1)S(1)}, bf16[160,2048]{1,0:T(8,128)(2,1)S(1)}, u32[]{:S(2)}, u32[]{:S(2)}) %collective-permute-start.11) | collective-permute-done | bytes 655392 | tf_op jit(solution)/shard_map/ppermute | solution.py:50
  365.6 13.7 %collective-permute-done.14.refs_3_ = bf16[160,2048]{1,0:T(8,128)(2,1)S(1)} collective-permute-done((bf16[160,2048]{1,0:T(8,128)(2,1)S(1)}, bf16[160,2048]{1,0:T(8,128)(2,1)S(1)}, u32[]{:S(2)}, u32[]{:S(2)}) %collective-permute-start.14) | collective-permute-done | bytes 655392 | tf_op jit(solution)/shard_map/ppermute | solution.py:50
  381.1 12.9 %collective-permute-done.16.refs_5_ = bf16[160,2048]{1,0:T(8,128)(2,1)} collective-permute-done((bf16[160,2048]{1,0:T(8,128)(2,1)S(1)}, bf16[160,2048]{1,0:T(8,128)(2,1)}, u32[]{:S(2)}, u32[]{:S(2)}) %collective-permute-start.16) | collective-permute-done | bytes 655392 | tf_op jit(solution)/shard_map/ppermute | solution.py:50
  409.5 6.3 collective-permute-done.20.refs_7_
  415.8 4.2 all-to-all-start.3
  422.5 44.4 %feed_inner.1 = (bf16[1152,2048]{1,0:T(8,128)(2,1)}, bf16[1152,2048]{1,0:T(8,128)(2,1)}, bf16[1152,2048]{1,0:T(8,128)(2,1)}, bf16[1152,2048]{1,0:T(8,128)(2,1)},...) custom-call(s32[8]{0:T(128)} %gather_fusion.1, bf16[160,2048]{1,0:T(8,128)(2,1)} %copy-done.50, ...), custom_call_target="tpu_custom_call" | custom-call | flops 28991028 | bytes 60293 | tf_op jit(solution)/shard_map/feed_inner/pallas_call | solution.py:283
  468.1 14.4 %convolution_convert_fusion = bf16[2048,2048]{1,0:T(8,128)(2,1)S(1)} fusion(bf16[1152,2048]{1,0:T(8,128)(2,1)} %get-tuple-element.213.mid_ref, bf16[1152,2048]{1,0:T(8,128)(2,1)} %get-tuple-element.207), kind=kOutput, calls=%fused_computation.4 | convolution fusion | flops 9667870720 | bytes 17825792 | tf_op jit(solution)/shard_map/dot_general | solution.py:25
  487.8 15.3 %feed_down.1 = bf16[1152,2048]{1,0:T(8,128)(2,1)} custom-call(bf16[1152,2048]{1,0:T(8,128)(2,1)} %get-tuple-element.213.mid_ref, bf16[512,2048]{1,0:T(8,128)(2,1)} %bitcast.532, bf16[512,2048]{1,0:T(8,128)(2,1)} %copy-done.12, bf16[512,2048]{1,0:T(8,128)(2,1)} %copy-done.13, bf16[512,2048]{1,0:T(8,128)(2,1)} %collective-permute-done.21.refs_20_.refs_3_), custom_call_target="tpu_custom_call" | custom-call | flops 9663676 | bytes 17825 | tf_op jit(solution)/shard_map/feed_down/pallas_call | solution.py:283
  503.1 4.5 add_convert_fusion.7
  511.3 15.8 %feed_grads.2 = (bf16[2048,512]{1,0:T(8,128)(2,1)}, bf16[2048,512]{1,0:T(8,128)(2,1)}, bf16[2048,512]{1,0:T(8,128)(2,1)}, bf16[2048,512]{1,0:T(8,128)(2,1)}) custom-call(bf16[1152,2048]{1,0:T(8,128)(2,1)} %get-tuple-element.218.left_ref, bf16[1152,2048]{1,0:T(8,128)(2,1)} %get-tuple-element.250.right_ref.dg_ref), custom_call_target="tpu_custom_call" | custom-call | flops 9663676 | bytes 17825 | tf_op jit(solution)/shard_map/feed_grads/pallas_call | solution.py:283
  544.9 8.5 feed_action.1
  553.4 16.4 %feed_grads.3 = (bf16[2048,512]{1,0:T(8,128)(2,1)}, bf16[2048,512]{1,0:T(8,128)(2,1)}, bf16[2048,512]{1,0:T(8,128)(2,1)}, bf16[2048,512]{1,0:T(8,128)(2,1)}) custom-call(bf16[1152,2048]{1,0:T(8,128)(2,1)} %get-tuple-element.218.left_ref, bf16[1152,2048]{1,0:T(8,128)(2,1)} %get-tuple-element.251.right_ref.du_ref), custom_call_target="tpu_custom_call" | custom-call | flops 9663676 | bytes 17825 | tf_op jit(solution)/shard_map/feed_grads/pallas_call | solution.py:283
  581.7 5.3 all-to-all-start.4
  587.0 27.1 %feed_outer.1 = bf16[1152,2048]{1,0:T(8,128)(2,1)} custom-call(bf16[1152,2048]{1,0:T(8,128)(2,1)} %get-tuple-element.250.right_ref.dg_ref, bf16[1152,2048]{1,0:T(8,128)(2,1)} %get-tuple-element.251.right_ref.du_ref, bf16[2048,512]{1,0:T(8,128)(2,1)} %bitcast.2.refs_9_.refs_0_, bf16[2048,512]{1,0:T(8,128)(2,1)} %collective-permute-done.6.refs_10_.refs_1_, ...), custom_call_target="tpu_custom_call" | custom-call | flops 19327352 | bytes 30932 | tf_op jit(solution)/shard_map/feed_outer/pallas_call | solution.py:283
  643.0 9.0 all-to-all-done.4
  654.8 14.5 %collective-permute-done.37 = bf16[176,2048]{1,0:T(8,128)(2,1)S(1)} collective-permute-done((bf16[176,2048]{1,0:T(8,128)(2,1)}, bf16[176,2048]{1,0:T(8,128)(2,1)S(1)}, u32[]{:S(2)}, u32[]{:S(2)}) %collective-permute-start.37) | collective-permute-done | bytes 720928 | tf_op jit(solution)/shard_map/ppermute | solution.py:50
  672.1 14.4 %collective-permute-done.39 = bf16[176,2048]{1,0:T(8,128)(2,1)S(1)} collective-permute-done((bf16[176,2048]{1,0:T(8,128)(2,1)S(1)}, bf16[176,2048]{1,0:T(8,128)(2,1)S(1)}, u32[]{:S(2)}, u32[]{:S(2)}) %collective-permute-start.39) | collective-permute-done | bytes 720928 | tf_op jit(solution)/shard_map/ppermute | solution.py:50
  690.2 9.4 collective-permute-done.42
  705.1 11.4 %collective-permute-done.44 = bf16[8,384,128]{2,1,0:T(8,128)(2,1)S(1)} collective-permute-done((bf16[8,384,128]{2,1,0:T(8,128)(2,1)S(1)}, bf16[8,384,128]{2,1,0:T(8,128)(2,1)S(1)}, u32[]{:S(2)}, u32[]{:S(2)}) %collective-permute-start.44) | collective-permute-done | bytes 786464 | tf_op jit(solution)/shard_map/ppermute | solution.py:45
  728.1 8.1 collective-permute-done.47
  737.6 5.5 collective-permute-start.48
  758.5 4.5 all-to-all-start.6
  778.4 4.6 convolution_convert_fusion.6
  783.2 4.6 collective-permute-start.51
  788.3 18.7 %collective-permute-done.51 = bf16[560,128]{1,0:T(8,128)(2,1)S(1)} collective-permute-done((bf16[560,128]{1,0:T(8,128)(2,1)S(1)}, bf16[560,128]{1,0:T(8,128)(2,1)S(1)}, u32[]{:S(2)}, u32[]{:S(2)}) %collective-permute-start.51) | collective-permute-done | bytes 143392 | tf_op jit(solution)/shard_map/ppermute | solution.py:45
  807.0 20.0 %all-to-all-done.6 = bf16[8,256,512]{2,1,0:T(8,128)(2,1)} async-done(((bf16[8,256,512]{2,1,0:T(8,128)(2,1)}), bf16[8,256,512]{2,1,0:T(8,128)(2,1)}, u32[]{:S(2)}, u32[]{:S(2)}) %all-to-all-start.6) | async-done | bytes 2097184 | tf_op jit(solution)/shard_map/all_to_all | solution.py:184
  834.0 10.6 %collective-permute-start.52 = (bf16[2,560,128]{2,1,0:T(8,128)(2,1)}, bf16[2,560,128]{2,1,0:T(8,128)(2,1)}, u32[]{:S(2)}, u32[]{:S(2)}) collective-permute-start(bf16[2,560,128]{2,1,0:T(8,128)(2,1)} %fusion.71), channel_id=1, source_target_pairs={{0,1},{1,0},{2,3},{3,2},{4,5},{5,4},{6,7},{7,6},{8,9},{9,8},{10,11... | collective-permute-start | bytes 860168 | tf_op jit(solution)/shard_map/ppermute | solution.py:45
  845.5 6.4 all-to-all-start.7
  854.4 5.1 collective-permute-done.53
  866.5 4.5 bitcast_convert_fusion.2
  886.2 10.7 %collective-permute-done.55 = bf16[160,2048]{1,0:T(8,128)(2,1)} collective-permute-done((bf16[160,2048]{1,0:T(8,128)(2,1)}, bf16[160,2048]{1,0:T(8,128)(2,1)}, u32[]{:S(2)}, u32[]{:S(2)}) %collective-permute-start.55) | collective-permute-done | bytes 655392 | tf_op jit(solution)/shard_map/ppermute | solution.py:45
  899.6 5.3 reduce-scatter.6.cloned.1.call-done
  906.8 5.8 all-to-all-done.7
  948.0 10.4 %collective-permute-done.45 = bf16[160,2048]{1,0:T(8,128)(2,1)S(1)} collective-permute-done((bf16[160,2048]{1,0:T(8,128)(2,1)S(1)}, bf16[160,2048]{1,0:T(8,128)(2,1)S(1)}, u32[]{:S(2)}, u32[]{:S(2)}) %collective-permute-start.45) | collective-permute-done | bytes 655392 | tf_op jit(solution)/shard_map/ppermute | solution.py:45
  974.2 16.7 %reduce-scatter.8.cloned.1.call-done = bf16[1,384,640]{2,1,0:T(8,128)(2,1)} async-done(((bf16[8,384,640]{2,1,0:T(8,128)(2,1)}), bf16[1,384,640]{2,1,0:T(8,128)(2,1)}) %reduce-scatter.8.cloned.1.call-update) | async-done | bytes 491536 | tf_op jit(solution)/shard_map/reduce_scatter | solution.py:752
  (658 shorter events, 330.7 us)
Async XLA Ops:
  7.2 112.6 %all-gather.7.cloned.1.call-start = ((), (), s32[]{:S(2)}) async-start(), calls=%async_computation.14 | async-start | bytes 4608000 | tf_op jit(solution)/shard_map/all_gather | solution.py:549
  13.2 91.3 %all-to-all-start = ((bf16[8,256,512]{2,1,0:T(8,128)(2,1)}), bf16[8,256,512]{2,1,0:T(8,128)(2,1)}, u32[]{:S(2)}, u32[]{:S(2)}) async-start(bf16[8,256,512]{2,1,0:T(8,128)(2,1)} %bitcast.524), calls=%async_computation | async-start | bytes 4194304 | tf_op jit(solution)/shard_map/all_to_all | solution.py:184
  19.7 208.4 %all-gather.9.cloned.1.call-start = ((), (), s32[]{:S(2)}) async-start(), calls=%async_computation.15 | async-start | bytes 3538944 | tf_op jit(solution)/shard_map/all_gather | solution.py:553
  149.1 77.0 %all-to-all-start.1 = ((bf16[8,256,512]{2,1,0:T(8,128)(2,1)}), bf16[8,256,512]{2,1,0:T(8,128)(2,1)}, u32[]{:S(2)}, u32[]{:S(2)}) async-start(bf16[8,256,512]{2,1,0:T(8,128)(2,1)} %bitcast.556), calls=%async_computation.1 | async-start | bytes 4194304 | tf_op jit(solution)/shard_map/all_to_all | solution.py:184
  153.5 186.9 %all-gather.11.cloned.1.call-start = ((), (), s32[]{:S(2)}) async-start(), calls=%async_computation.16 | async-start | bytes 5898240 | tf_op jit(solution)/shard_map/all_gather | solution.py:582
  158.7 47.4 %collective-permute-start.6 = (bf16[2048,512]{1,0:T(8,128)(2,1)}, bf16[2048,512]{1,0:T(8,128)(2,1)}, u32[]{:S(2)}, u32[]{:S(2)}) collective-permute-start(bf16[2048,512]{1,0:T(8,128)(2,1)} %bitcast.2.refs_9_.refs_0_), channel_id=1, source_target_pairs={{0,2},{2,0},{1,3},{3,1},{4,6},{6,4},{5,7},{7,5},{8,10},{10,8},{9,1... | collective-permute-start | bytes 6291464 | tf_op jit(solution)/shard_map/ppermute | solution.py:45
  226.1 46.9 %collective-permute-start.7 = (bf16[2048,512]{1,0:T(8,128)(2,1)}, bf16[2048,512]{1,0:T(8,128)(2,1)}, u32[]{:S(2)}, u32[]{:S(2)}) collective-permute-start(bf16[2048,512]{1,0:T(8,128)(2,1)} %bitcast.39.refs_13_.refs_4_), channel_id=1, source_target_pairs={{0,2},{2,0},{1,3},{3,1},{4,6},{6,4},{5,7},{7,5},{8,10},{10,8},{9,1... | collective-permute-start | bytes 6291464 | tf_op jit(solution)/shard_map/ppermute | solution.py:45
  227.3 45.7 %collective-permute-start.8 = (bf16[2048,512]{1,0:T(8,128)(2,1)}, bf16[2048,512]{1,0:T(8,128)(2,1)}, u32[]{:S(2)}, u32[]{:S(2)}) collective-permute-start(bf16[2048,512]{1,0:T(8,128)(2,1)} %bitcast.39.refs_13_.refs_4_), channel_id=1, source_target_pairs={{0,1},{1,0},{2,3},{3,2},{4,5},{5,4},{6,7},{7,6},{8,9},{9,8},{10,11... | collective-permute-start | bytes 6291464 | tf_op jit(solution)/shard_map/ppermute | solution.py:45
  244.7 90.1 %all-to-all-start.2 = ((bf16[8,512,256]{2,1,0:T(8,128)(2,1)}), bf16[8,512,256]{2,1,0:T(8,128)(2,1)}, u32[]{:S(2)}, u32[]{:S(2)}) async-start(bf16[8,512,256]{2,1,0:T(8,128)(2,1)} %bitcast.604), calls=%async_computation.2 | async-start | bytes 4194304 | tf_op jit(solution)/shard_map/all_to_all | solution.py:184
  282.7 16.1 %collective-permute-start.10 = (bf16[160,2048]{1,0:T(8,128)(2,1)S(1)}, bf16[160,2048]{1,0:T(8,128)(2,1)}, u32[]{:S(2)}, u32[]{:S(2)}) collective-permute-start(bf16[160,2048]{1,0:T(8,128)(2,1)S(1)} %fusion.51), channel_id=1, source_target_pairs={{0,2},{2,0},{1,3},{3,1},{4,6},{6,4},{5,7},{7,5},{8,10},{10,8},{9,1... | collective-permute-start | bytes 1966088 | tf_op jit(solution)/shard_map/ppermute | solution.py:45
  284.0 64.7 %collective-permute-start.13 = (bf16[2048,512]{1,0:T(8,128)(2,1)}, bf16[2048,512]{1,0:T(8,128)(2,1)}, u32[]{:S(2)}, u32[]{:S(2)}) collective-permute-start(bf16[2048,512]{1,0:T(8,128)(2,1)} %collective-permute-done.7.refs_14_.refs_5_), channel_id=1, source_target_pairs={{0,1},{1,0},{2,3},{3,2},{4,5},{5,4},{6,7},{7,6},{8,9},{9,8},{10,11... | collective-permute-start | bytes 6291464 | tf_op jit(solution)/shard_map/ppermute | solution.py:45
  344.9 49.4 %collective-permute-start.18 = (bf16[512,2048]{1,0:T(8,128)(2,1)S(1)}, bf16[512,2048]{1,0:T(8,128)(2,1)S(1)}, u32[]{:S(2)}, u32[]{:S(2)}) collective-permute-start(bf16[512,2048]{1,0:T(8,128)(2,1)S(1)} %bitcast.529), channel_id=1, source_target_pairs={{0,2},{2,0},{1,3},{3,1},{4,6},{6,4},{5,7},{7,5},{8,10},{10,8},{9,1... | collective-permute-start | bytes 6291464 | tf_op jit(solution)/shard_map/ppermute | solution.py:45
  345.3 49.0 %collective-permute-start.19 = (bf16[512,2048]{1,0:T(8,128)(2,1)S(1)}, bf16[512,2048]{1,0:T(8,128)(2,1)S(1)}, u32[]{:S(2)}, u32[]{:S(2)}) collective-permute-start(bf16[512,2048]{1,0:T(8,128)(2,1)S(1)} %bitcast.530), channel_id=1, source_target_pairs={{0,1},{1,0},{2,3},{3,2},{4,5},{5,4},{6,7},{7,6},{8,9},{9,8},{10,11... | collective-permute-start | bytes 6291464 | tf_op jit(solution)/shard_map/ppermute | solution.py:45
  347.2 16.4 %collective-permute-start.11 = (bf16[160,2048]{1,0:T(8,128)(2,1)S(1)}, bf16[160,2048]{1,0:T(8,128)(2,1)S(1)}, u32[]{:S(2)}, u32[]{:S(2)}) collective-permute-start(bf16[160,2048]{1,0:T(8,128)(2,1)S(1)} %maximum_maximum_fusion.11.refs_0_), channel_id=1, source_target_pairs={{0,4},{8,0},{16,8},{24,16},{28,24},{20,28},{12,20},{4,12},{1,5},{9... | collective-permute-start | bytes 1966088 | tf_op jit(solution)/shard_map/ppermute | solution.py:50
  396.5 19.3 %collective-permute-start.21 = (bf16[512,2048]{1,0:T(8,128)(2,1)S(1)}, bf16[512,2048]{1,0:T(8,128)(2,1)}, u32[]{:S(2)}, u32[]{:S(2)}) collective-permute-start(bf16[512,2048]{1,0:T(8,128)(2,1)S(1)} %collective-permute-done.18.refs_18_.refs_1_), channel_id=1, source_target_pairs={{0,1},{1,0},{2,3},{3,2},{4,5},{5,4},{6,7},{7,6},{8,9},{9,8},{10,11... | collective-permute-start | bytes 6291464 | tf_op jit(solution)/shard_map/ppermute | solution.py:45
  399.4 23.1 %collective-permute-start.22 = (bf16[2048,512]{1,0:T(8,128)(2,1)}, bf16[2048,512]{1,0:T(8,128)(2,1)}, u32[]{:S(2)}, u32[]{:S(2)}) collective-permute-start(bf16[2048,512]{1,0:T(8,128)(2,1)} %collective-permute-done.6.refs_10_.refs_1_), channel_id=1, source_target_pairs={{0,1},{1,0},{2,3},{3,2},{4,5},{5,4},{6,7},{7,6},{8,9},{9,8},{10,11... | collective-permute-start | bytes 6291464 | tf_op jit(solution)/shard_map/ppermute | solution.py:45
  399.5 16.4 %collective-permute-start.20 = (bf16[160,2048]{1,0:T(8,128)(2,1)}, bf16[160,2048]{1,0:T(8,128)(2,1)}, u32[]{:S(2)}, u32[]{:S(2)}) collective-permute-start(bf16[160,2048]{1,0:T(8,128)(2,1)} %collective-permute-done.16.refs_5_), channel_id=1, source_target_pairs={{0,4},{8,0},{16,8},{24,16},{28,24},{20,28},{12,20},{4,12},{1,5},{9... | collective-permute-start | bytes 1966088 | tf_op jit(solution)/shard_map/ppermute | solution.py:50
  415.8 51.1 %all-to-all-start.3 = ((bf16[8,384,128]{2,1,0:T(8,128)(2,1)}), bf16[8,384,128]{2,1,0:T(8,128)(2,1)}, u32[]{:S(2)}, u32[]{:S(2)}) async-start(bf16[8,384,128]{2,1,0:T(8,128)(2,1)} %pad_maximum_fusion.1), calls=%async_computation.3 | async-start | bytes 1572864 | tf_op jit(solution)/shard_map/all_to_all | solution.py:184
  420.0 220.6 %reduce-scatter.4.cloned.1.call-start = ((), (), s32[]{:S(2)}) async-start(), calls=%async_computation.11 | async-start | bytes 5308416 | tf_op jit(solution)/shard_map/reduce_scatter | solution.py:639
  467.0 18.3 %collective-permute-start.23 = (bf16[8,384,128]{2,1,0:T(8,128)(2,1)}, bf16[8,384,128]{2,1,0:T(8,128)(2,1)}, u32[]{:S(2)}, u32[]{:S(2)}) collective-permute-start(bf16[8,384,128]{2,1,0:T(8,128)(2,1)} %all-to-all-done.3.refs_0_), channel_id=1, source_target_pairs={{0,2},{2,0},{1,3},{3,1},{4,6},{6,4},{5,7},{7,5},{8,10},{10,8},{9,1... | collective-permute-start | bytes 2359304 | tf_op jit(solution)/shard_map/ppermute | solution.py:45
  485.2 17.9 %collective-permute-start.25 = (bf16[512,2048]{1,0:T(8,128)(2,1)}, bf16[512,2048]{1,0:T(8,128)(2,1)}, u32[]{:S(2)}, u32[]{:S(2)}) collective-permute-start(bf16[512,2048]{1,0:T(8,128)(2,1)} %get-tuple-element.212), channel_id=1, source_target_pairs={{0,1},{1,0},{2,3},{3,2},{4,5},{5,4},{6,7},{7,6},{8,9},{9,8},{10,11... | collective-permute-start | bytes 6291464 | tf_op jit(solution)/shard_map/ppermute | solution.py:45
  487.3 20.3 %collective-permute-start.24 = (bf16[512,2048]{1,0:T(8,128)(2,1)}, bf16[512,2048]{1,0:T(8,128)(2,1)}, u32[]{:S(2)}, u32[]{:S(2)}) collective-permute-start(bf16[512,2048]{1,0:T(8,128)(2,1)} %get-tuple-element.210), channel_id=1, source_target_pairs={{0,1},{1,0},{2,3},{3,2},{4,5},{5,4},{6,7},{7,6},{8,9},{9,8},{10,11... | collective-permute-start | bytes 6291464 | tf_op jit(solution)/shard_map/ppermute | solution.py:45
  487.3 24.0 %collective-permute-start.26 = (bf16[8,384,128]{2,1,0:T(8,128)(2,1)}, bf16[8,384,128]{2,1,0:T(8,128)(2,1)}, u32[]{:S(2)}, u32[]{:S(2)}) collective-permute-start(bf16[8,384,128]{2,1,0:T(8,128)(2,1)} %all-to-all-done.3.refs_0_), channel_id=1, source_target_pairs={{0,1},{1,0},{2,3},{3,2},{4,5},{5,4},{6,7},{7,6},{8,9},{9,8},{10,11... | collective-permute-start | bytes 2359304 | tf_op jit(solution)/shard_map/ppermute | solution.py:45
  487.8 23.5 %collective-permute-start.27 = (bf16[8,384,128]{2,1,0:T(8,128)(2,1)}, bf16[8,384,128]{2,1,0:T(8,128)(2,1)}, u32[]{:S(2)}, u32[]{:S(2)}) collective-permute-start(bf16[8,384,128]{2,1,0:T(8,128)(2,1)} %collective-permute-done.23.refs_1_), channel_id=1, source_target_pairs={{0,1},{1,0},{2,3},{3,2},{4,5},{5,4},{6,7},{7,6},{8,9},{9,8},{10,11... | collective-permute-start | bytes 2359304 | tf_op jit(solution)/shard_map/ppermute | solution.py:45
  527.2 42.6 %collective-permute-start.30 = (bf16[2048,512]{1,0:T(8,128)(2,1)}, bf16[2048,512]{1,0:T(8,128)(2,1)}, u32[]{:S(2)}, u32[]{:S(2)}) collective-permute-start(bf16[2048,512]{1,0:T(8,128)(2,1)} %get-tuple-element.232), channel_id=1, source_target_pairs={{0,1},{1,0},{2,3},{3,2},{4,5},{5,4},{6,7},{7,6},{8,9},{9,8},{10,11... | collective-permute-start | bytes 6291464 | tf_op jit(solution)/shard_map/ppermute | solution.py:45
  527.7 45.8 %collective-permute-start.29 = (bf16[2048,512]{1,0:T(8,128)(2,1)}, bf16[2048,512]{1,0:T(8,128)(2,1)}, u32[]{:S(2)}, u32[]{:S(2)}) collective-permute-start(bf16[2048,512]{1,0:T(8,128)(2,1)} %get-tuple-element.230), channel_id=1, source_target_pairs={{0,1},{1,0},{2,3},{3,2},{4,5},{5,4},{6,7},{7,6},{8,9},{9,8},{10,11... | collective-permute-start | bytes 6291464 | tf_op jit(solution)/shard_map/ppermute | solution.py:45
  527.7 48.1 %collective-permute-start.28 = (bf16[512,2048]{1,0:T(8,128)(2,1)}, bf16[512,2048]{1,0:T(8,128)(2,1)}, u32[]{:S(2)}, u32[]{:S(2)}) collective-permute-start(bf16[512,2048]{1,0:T(8,128)(2,1)} %add_convert_fusion.7), channel_id=1, source_target_pairs={{0,2},{2,0},{1,3},{3,1},{4,6},{6,4},{5,7},{7,5},{8,10},{10,8},{9,1... | collective-permute-start | bytes 6291464 | tf_op jit(solution)/shard_map/ppermute | solution.py:45
  578.2 47.1 %collective-permute-start.35 = (bf16[8,384,128]{2,1,0:T(8,128)(2,1)}, bf16[8,384,128]{2,1,0:T(8,128)(2,1)}, u32[]{:S(2)}, u32[]{:S(2)}) collective-permute-start(bf16[8,384,128]{2,1,0:T(8,128)(2,1)} %get-tuple-element.265), channel_id=1, source_target_pairs={{0,1},{1,0},{2,3},{3,2},{4,5},{5,4},{6,7},{7,6},{8,9},{9,8},{10,11... | collective-permute-start | bytes 2359304 | tf_op jit(solution)/shard_map/ppermute | solution.py:45
  579.1 48.5 %collective-permute-start.34 = (bf16[8,384,128]{2,1,0:T(8,128)(2,1)}, bf16[8,384,128]{2,1,0:T(8,128)(2,1)}, u32[]{:S(2)}, u32[]{:S(2)}) collective-permute-start(bf16[8,384,128]{2,1,0:T(8,128)(2,1)} %get-tuple-element.263), channel_id=1, source_target_pairs={{0,1},{1,0},{2,3},{3,2},{4,5},{5,4},{6,7},{7,6},{8,9},{9,8},{10,11... | collective-permute-start | bytes 2359304 | tf_op jit(solution)/shard_map/ppermute | solution.py:45
  579.2 50.8 %collective-permute-start.33 = (bf16[2048,512]{1,0:T(8,128)(2,1)}, bf16[2048,512]{1,0:T(8,128)(2,1)}, u32[]{:S(2)}, u32[]{:S(2)}) collective-permute-start(bf16[2048,512]{1,0:T(8,128)(2,1)} %get-tuple-element.260), channel_id=1, source_target_pairs={{0,1},{1,0},{2,3},{3,2},{4,5},{5,4},{6,7},{7,6},{8,9},{9,8},{10,11... | collective-permute-start | bytes 6291464 | tf_op jit(solution)/shard_map/ppermute | solution.py:45
  579.6 54.0 %collective-permute-start.32 = (bf16[2048,512]{1,0:T(8,128)(2,1)}, bf16[2048,512]{1,0:T(8,128)(2,1)}, u32[]{:S(2)}, u32[]{:S(2)}) collective-permute-start(bf16[2048,512]{1,0:T(8,128)(2,1)} %get-tuple-element.258), channel_id=1, source_target_pairs={{0,1},{1,0},{2,3},{3,2},{4,5},{5,4},{6,7},{7,6},{8,9},{9,8},{10,11... | collective-permute-start | bytes 6291464 | tf_op jit(solution)/shard_map/ppermute | solution.py:45
  579.7 57.4 %collective-permute-start.31 = (bf16[2048,512]{1,0:T(8,128)(2,1)}, bf16[2048,512]{1,0:T(8,128)(2,1)}, u32[]{:S(2)}, u32[]{:S(2)}) collective-permute-start(bf16[2048,512]{1,0:T(8,128)(2,1)} %add_convert_fusion.4), channel_id=1, source_target_pairs={{0,2},{2,0},{1,3},{3,1},{4,6},{6,4},{5,7},{7,5},{8,10},{10,8},{9,1... | collective-permute-start | bytes 6291464 | tf_op jit(solution)/shard_map/ppermute | solution.py:45
  581.7 70.4 %all-to-all-start.4 = ((bf16[8,512,256]{2,1,0:T(8,128)(2,1)}), bf16[8,512,256]{2,1,0:T(8,128)(2,1)}, u32[]{:S(2)}, u32[]{:S(2)}) async-start(bf16[8,512,256]{2,1,0:T(8,128)(2,1)} %bitcast.557), calls=%async_computation.4 | async-start | bytes 4194304 | tf_op jit(solution)/shard_map/all_to_all | solution.py:184
  652.1 17.2 %collective-permute-start.37 = (bf16[176,2048]{1,0:T(8,128)(2,1)}, bf16[176,2048]{1,0:T(8,128)(2,1)S(1)}, u32[]{:S(2)}, u32[]{:S(2)}) collective-permute-start(bf16[176,2048]{1,0:T(8,128)(2,1)} %maximum_maximum_fusion.8), channel_id=1, source_target_pairs={{0,4},{8,0},{16,8},{24,16},{28,24},{20,28},{12,20},{4,12},{1,5},{9... | collective-permute-start | bytes 2162696 | tf_op jit(solution)/shard_map/ppermute | solution.py:50
  653.3 17.0 %collective-permute-start.36 = (bf16[176,2048]{1,0:T(8,128)(2,1)}, bf16[176,2048]{1,0:T(8,128)(2,1)S(1)}, u32[]{:S(2)}, u32[]{:S(2)}) collective-permute-start(bf16[176,2048]{1,0:T(8,128)(2,1)} %maximum_maximum_fusion.9), channel_id=1, source_target_pairs={{0,8},{8,16},{16,24},{24,28},{28,20},{20,12},{12,4},{4,0},{1,9},{9... | collective-permute-start | bytes 2162696 | tf_op jit(solution)/shard_map/ppermute | solution.py:50
  653.5 46.1 %collective-permute-start.42 = (bf16[2048,512]{1,0:T(8,128)(2,1)}, bf16[2048,512]{1,0:T(8,128)(2,1)S(1)}, u32[]{:S(2)}, u32[]{:S(2)}) collective-permute-start(bf16[2048,512]{1,0:T(8,128)(2,1)} %add_convert_fusion.1), channel_id=1, source_target_pairs={{0,2},{2,0},{1,3},{3,1},{4,6},{6,4},{5,7},{7,5},{8,10},{10,8},{9,1... | collective-permute-start | bytes 6291464 | tf_op jit(solution)/shard_map/ppermute | solution.py:45
  688.1 28.4 %collective-permute-start.44 = (bf16[8,384,128]{2,1,0:T(8,128)(2,1)S(1)}, bf16[8,384,128]{2,1,0:T(8,128)(2,1)S(1)}, u32[]{:S(2)}, u32[]{:S(2)}) collective-permute-start(bf16[8,384,128]{2,1,0:T(8,128)(2,1)S(1)} %copy-done.71), channel_id=1, source_target_pairs={{0,2},{2,0},{1,3},{3,1},{4,6},{6,4},{5,7},{7,5},{8,10},{10,8},{9,1... | collective-permute-start | bytes 2359304 | tf_op jit(solution)/shard_map/ppermute | solution.py:45
  724.6 23.4 %all-to-all-start.5 = ((bf16[8,384,128]{2,1,0:T(8,128)(2,1)}), bf16[8,384,128]{2,1,0:T(8,128)(2,1)S(1)}, u32[]{:S(2)}, u32[]{:S(2)}) async-start(bf16[8,384,128]{2,1,0:T(8,128)(2,1)} %add_convert_fusion.9), calls=%async_computation.6 | async-start | bytes 1572864 | tf_op jit(solution)/shard_map/all_to_all | solution.py:184
  758.5 68.5 %all-to-all-start.6 = ((bf16[8,256,512]{2,1,0:T(8,128)(2,1)}), bf16[8,256,512]{2,1,0:T(8,128)(2,1)}, u32[]{:S(2)}, u32[]{:S(2)}) async-start(bf16[8,256,512]{2,1,0:T(8,128)(2,1)} %bitcast.139), calls=%async_computation.7 | async-start | bytes 4194304 | tf_op jit(solution)/shard_map/all_to_all | solution.py:184
  763.0 141.9 %reduce-scatter.6.cloned.1.call-start = ((), (), s32[]{:S(2)}) async-start(), calls=%async_computation.12 | async-start | bytes 3538944 | tf_op jit(solution)/shard_map/reduce_scatter | solution.py:696
  783.2 23.8 %collective-permute-start.51 = (bf16[560,128]{1,0:T(8,128)(2,1)S(1)}, bf16[560,128]{1,0:T(8,128)(2,1)S(1)}, u32[]{:S(2)}, u32[]{:S(2)}) collective-permute-start(bf16[560,128]{1,0:T(8,128)(2,1)S(1)} %slice.685), channel_id=1, source_target_pairs={{0,28},{4,0},{8,4},{12,8},{16,12},{20,16},{24,20},{28,24},{1,29},{... | collective-permute-start | bytes 430088 | tf_op jit(solution)/shard_map/ppermute | solution.py:45
  834.0 18.5 %collective-permute-start.52 = (bf16[2,560,128]{2,1,0:T(8,128)(2,1)}, bf16[2,560,128]{2,1,0:T(8,128)(2,1)}, u32[]{:S(2)}, u32[]{:S(2)}) collective-permute-start(bf16[2,560,128]{2,1,0:T(8,128)(2,1)} %fusion.71), channel_id=1, source_target_pairs={{0,1},{1,0},{2,3},{3,2},{4,5},{5,4},{6,7},{7,6},{8,9},{9,8},{10,11... | collective-permute-start | bytes 860168 | tf_op jit(solution)/shard_map/ppermute | solution.py:45
  845.5 67.2 %all-to-all-start.7 = ((bf16[8,256,512]{2,1,0:T(8,128)(2,1)}), bf16[8,256,512]{2,1,0:T(8,128)(2,1)}, u32[]{:S(2)}, u32[]{:S(2)}) async-start(bf16[8,256,512]{2,1,0:T(8,128)(2,1)} %bitcast.553), calls=%async_computation.8 | async-start | bytes 4194304 | tf_op jit(solution)/shard_map/all_to_all | solution.py:184
  851.9 139.1 %reduce-scatter.8.cloned.1.call-start = ((), (), s32[]{:S(2)}) async-start(), calls=%async_computation.13 | async-start | bytes 4423680 | tf_op jit(solution)/shard_map/reduce_scatter | solution.py:752
  880.5 16.3 %collective-permute-start.55 = (bf16[160,2048]{1,0:T(8,128)(2,1)}, bf16[160,2048]{1,0:T(8,128)(2,1)}, u32[]{:S(2)}, u32[]{:S(2)}) collective-permute-start(bf16[160,2048]{1,0:T(8,128)(2,1)} %fusion.52), channel_id=1, source_target_pairs={{0,2},{2,0},{1,3},{3,1},{4,6},{6,4},{5,7},{7,5},{8,10},{10,8},{9,1... | collective-permute-start | bytes 1966088 | tf_op jit(solution)/shard_map/ppermute | solution.py:45
  930.3 28.1 %collective-permute-start.45 = (bf16[160,2048]{1,0:T(8,128)(2,1)S(1)}, bf16[160,2048]{1,0:T(8,128)(2,1)S(1)}, u32[]{:S(2)}, u32[]{:S(2)}) collective-permute-start(bf16[160,2048]{1,0:T(8,128)(2,1)S(1)} %get-tuple-element.434), channel_id=1, source_target_pairs={{0,2},{2,0},{1,3},{3,1},{4,6},{6,4},{5,7},{7,5},{8,10},{10,8},{9,1... | collective-permute-start | bytes 1966088 | tf_op jit(solution)/shard_map/ppermute | solution.py:45
  939.2 27.8 %collective-permute-start.62 = (f32[1,768]{1,0:T(1,128)S(1)}, f32[1,768]{1,0:T(1,128)S(1)}, u32[]{:S(2)}, u32[]{:S(2)}) collective-permute-start(f32[1,768]{1,0:T(1,128)S(1)} %add.497), channel_id=1, source_target_pairs={{0,2},{2,0},{1,3},{3,1},{4,6},{6,4},{5,7},{7,5},{8,10},{10,8},{9,1... | collective-permute-start | bytes 9224 | tf_op jit(solution)/shard_map/ppermute | solution.py:45
  944.6 23.9 %collective-permute-start.57 = (bf16[2,160,2048]{2,1,0:T(8,128)(2,1)S(1)}, bf16[2,160,2048]{2,1,0:T(8,128)(2,1)S(1)}, u32[]{:S(2)}, u32[]{:S(2)}) collective-permute-start(bf16[2,160,2048]{2,1,0:T(8,128)(2,1)S(1)} %maximum_select_fusion.7), channel_id=1, source_target_pairs={{0,1},{1,0},{2,3},{3,2},{4,5},{5,4},{6,7},{7,6},{8,9},{9,8},{10,11... | collective-permute-start | bytes 3932168 | tf_op jit(solution)/shard_map/ppermute | solution.py:45
  (156 other events, 2243.4 us)
Sparse Core Ops, SparseCore 0:
  11.8 107.9 all-gather.6
  122.6 94.2 all-gather.8
  219.1 121.3 all-gather.10
  511.5 112.1 reduce-scatter.3
  776.7 128.1 reduce-scatter.5
  908.4 82.4 reduce-scatter.7
